TPU v7x, 128 devices: a whole 4x4x4 slice. The times are simulated.
128 devices in a mesh: row: 8 (over x_lo, y), col: 16 (over x_hi, z, core).
Axes of the slice: x: 4 (x_hi: 2, x_lo: 2; x = x_hi * 2 + x_lo), y: 4, z: 4, core: 2. Of those that a mesh axis runs over, the one named last changes fastest.
Arguments:
- features: bfloat16 [65536, 512], P(('row', 'col')), may hold values from -6 to 6
- tile_cols: int32 [8, 16, 32, 8], P('row', 'col'), may hold values from 0 to 63, as said below
- tile_masks: bfloat16 [8, 16, 32, 8, 128, 128], P('row', 'col'), may hold values from 0 to 1, as said below
- degree: int32 [65536], P(('row', 'col')), may hold values from 8 to 32
- owner_nodes: int32 [65536], P(('row', 'col')), may hold values from 0 to 65535, as said below
- owner_position: int32 [65536], P(('row', 'col')), may hold values from 0 to 65535, as said below
- self_weight: bfloat16 [512, 512], replicated, may hold values from -0.25 to 0.25
- neigh_weight: bfloat16 [512, 512], replicated, may hold values from -0.25 to 0.25
- cotangent: bfloat16 [65536, 512], P(('row', 'col')), may hold values from -6 to 6
Outputs:
- hidden: bfloat16 [65536, 512], P(('row', 'col'))
- grad_features: bfloat16 [65536, 512], P(('row', 'col'))
- grad_self: float32 [512, 512], replicated
- grad_neigh: float32 [512, 512], replicated
Inputs may be any that keep to these rules, and one draw needn't show every extreme that they name: `tile_cols`: in each grid cell, the 8 entries of one tile row are different tile columns. `tile_masks`: entries are 0 or 1. `owner_nodes`: A permutation of the node numbers. For any two devices, the number of nodes of the first one's block that the second one holds in the owner layout is 0 or exactly 8. `owner_position`: the inverse permutation of owner_nodes.
All inputs are finite; a program needn't handle non-finite values.
Results may differ from a plain program's by a relative error of at most 0.013.
Values may be sent and summed in bfloat16 or wider, within the bound.
A program may use at most 128 MiB of HBM per device.

v0:
```python
import math

import jax
import jax.numpy as jnp
from jax import lax
from jax.sharding import PartitionSpec as P


def rank_within(group_keys, order_keys):
    same_group = group_keys[:, None] == group_keys[None, :]
    earlier = order_keys[None, :] < order_keys[:, None]
    return jnp.sum(same_group & earlier, axis=1)


def rank_running(group_keys, group_count):
    onehot_table = (
        group_keys[:, None] == jnp.arange(group_count, dtype=jnp.int32)[None, :]
    ).astype(jnp.int32)
    running = jnp.cumsum(onehot_table, axis=0)
    return jnp.take_along_axis(running, group_keys[:, None], axis=1)[:, 0] - 1


def on_device(
    features,
    tile_cols,
    tile_masks,
    degree,
    owner_nodes,
    owner_position,
    self_weight,
    neigh_weight,
    cotangent,
):
    row_count = features.shape[0]
    feat_width = features.shape[1]
    row_devices = lax.axis_size("row")
    col_devices = lax.axis_size("col")
    all_devices = row_devices * col_devices
    slot_count = 2 * row_count // all_devices
    pattern = tile_masks[0, 0]
    columns = tile_cols[0, 0]
    tile_size = pattern.shape[-1]
    breadth = pattern.shape[1]
    group_rows = row_count // tile_size
    own_dest = owner_nodes // row_count
    own_flat = own_dest * slot_count + rank_within(own_dest, jnp.arange(row_count, dtype=jnp.int32))
    node_source = owner_position // row_count
    node_flat = node_source * slot_count + rank_within(node_source, owner_position)
    outbound = (
        jnp.zeros((all_devices * slot_count, feat_width), jnp.bfloat16).at[own_flat].set(features)
    )
    inbound = lax.all_to_all(outbound, ("row", "col"), split_axis=0, concat_axis=0, tiled=True)
    node_feats = inbound[node_flat]
    column_feats = lax.all_gather(node_feats, "col", axis=0, tiled=True)
    feat_tiles = column_feats.reshape(-1, tile_size, feat_width)
    grid_lookup = lax.all_gather(owner_position, "row", axis=0, tiled=True)
    grid_dest = grid_lookup // row_count
    wide_slots = row_devices * slot_count
    grid_flat = grid_dest * wide_slots + rank_running(grid_dest, all_devices)
    row_total = row_devices * row_count
    tile_rows = row_total // tile_size
    groups = tile_rows // group_rows
    mask_block = pattern.reshape(groups, group_rows, breadth, tile_size, tile_size)
    col_block = columns.reshape(groups, group_rows, breadth)

    def one_group(operands):
        chosen = feat_tiles[operands[1]]
        return jnp.einsum("tkij,tkjf->tif", operands[0], chosen, preferred_element_type=jnp.float32)

    products = lax.map(one_group, (mask_block, col_block))
    partial_rows = products.reshape(row_total, feat_width).astype(jnp.bfloat16)
    outgoing = (
        jnp.zeros((all_devices * wide_slots, feat_width), jnp.bfloat16)
        .at[grid_flat]
        .set(partial_rows)
    )
    incoming = lax.all_to_all(outgoing, ("row", "col"), split_axis=0, concat_axis=0, tiled=True)
    home_block = owner_nodes // row_count
    home_col = home_block % col_devices
    home_row = home_block // col_devices * row_count + owner_nodes % row_count
    home_rank = rank_within(home_col, home_row)
    sources = jnp.arange(row_devices, dtype=jnp.int32)[:, None] * col_devices + home_col[None, :]
    summed = jnp.sum(
        incoming[sources * wide_slots + home_rank[None, :]].astype(jnp.float32), axis=0
    )
    degrees = degree.astype(jnp.float32)[:, None]
    aggregate = (summed / degrees).astype(jnp.bfloat16)
    preact = jnp.dot(features, self_weight, preferred_element_type=jnp.float32) + jnp.dot(
        aggregate, neigh_weight, preferred_element_type=jnp.float32
    )
    hidden = jax.nn.silu(preact).astype(jnp.bfloat16)
    gate_value = jax.nn.sigmoid(preact)
    slopes = (
        cotangent.astype(jnp.float32) * gate_value * (1.0 + preact * (1.0 - gate_value))
    ).astype(jnp.bfloat16)
    along_rows = (((0,), (0,)), ((), ()))
    grad_terms = (
        lax.dot_general(features, slopes, along_rows, preferred_element_type=jnp.float32),
        lax.dot_general(aggregate, slopes, along_rows, preferred_element_type=jnp.float32),
    )
    along_cols = (((1,), (1,)), ((), ()))
    own_back = lax.dot_general(slopes, self_weight, along_cols, preferred_element_type=jnp.float32)
    spread = (
        lax.dot_general(slopes, neigh_weight, along_cols, preferred_element_type=jnp.float32)
        / degrees
    ).astype(jnp.bfloat16)
    block_slots = (
        jnp.zeros((col_devices * wide_slots, feat_width), jnp.bfloat16)
        .at[home_col * wide_slots + home_rank]
        .set(spread)
    )
    outgoing_back = jnp.broadcast_to(
        block_slots[None], (row_devices, col_devices * wide_slots, feat_width)
    ).reshape(all_devices * wide_slots, feat_width)
    grid_spread = lax.all_to_all(
        outgoing_back, ("row", "col"), split_axis=0, concat_axis=0, tiled=True
    )[grid_flat]
    spread_tiles = grid_spread.reshape(-1, tile_size, feat_width)
    col_tiles = column_feats.shape[0] // tile_size
    group_total = pattern.shape[0] // group_rows

    def add_group(group_index, totals):
        mask_part = lax.dynamic_slice_in_dim(pattern, group_index * group_rows, group_rows, 0)
        col_part = lax.dynamic_slice_in_dim(columns, group_index * group_rows, group_rows, 0)
        row_part = lax.dynamic_slice_in_dim(spread_tiles, group_index * group_rows, group_rows, 0)
        pieces = jnp.einsum(
            "tkij,tif->tkjf", mask_part, row_part, preferred_element_type=jnp.float32
        )
        return totals.at[col_part.reshape(-1)].add(pieces.reshape(-1, tile_size, feat_width))

    start_zero = jnp.zeros((col_tiles, tile_size, feat_width), jnp.float32)
    back_terms = lax.fori_loop(0, group_total, add_group, start_zero).reshape(-1, feat_width)
    node_back = lax.psum_scatter(
        back_terms.astype(jnp.bfloat16), "col", scatter_dimension=0, tiled=True
    ).astype(jnp.float32)
    outgoing_sum = (
        jnp.zeros((all_devices * slot_count, feat_width), jnp.float32).at[node_flat].set(node_back)
    )
    neigh_back = lax.all_to_all(
        outgoing_sum.astype(jnp.bfloat16), ("row", "col"), split_axis=0, concat_axis=0, tiled=True
    ).astype(outgoing_sum.dtype)[own_flat]
    grad_features = (own_back + neigh_back).astype(jnp.bfloat16)
    summed_grads = lax.psum((grad_terms[0], grad_terms[1]), ("row", "col"))
    grad_scale = 1.0 / math.sqrt(row_count * all_devices)
    return (hidden, grad_features, summed_grads[0] * grad_scale, summed_grads[1] * grad_scale)


def solution(mesh):
    placed = (
        P(("row", "col"), None),
        P("row", "col", None, None),
        P("row", "col", None, None, None, None),
        P(("row", "col")),
        P(("row", "col")),
        P(("row", "col")),
        P(),
        P(),
        P(("row", "col"), None),
    )
    return jax.shard_map(
        on_device,
        mesh=mesh,
        in_specs=placed,
        out_specs=(P(("row", "col"), None), P(("row", "col"), None), P(), P()),
        check_vma=False,
    )
```

profile of v0, /device:TPU:1, one launch (start us, length us, event | category | flops | bytes accessed | tf_op | source)
XLA Modules:
  0.0 999.1 jit_solution(15960045363965464775)
XLA Ops:
  13.1 11.5 %all-to-all-start = ((bf16[128,8,512]{2,1,0:T(8,128)(2,1)}), bf16[128,8,512]{2,1,0:T(8,128)(2,1)S(1)}, u32[]{:S(2)}, u32[]{:S(2)}) async-start(bf16[128,8,512]{2,1,0:T(8,128)(2,1)} %bitcast.21), calls=%async_computation | async-start | bytes 2097152 | tf_op jit(solution)/shard_map/all_to_all | solution.py:52
  27.1 16.7 %all-to-all-done = bf16[128,8,512]{2,1,0:T(8,128)(2,1)S(1)} async-done(((bf16[128,8,512]{2,1,0:T(8,128)(2,1)}), bf16[128,8,512]{2,1,0:T(8,128)(2,1)S(1)}, u32[]{:S(2)}, u32[]{:S(2)}) %all-to-all-start) | async-done | bytes 1048608 | tf_op jit(solution)/shard_map/all_to_all | solution.py:52
  46.5 20.5 %all-gather.1 = s32[8,1,512]{2,1,0:T(1,128)S(1)} all-gather(s32[1,1,512]{2,1,0:T(1,128)S(1)} %bitcast.109), channel_id=1, replica_groups=mesh['row'=8,'col'=16] {'row'}, dimensions={0}, use_global_device_ids=true | all-gather | bytes 18432 | tf_op jit(solution)/shard_map/all_gather | solution.py:56
  72.8 33.0 %gather_fusion.5 = s32[4096]{0:T(1024)S(1)} fusion(s32[4096,128]{0,1:T(8,128)S(1)} %bitcast.91, s32[4096]{0:T(1024)S(1)} %bitcast.90), kind=kCustom, calls=%fused_computation.5 | custom fusion | bytes 65536 | tf_op jit(solution)/shard_map/jit(take_along_axis)/gather | solution.py:20
  105.9 10.3 %all-gather.4.cloned.1.call-done = bf16[8192,512]{1,0:T(8,128)(2,1)} async-done(((bf16[512,512]{1,0:T(8,128)(2,1)}), bf16[8192,512]{1,0:T(8,128)(2,1)}) %all-gather.4.cloned.1.call-update) | async-done | bytes 8388624 | tf_op jit(solution)/shard_map/all_gather | solution.py:54
  116.2 82.2 %while.23 = (s32[]{:T(128)}, bf16[8,4,128,512]{3,2,1,0:T(8,128)(2,1)}, bf16[8,4,8,128,128]{4,3,2,1,0:T(8,128)(2,1)}, s32[8,4,8]{2,1,0:T(4,128)S(1)}, bf16[64,128,512]{2,1,0:T(8,128)(2,1)}, /*index=5*/s32[]{:T(128)}) while((s32[]{:T(128)}, bf16[8,4,128,512]{3,2,1,0:T(8,128)(2,1)}, bf16[8,4,8,128,128]{4,3,2,1,0:T(8,128)(2,1)}, ...), condition=%wide.region_6.7_spmd, body=%wide.region_5.6_spmd.sunk | while | flops 536872064 | bytes 14686033 | solution.py:70
  116.3 6.1 gather_fusion
  122.4 4.0 fusion.60
  126.5 6.1 gather_fusion
  132.7 4.0 fusion.60
  136.8 6.1 gather_fusion
  143.0 4.1 fusion.60
  147.1 6.1 gather_fusion
  157.4 6.1 gather_fusion
  167.6 6.1 gather_fusion
  173.8 4.1 fusion.60
  177.9 6.1 gather_fusion
  188.2 6.1 gather_fusion
  198.4 23.4 %scatter_custom_fusion.2 = bf16[8192,512]{1,0:T(8,128)(2,1)} fusion(s32[4096]{0:T(1024)S(1)} %get-tuple-element.166, bf16[4096,512]{1,0:T(8,128)(2,1)} %bitcast.110, bf16[]{:T(256)} %constant.146.clone.1), kind=kCustom, calls=%fused_computation.27 | custom fusion | bytes 8389120 | tf_op jit(solution)/shard_map/scatter | solution.py:75
  221.8 6.0 all-to-all-start.1
  228.4 101.8 %all-to-all-done.1 = bf16[128,64,512]{2,1,0:T(8,128)(2,1)} async-done(((bf16[128,64,512]{2,1,0:T(8,128)(2,1)}), bf16[128,64,512]{2,1,0:T(8,128)(2,1)}, u32[]{:S(2)}, u32[]{:S(2)}) %all-to-all-start.1) | async-done | bytes 8388640 | tf_op jit(solution)/shard_map/all_to_all | solution.py:77
  330.2 21.9 %gather_fusion.2 = bf16[4096,512]{1,0:T(8,128)(2,1)} fusion(bf16[8192,512]{1,0:T(8,128)(2,1)} %bitcast.26, s32[4096]{0:T(1024)S(1)} %broadcast_clamp_fusion.1), kind=kCustom, calls=%fused_computation.2 | custom fusion | bytes 8404992 | tf_op jit(solution)/shard_map/gather | solution.py:84
  365.2 10.2 %all-to-all-start.2 = ((bf16[128,64,512]{2,1,0:T(8,128)(2,1)}), bf16[128,64,512]{2,1,0:T(8,128)(2,1)}, u32[]{:S(2)}, u32[]{:S(2)}) async-start(bf16[128,64,512]{2,1,0:T(8,128)(2,1)} %bitcast.95), calls=%async_computation.2 | async-start | bytes 16777216 | tf_op jit(solution)/shard_map/all_to_all | solution.py:115
  375.7 12.0 %copy.42 = bf16[1,1,32,8,128,128]{4,5,3,2,1,0:T(8,128)(2,1)} copy(bf16[1,1,32,8,128,128]{5,4,3,2,1,0:T(8,128)(2,1)} %bitcast.99) | data formatting | bytes 16777216 | tf_op args[2]
  387.7 90.3 %all-to-all-done.2 = bf16[128,64,512]{2,1,0:T(8,128)(2,1)} async-done(((bf16[128,64,512]{2,1,0:T(8,128)(2,1)}), bf16[128,64,512]{2,1,0:T(8,128)(2,1)}, u32[]{:S(2)}, u32[]{:S(2)}) %all-to-all-start.2) | async-done | bytes 8388640 | tf_op jit(solution)/shard_map/all_to_all | solution.py:115
  478.0 21.9 %gather_fusion.3 = bf16[4096,512]{1,0:T(8,128)(2,1)} fusion(bf16[8192,512]{1,0:T(8,128)(2,1)} %bitcast.31, s32[4096]{0:T(1024)S(1)} %get-tuple-element.165), kind=kCustom, calls=%fused_computation.3 | custom fusion | bytes 8404992 | tf_op jit(solution)/shard_map/gather | solution.py:115
  499.9 7.9 broadcast_in_dim.36
  507.8 198.1 %while.24 = (s32[]{:T(128)}, f32[64,128,512]{2,1,0:T(8,128)}, s32[32,8]{1,0:T(8,128)S(1)}, bf16[32,8,128,128]{2,3,1,0:T(8,128)(2,1)}, bf16[32,128,512]{2,1,0:T(8...) while((s32[]{:T(128)}, f32[64,128,512]{2,1,0:T(8,128)}, s32[32,8]{1,0:T(8,128)S(1)}, ...), condition=%wide.region_13.14_spmd, body=%wide.region_11.13_spmd.sunk | while | flops 538968192 | bytes 35129368 | solution.py:132
  507.9 5.8 fusion.64
  513.7 18.9 %scatter_fusion = f32[64,128,512]{2,1,0:T(8,128)} fusion(f32[64,128,512]{2,1,0:T(8,128)} %get-tuple-element.267, s32[32]{0:T(128)S(1)} %fusion.63, f32[32,128,512]{2,1,0:T(8,128)} %bitcast.88), kind=kCustom, calls=%fused_computation.6.clone.1 | custom fusion | flops 2097152 | bytes 25165952 | tf_op jit(solution)/shard_map/while/body/eval_jaxpr/scatter-add | solution.py:129
  532.7 5.8 fusion.64
  538.5 18.8 %scatter_fusion = f32[64,128,512]{2,1,0:T(8,128)} fusion(f32[64,128,512]{2,1,0:T(8,128)} %get-tuple-element.267, s32[32]{0:T(128)S(1)} %fusion.63, f32[32,128,512]{2,1,0:T(8,128)} %bitcast.88), kind=kCustom, calls=%fused_computation.6.clone.1 | custom fusion | flops 2097152 | bytes 25165952 | tf_op jit(solution)/shard_map/while/body/eval_jaxpr/scatter-add | solution.py:129
  557.4 5.8 fusion.64
  563.2 18.9 %scatter_fusion = f32[64,128,512]{2,1,0:T(8,128)} fusion(f32[64,128,512]{2,1,0:T(8,128)} %get-tuple-element.267, s32[32]{0:T(128)S(1)} %fusion.63, f32[32,128,512]{2,1,0:T(8,128)} %bitcast.88), kind=kCustom, calls=%fused_computation.6.clone.1 | custom fusion | flops 2097152 | bytes 25165952 | tf_op jit(solution)/shard_map/while/body/eval_jaxpr/scatter-add | solution.py:129
  582.2 5.8 fusion.64
  588.0 18.8 %scatter_fusion = f32[64,128,512]{2,1,0:T(8,128)} fusion(f32[64,128,512]{2,1,0:T(8,128)} %get-tuple-element.267, s32[32]{0:T(128)S(1)} %fusion.63, f32[32,128,512]{2,1,0:T(8,128)} %bitcast.88), kind=kCustom, calls=%fused_computation.6.clone.1 | custom fusion | flops 2097152 | bytes 25165952 | tf_op jit(solution)/shard_map/while/body/eval_jaxpr/scatter-add | solution.py:129
  606.9 5.8 fusion.64
  612.7 18.8 %scatter_fusion = f32[64,128,512]{2,1,0:T(8,128)} fusion(f32[64,128,512]{2,1,0:T(8,128)} %get-tuple-element.267, s32[32]{0:T(128)S(1)} %fusion.63, f32[32,128,512]{2,1,0:T(8,128)} %bitcast.88), kind=kCustom, calls=%fused_computation.6.clone.1 | custom fusion | flops 2097152 | bytes 25165952 | tf_op jit(solution)/shard_map/while/body/eval_jaxpr/scatter-add | solution.py:129
  631.6 5.8 fusion.64
  637.4 18.8 %scatter_fusion = f32[64,128,512]{2,1,0:T(8,128)} fusion(f32[64,128,512]{2,1,0:T(8,128)} %get-tuple-element.267, s32[32]{0:T(128)S(1)} %fusion.63, f32[32,128,512]{2,1,0:T(8,128)} %bitcast.88), kind=kCustom, calls=%fused_computation.6.clone.1 | custom fusion | flops 2097152 | bytes 25165952 | tf_op jit(solution)/shard_map/while/body/eval_jaxpr/scatter-add | solution.py:129
  656.3 5.8 fusion.64
  662.2 19.0 %scatter_fusion = f32[64,128,512]{2,1,0:T(8,128)} fusion(f32[64,128,512]{2,1,0:T(8,128)} %get-tuple-element.267, s32[32]{0:T(128)S(1)} %fusion.63, f32[32,128,512]{2,1,0:T(8,128)} %bitcast.88), kind=kCustom, calls=%fused_computation.6.clone.1 | custom fusion | flops 2097152 | bytes 25165952 | tf_op jit(solution)/shard_map/while/body/eval_jaxpr/scatter-add | solution.py:129
  681.2 5.8 fusion.64
  687.1 18.8 %scatter_fusion = f32[64,128,512]{2,1,0:T(8,128)} fusion(f32[64,128,512]{2,1,0:T(8,128)} %get-tuple-element.267, s32[32]{0:T(128)S(1)} %fusion.63, f32[32,128,512]{2,1,0:T(8,128)} %bitcast.88), kind=kCustom, calls=%fused_computation.6.clone.1 | custom fusion | flops 2097152 | bytes 25165952 | tf_op jit(solution)/shard_map/while/body/eval_jaxpr/scatter-add | solution.py:129
  705.9 9.0 convert_element_type.75
  717.9 99.7 %reduce-scatter.2.cloned.1.call-done = bf16[512,512]{1,0:T(8,128)(2,1)} async-done(((bf16[8192,512]{1,0:T(8,128)(2,1)}), bf16[512,512]{1,0:T(8,128)(2,1)}) %reduce-scatter.2.cloned.1.call-update) | async-done | bytes 524304 | tf_op jit(solution)/shard_map/reduce_scatter | solution.py:133
  822.1 8.9 all-to-all-start.3
  831.0 150.9 %all-reduce.3.cloned.1.call-done = (f32[512,512]{0,1:T(8,128)}, f32[512,512]{0,1:T(8,128)}) async-done(((f32[512,512]{0,1:T(8,128)}, f32[512,512]{0,1:T(8,128)}), (f32[512,512]{0,1:T(8,128)}, f32[512,512]{0,1:T(8,128)})) %all-reduce.3.cloned.1.call-update) | async-done | bytes 2097168 | tf_op jit(solution)/shard_map/psum | solution.py:143
  (131 shorter events, 66.4 us)
Async XLA Ops:
  7.2 347.9 %copy-start = (bf16[512,512]{1,0:T(8,128)(2,1)S(1)}, bf16[512,512]{1,0:T(8,128)(2,1)}, u32[]{:S(2)}) copy-start(bf16[512,512]{1,0:T(8,128)(2,1)} %param.20) | copy-start | bytes 1572868
  9.1 37.4 %copy-start.8 = (s32[512]{0:T(512)S(1)}, s32[512]{0:T(512)}, u32[]{:S(2)}) copy-start(s32[512]{0:T(512)} %param.18) | copy-start | bytes 6148
  13.1 30.8 %all-to-all-start = ((bf16[128,8,512]{2,1,0:T(8,128)(2,1)}), bf16[128,8,512]{2,1,0:T(8,128)(2,1)S(1)}, u32[]{:S(2)}, u32[]{:S(2)}) async-start(bf16[128,8,512]{2,1,0:T(8,128)(2,1)} %bitcast.21), calls=%async_computation | async-start | bytes 2097152 | tf_op jit(solution)/shard_map/all_to_all | solution.py:52
  24.6 91.6 %all-gather.4.cloned.1.call-start = ((), (), s32[]{:S(2)}) async-start(), calls=%async_computation.6 | async-start | bytes 8912896 | tf_op jit(solution)/shard_map/all_gather | solution.py:54
  68.1 4.5 copy-start.9
  221.8 6.1 copy-start.10
  221.8 6.2 copy-start.2
  221.8 6.2 copy-start.4
  221.8 108.4 %all-to-all-start.1 = ((bf16[128,64,512]{2,1,0:T(8,128)(2,1)}), bf16[128,64,512]{2,1,0:T(8,128)(2,1)}, u32[]{:S(2)}, u32[]{:S(2)}) async-start(bf16[128,64,512]{2,1,0:T(8,128)(2,1)} %bitcast.94), calls=%async_computation.1 | async-start | bytes 16777216 | tf_op jit(solution)/shard_map/all_to_all | solution.py:77
  352.1 2.9 copy-start.11
  355.1 1.7 copy-start.5
  356.7 359.7 %copy-start.3 = (bf16[512,512]{1,0:T(8,128)(2,1)}, bf16[512,512]{1,0:T(8,128)(2,1)S(1)}, u32[]{:S(2)}) copy-start(bf16[512,512]{1,0:T(8,128)(2,1)S(1)} %get-tuple-element.169) | copy-start | bytes 1572868
  365.2 112.8 %all-to-all-start.2 = ((bf16[128,64,512]{2,1,0:T(8,128)(2,1)}), bf16[128,64,512]{2,1,0:T(8,128)(2,1)}, u32[]{:S(2)}, u32[]{:S(2)}) async-start(bf16[128,64,512]{2,1,0:T(8,128)(2,1)} %bitcast.95), calls=%async_computation.2 | async-start | bytes 16777216 | tf_op jit(solution)/shard_map/all_to_all | solution.py:115
  375.4 442.2 %reduce-scatter.2.cloned.1.call-start = ((), (), s32[]{:S(2)}) async-start(), calls=%async_computation.5 | async-start | bytes 8912896 | tf_op jit(solution)/shard_map/reduce_scatter | solution.py:133
  714.9 1.5 copy-start.6
  714.9 266.9 %all-reduce.3.cloned.1.call-start = ((), (), s32[]{:S(2)}) async-start(), calls=%async_computation.7 | async-start | bytes 4194304 | tf_op jit(solution)/shard_map/psum | solution.py:143
  822.1 163.9 %all-to-all-start.3 = ((bf16[128,8,512]{2,1,0:T(8,128)(2,1)}), bf16[128,8,512]{2,1,0:T(8,128)(2,1)}, u32[]{:S(2)}, u32[]{:S(2)}) async-start(bf16[128,8,512]{2,1,0:T(8,128)(2,1)} %convert_bitcast_fusion), calls=%async_computation.4 | async-start | bytes 2097152 | tf_op jit(solution)/shard_map/all_to_all | solution.py:139
  981.8 2.7 copy-start.7
  986.0 6.6 copy-start.1
Sparse Core Ops, SparseCore 0:
  46.6 69.4 all-gather.3
  715.0 102.5 reduce-scatter.1
  823.3 158.5 all-reduce.2
where the time goes:
time: 1000 us; the launch traced here: 999 us
  waiting for transfers between devices  470 us (47%)
  local copies, waits for them, and re-layouts  194 us (19%)
  other arithmetic  176 us (18%)
  matrix products  87.6 us (9%)
  starting transfers between devices  37 us (4%)
  blocking collectives  20.5 us (2%)
  between operations  14 us (1%)
    scatter-add x8, other arithmetic, add_group(): totals.at[col_part.reshape(-1)]  151 us
    psum x1, waiting for transfers between devices, on_device(): summed_grads = lax.psum((grad_terms[0], grad_terms[1]), ('row', 'col'))  151 us
    all_to_all x1, waiting for transfers between devices, on_device(): lax.all_to_all(outgoing, ('row', 'col'), split_axis=0, concat_axis=0, til...  102 us
    reduce_scatter x1, waiting for transfers between devices, on_device(): lax.psum_scatter(back_terms.astype(jnp.bfloat16), 'col', scatter_dimensio...  99.7 us
    all_to_all x1, waiting for transfers between devices, on_device(): lax.all_to_all(outgoing_back, ('row', 'col'), split_axis=0, concat_axis=0...  90.3 us
    gather x8, local copies, waits for them, and re-layouts, one_group(): chosen = feat_tiles[operands[1]]  49.1 us
    dot_general x8, matrix products, add_group(): jnp.einsum('tkij,tif->tkjf', mask_part, row_part, preferred_element_type=...  46.4 us
    gather x1, local copies, waits for them, and re-layouts, rank_running(): return jnp.take_along_axis(running, group_keys[:, None], axis=1)[:, 0] - 1  33 us
  transfers between devices with their start and end apart: 7, of which 6 were waited for; matrix products, arithmetic and copies ran while one was open for 7% of the time, Pallas kernels for 0%

commit v1 on v0

v1 whole, which is shorter than its diff:
```python
import functools
import math

import jax
import jax.numpy as jnp
from jax import lax
from jax.experimental import pallas as pl
from jax.experimental.pallas import tpu as pltpu
from jax.sharding import PartitionSpec as P

F32 = jnp.float32
BF16 = jnp.bfloat16
VMEM_LIMIT = 60 * 1024 * 1024
ROW_T = (((0,), (0,)), ((), ()))
COL_T = (((1,), (1,)), ((), ()))


def rank_within(group_keys, order_keys):
    same_group = group_keys[:, None] == group_keys[None, :]
    earlier = order_keys[None, :] < order_keys[:, None]
    return jnp.sum(same_group & earlier, axis=1)


def params(**kw):
    return pltpu.CompilerParams(vmem_limit_bytes=VMEM_LIMIT, **kw)


def pack_kernel(flat_ref, data_ref, out_ref):
    step = pl.program_id(0)
    size = out_ref.shape[0]
    slot = lax.broadcasted_iota(jnp.int32, (size, flat_ref.shape[1]), 0) + step * size
    pick = jnp.where(slot == flat_ref[...], 1.0, 0.0).astype(BF16)
    out_ref[...] = jnp.dot(pick, data_ref[...], preferred_element_type=F32).astype(BF16)


def pack(flat, data, slots):
    rows, width = data.shape
    parts = 4
    return pl.pallas_call(
        pack_kernel,
        grid=(parts,),
        in_specs=[
            pl.BlockSpec((1, rows), lambda i: (0, 0)),
            pl.BlockSpec((rows, width), lambda i: (0, 0)),
        ],
        out_specs=pl.BlockSpec((slots // parts, width), lambda i: (i, 0)),
        out_shape=jax.ShapeDtypeStruct((slots, width), BF16),
        name="pack",
    )(flat.reshape(1, rows), data)


def unpack_kernel(flat_ref, data_ref, out_ref):
    size = out_ref.shape[0]
    slot = lax.broadcasted_iota(jnp.int32, (size, data_ref.shape[0]), 1)
    pick = jnp.where(slot == flat_ref[...], 1.0, 0.0).astype(BF16)
    out_ref[...] = jnp.dot(pick, data_ref[...], preferred_element_type=F32).astype(BF16)


def unpack(flat, data):
    slots, width = data.shape
    rows = flat.shape[0]
    parts = 4
    return pl.pallas_call(
        unpack_kernel,
        grid=(parts,),
        in_specs=[
            pl.BlockSpec((rows // parts, 1), lambda i: (i, 0)),
            pl.BlockSpec((slots, width), lambda i: (0, 0)),
        ],
        out_specs=pl.BlockSpec((rows // parts, width), lambda i: (i, 0)),
        out_shape=jax.ShapeDtypeStruct((rows, width), BF16),
        name="unpack",
    )(flat.reshape(rows, 1), data)


def gather_product_kernel(cols_ref, mask_ref, x_ref, out_ref):
    row = pl.program_id(0)
    breadth, tile = mask_ref.shape[1], mask_ref.shape[2]
    left = jnp.concatenate([mask_ref[0, k] for k in range(breadth)], axis=1)
    right = jnp.concatenate(
        [x_ref[pl.ds(pl.multiple_of(cols_ref[row, k] * tile, tile), tile), :] for k in range(breadth)], axis=0
    )
    out_ref[...] = jnp.dot(left, right, preferred_element_type=F32).astype(BF16)


def gather_product(columns, pattern, x):
    trows, breadth, tile, _ = pattern.shape
    width = x.shape[1]
    return pl.pallas_call(
        gather_product_kernel,
        grid_spec=pltpu.PrefetchScalarGridSpec(
            num_scalar_prefetch=1,
            grid=(trows,),
            in_specs=[
                pl.BlockSpec((1, breadth, tile, tile), lambda i, c: (i, 0, 0, 0)),
                pl.BlockSpec(x.shape, lambda i, c: (0, 0), pipeline_mode=pl.Buffered(1)),
            ],
            out_specs=pl.BlockSpec((tile, width), lambda i, c: (i, 0)),
        ),
        out_shape=jax.ShapeDtypeStruct((trows * tile, width), BF16),
        compiler_params=params(),
        name="gather_product",
    )(columns, pattern, x)


def scatter_product_kernel(cols_ref, mask_ref, s_ref, out_ref, total):
    row = pl.program_id(0)
    breadth, tile = mask_ref.shape[1], mask_ref.shape[2]

    @pl.when(row == 0)
    def _():
        total[...] = jnp.zeros_like(total)

    for k in range(breadth):
        piece = lax.dot_general(mask_ref[0, k], s_ref[...], ROW_T, preferred_element_type=F32)
        at = pl.ds(pl.multiple_of(cols_ref[row, k] * tile, tile), tile)
        total[at, :] += piece

    @pl.when(row == pl.num_programs(0) - 1)
    def _():
        out_ref[...] = total[...].astype(BF16)


def scatter_product(columns, pattern, spread, total_rows):
    trows, breadth, tile, _ = pattern.shape
    width = spread.shape[1]
    return pl.pallas_call(
        scatter_product_kernel,
        grid_spec=pltpu.PrefetchScalarGridSpec(
            num_scalar_prefetch=1,
            grid=(trows,),
            in_specs=[
                pl.BlockSpec((1, breadth, tile, tile), lambda i, c: (i, 0, 0, 0)),
                pl.BlockSpec((tile, width), lambda i, c: (i, 0)),
            ],
            out_specs=pl.BlockSpec((total_rows, width), lambda i, c: (0, 0), pipeline_mode=pl.Buffered(1)),
            scratch_shapes=[pltpu.VMEM((total_rows, width), F32)],
        ),
        out_shape=jax.ShapeDtypeStruct((total_rows, width), BF16),
        compiler_params=params(),
        name="scatter_product",
    )(columns, pattern, spread)


def dense_kernel(
    part_ref, x_ref, extra_ref, ws_ref, wn_ref, hidden_ref, own_ref, spread_ref, gs_ref, gn_ref
):
    step = pl.program_id(0)
    width = x_ref.shape[1]
    x = x_ref[...]
    degrees = extra_ref[:, pl.ds(width, 1)].astype(F32)
    cot = extra_ref[:, pl.ds(0, width)].astype(F32)
    summed = part_ref[0].astype(F32)
    for r in range(1, part_ref.shape[0]):
        summed = summed + part_ref[r].astype(F32)
    aggregate = (summed / degrees).astype(BF16)
    preact = jnp.dot(x, ws_ref[...], preferred_element_type=F32) + jnp.dot(
        aggregate, wn_ref[...], preferred_element_type=F32
    )
    gate = jax.nn.sigmoid(preact)
    hidden_ref[...] = (preact * gate).astype(BF16)
    slopes = (cot * gate * (1.0 + preact * (1.0 - gate))).astype(BF16)
    gs = lax.dot_general(x, slopes, ROW_T, preferred_element_type=F32)
    gn = lax.dot_general(aggregate, slopes, ROW_T, preferred_element_type=F32)

    @pl.when(step == 0)
    def _():
        gs_ref[...] = gs
        gn_ref[...] = gn

    @pl.when(step > 0)
    def _():
        gs_ref[...] += gs
        gn_ref[...] += gn

    own_ref[...] = lax.dot_general(slopes, ws_ref[...], COL_T, preferred_element_type=F32)
    spread_ref[...] = (
        lax.dot_general(slopes, wn_ref[...], COL_T, preferred_element_type=F32) / degrees
    ).astype(BF16)


def dense(parts, x, extra, ws, wn):
    rows, width = x.shape
    step = 128
    whole = lambda i: (0, 0)
    rowwise = lambda i: (i, 0)
    return pl.pallas_call(
        dense_kernel,
        grid=(rows // step,),
        in_specs=[
            pl.BlockSpec((parts.shape[0], step, width), lambda i: (0, i, 0)),
            pl.BlockSpec((step, width), rowwise),
            pl.BlockSpec((step, extra.shape[1]), rowwise),
            pl.BlockSpec((width, width), whole),
            pl.BlockSpec((width, width), whole),
        ],
        out_specs=[
            pl.BlockSpec((step, width), rowwise),
            pl.BlockSpec((step, width), rowwise),
            pl.BlockSpec((step, width), rowwise),
            pl.BlockSpec((width, width), whole),
            pl.BlockSpec((width, width), whole),
        ],
        out_shape=[
            jax.ShapeDtypeStruct((rows, width), BF16),
            jax.ShapeDtypeStruct((rows, width), F32),
            jax.ShapeDtypeStruct((rows, width), BF16),
            jax.ShapeDtypeStruct((width, width), F32),
            jax.ShapeDtypeStruct((width, width), F32),
        ],
        compiler_params=params(),
        name="dense",
    )(parts, x, extra, ws, wn)


def swap_all(data, axes):
    return lax.all_to_all(data, axes, split_axis=0, concat_axis=0, tiled=True)


def on_device(
    features, tile_cols, tile_masks, degree, owner_nodes, owner_position, self_weight, neigh_weight, cotangent
):
    rows, width = features.shape
    n_row, n_col = lax.axis_size("row"), lax.axis_size("col")
    devices = n_row * n_col
    slot_count = 2 * rows // devices
    slots = devices * slot_count
    pattern, columns = tile_masks[0, 0], tile_cols[0, 0]
    own_dest = owner_nodes // rows
    own_flat = own_dest * slot_count + rank_within(own_dest, jnp.arange(rows, dtype=jnp.int32))
    node_source = owner_position // rows
    node_flat = node_source * slot_count + rank_within(node_source, owner_position)

    both = ("row", "col")
    degree_cols = jnp.broadcast_to(degree.astype(BF16)[:, None], (rows, 128))
    node_x = unpack(node_flat, swap_all(pack(own_flat, features, slots), both))
    extra = jnp.concatenate([cotangent, degree_cols], axis=1)
    node_extra = unpack(node_flat, swap_all(pack(own_flat, extra, slots), both))
    column_x = lax.all_gather(node_x, "col", axis=0, tiled=True)
    partial_rows = gather_product(columns, pattern, column_x)
    parts = swap_all(partial_rows.reshape(n_row, rows, width), "row")
    hidden, own_back, spread, grad_self, grad_neigh = dense(parts, node_x, node_extra, self_weight, neigh_weight)
    grid_spread = lax.all_gather(spread, "row", axis=0, tiled=True)
    back = scatter_product(columns, pattern, grid_spread, n_col * rows)
    node_back = lax.psum_scatter(back, "col", scatter_dimension=0, tiled=True)
    grad_node = (own_back + node_back.astype(F32)).astype(BF16)
    hidden_out = unpack(own_flat, swap_all(pack(node_flat, hidden, slots), both))
    grad_out = unpack(own_flat, swap_all(pack(node_flat, grad_node, slots), both))
    sums = lax.psum((grad_self, grad_neigh), both)
    grad_scale = 1.0 / math.sqrt(rows * devices)
    return hidden_out, grad_out, sums[0] * grad_scale, sums[1] * grad_scale


def solution(mesh):
    both = P(("row", "col"))
    wide = P(("row", "col"), None)
    placed = (
        wide,
        P("row", "col", None, None),
        P("row", "col", None, None, None, None),
        both,
        both,
        both,
        P(),
        P(),
        wide,
    )
    return jax.shard_map(
        on_device, mesh=mesh, in_specs=placed, out_specs=(wide, wide, P(), P()), check_vma=False
    )
```

time: 1000 us -> 580 us (0.58)
  local copies, waits for them, and re-layouts: 194 us -> 5.6 us
  other arithmetic: 176 us -> 10.7 us
  Pallas kernels: 0 us -> 96 us
  matrix products: 87.6 us -> 0 us
  waiting for transfers between devices: 470 us -> 415 us
  blocking collectives: 20.5 us -> 0 us
    scatter-add x8 -> x0, other arithmetic: 151 us -> none  [add_group(): totals.at[col_part.reshape(-1)]]
    all_to_all x4 -> x5, waiting for transfers between devices: 209 us -> 60.1 us  [swap_all(): return lax.all_to_all(data, axes, split_axis=0, concat_axis=0, tiled=True)]
    gather x13 -> x0, local copies, waits for them, and re-layouts: 131 us -> none  [the longest x8 49.1 us: one_group(): chosen = feat_tiles[operands[1]]]
    all_gather x1 -> x2, waiting for transfers between devices: 10.3 us -> 120 us  [the longest x1 70.4 us: on_device(): column_x = lax.all_gather(node_x, 'col', axis=0, tiled=True)]
    pallas_call x0 -> x11, Pallas kernels: none -> 96 us  [the longest x1 30.2 us: scatter_product(): pl.pallas_call(scatter_product_kernel, grid_spec=pltpu.PrefetchScalarGrid...]
    dot_general x22 -> x0, matrix products: 87.6 us -> none  [the longest x8 46.4 us: add_group(): jnp.einsum('tkij,tif->tkjf', mask_part, row_part, preferred_element_type=...]
    scatter x3 -> x0, local copies, waits for them, and re-layouts: 30.6 us -> none  [the longest x1 23.4 us: on_device(): outgoing = jnp.zeros((all_devices * wide_slots, feat_width), jnp.bfloat16...]
    all_gather x1 -> x0, blocking collectives: 20.5 us -> none  [on_device(): grid_lookup = lax.all_gather(owner_position, 'row', axis=0, tiled=True)]
  transfers between devices with their start and end apart: 7 -> 9, of which waited for: 6 -> 6; matrix products, arithmetic and copies ran while one was open for 7% -> 2% of each run, Pallas kernels for 0% -> 8%
where the time goes in v1:
time: 580 us; the launch traced here: 577 us
  waiting for transfers between devices  415 us (72%)
  Pallas kernels  96 us (17%)
  starting transfers between devices  36.4 us (6%)
  between operations  13.9 us (2%)
  other arithmetic  10.7 us (2%)
    psum x1, waiting for transfers between devices, on_device(): sums = lax.psum((grad_self, grad_neigh), both)  145 us
    reduce_scatter x1, waiting for transfers between devices, on_device(): node_back = lax.psum_scatter(back, 'col', scatter_dimension=0, tiled=True)  88.7 us
    all_gather x1, waiting for transfers between devices, on_device(): column_x = lax.all_gather(node_x, 'col', axis=0, tiled=True)  70.4 us
    all_to_all x5, waiting for transfers between devices, swap_all(): return lax.all_to_all(data, axes, split_axis=0, concat_axis=0, tiled=True)  60.1 us
    all_gather x1, waiting for transfers between devices, on_device(): grid_spread = lax.all_gather(spread, 'row', axis=0, tiled=True)  49.6 us
    all_to_all x5, starting transfers between devices, swap_all(): return lax.all_to_all(data, axes, split_axis=0, concat_axis=0, tiled=True)  36.3 us
    pallas_call x1, Pallas kernels, scatter_product(): pl.pallas_call(scatter_product_kernel, grid_spec=pltpu.PrefetchScalarGrid...  30.2 us
    pallas_call x1, Pallas kernels, gather_product(): pl.pallas_call(gather_product_kernel, grid_spec=pltpu.PrefetchScalarGridS...  26.1 us
  transfers between devices with their start and end apart: 9, of which 6 were waited for; matrix products, arithmetic and copies ran while one was open for 2% of the time, Pallas kernels for 8%

profile of v1, /device:TPU:1, one launch (start us, length us, event | category | flops | bytes accessed | tf_op | source)
XLA Modules:
  0.0 577.4 jit_solution(12983891471997072398)
XLA Ops:
  7.2 0.8 add_select_fusion.1
  7.9 0.3 convert_reduce_fusion.1
  8.2 1.3 multiply_add_fusion.1
  9.5 3.4 pack.4
  12.8 11.5 %all-to-all-start = ((bf16[128,8,512]{2,1,0:T(8,128)(2,1)}), bf16[128,8,512]{2,1,0:T(8,128)(2,1)S(1)}, u32[]{:S(2)}, u32[]{:S(2)}) async-start(bf16[128,8,512]{2,1,0:T(8,128)(2,1)} %bitcast.25), calls=%async_computation | async-start | bytes 2097152 | tf_op jit(solution)/shard_map/all_to_all | solution.py:217
  24.3 0.0 all-gather.3.cloned.1.call-start
  24.4 0.7 add_select_fusion
  25.1 1.1 convert_reduce_fusion
  26.2 0.7 multiply_add_fusion
  26.9 0.9 copy.20.flat_ref
  27.7 15.9 %all-to-all-done = bf16[128,8,512]{2,1,0:T(8,128)(2,1)S(1)} async-done(((bf16[128,8,512]{2,1,0:T(8,128)(2,1)}), bf16[128,8,512]{2,1,0:T(8,128)(2,1)S(1)}, u32[]{:S(2)}, u32[]{:S(2)}) %all-to-all-start) | async-done | bytes 1048608 | tf_op jit(solution)/shard_map/all_to_all | solution.py:217
  43.6 1.0 copy-done.3
  44.6 4.2 unpack.4.x_ref
  48.8 0.0 all-gather.3.cloned.1.call-update
  48.8 0.1 broadcast_in_dim.2
  49.0 0.9 pad_maximum_fusion.data_ref
  49.8 3.7 pack.5
  53.5 4.6 all-to-all-start.2
  58.1 0.7 copy.19
  58.8 70.4 %all-gather.3.cloned.1.call-done.x_ref = bf16[8192,512]{1,0:T(8,128)(2,1)} async-done(((bf16[512,512]{1,0:T(8,128)(2,1)}), bf16[8192,512]{1,0:T(8,128)(2,1)}) %all-gather.3.cloned.1.call-update) | async-done | bytes 8388624 | tf_op jit(solution)/shard_map/all_gather | solution.py:239
  129.2 26.1 %gather_product.1 = bf16[4096,512]{1,0:T(8,128)(2,1)} custom-call(s32[32,8]{1,0:T(8,128)} %bitcast.26, bf16[32,8,128,128]{3,2,1,0:T(8,128)(2,1)} %bitcast.15, bf16[8192,512]{1,0:T(8,128)(2,1)} %all-gather.3.cloned.1.call-done.x_ref), custom_call_target="tpu_custom_call" | custom-call | tf_op jit(solution)/shard_map/gather_product/pallas_call | solution.py:89
  155.3 0.0 all-to-all-done.2
  155.3 1.1 copy-done
  156.4 4.6 all-to-all-start.1
  160.9 0.0 all-gather.5.cloned.1.call-start
  161.0 4.4 unpack.5.extra_ref
  165.4 44.2 %all-to-all-done.1.part_ref = bf16[8,512,512]{2,1,0:T(8,128)(2,1)} async-done(((bf16[8,512,512]{2,1,0:T(8,128)(2,1)}), bf16[8,512,512]{2,1,0:T(8,128)(2,1)}, u32[]{:S(2)}, u32[]{:S(2)}) %all-to-all-start.1) | async-done | bytes 4194336 | tf_op jit(solution)/shard_map/all_to_all | solution.py:217
  209.6 8.9 %dense.1 = (bf16[512,512]{1,0:T(8,128)(2,1)}, f32[512,512]{1,0:T(8,128)}, bf16[512,512]{1,0:T(8,128)(2,1)}, f32[512,512]{1,0:T(8,128)}, f32[512,512]{1,0:T(8,128)}) custom-call(bf16[8,512,512]{2,1,0:T(8,128)(2,1)} %all-to-all-done.1.part_ref, bf16[512,512]{1,0:T(8,128)(2,1)} %unpack.4.x_ref, bf16[512,640]{1,0:T(8,128)(2,1)} %unpack.5.extra_ref, ...), custom_call_target="tpu_custom_call" | custom-call | tf_op jit(solution)/shard_map/dense/pallas_call | solution.py:187
  218.5 0.0 all-gather.5.cloned.1.call-update
  218.5 0.0 reduce-scatter.2.cloned.1.call-start
  218.6 49.6 %all-gather.5.cloned.1.call-done.s_ref = bf16[4096,512]{1,0:T(8,128)(2,1)} async-done(((bf16[512,512]{1,0:T(8,128)(2,1)}), bf16[4096,512]{1,0:T(8,128)(2,1)}) %all-gather.5.cloned.1.call-update) | async-done | bytes 4194320 | tf_op jit(solution)/shard_map/all_gather | solution.py:243
  268.1 30.2 %scatter_product.1 = bf16[8192,512]{1,0:T(8,128)(2,1)} custom-call(s32[32,8]{1,0:T(8,128)} %bitcast.27, bf16[32,8,128,128]{3,2,1,0:T(8,128)(2,1)} %bitcast.16, bf16[4096,512]{1,0:T(8,128)(2,1)} %all-gather.5.cloned.1.call-done.s_ref), custom_call_target="tpu_custom_call" | custom-call | tf_op jit(solution)/shard_map/scatter_product/pallas_call | solution.py:127
  298.3 0.0 reduce-scatter.2.cloned.1.call-update
  298.3 0.0 copy-start.4
  298.3 3.5 pack.6
  301.8 7.2 %all-to-all-start.3 = ((bf16[128,8,512]{2,1,0:T(8,128)(2,1)}), bf16[128,8,512]{2,1,0:T(8,128)(2,1)S(1)}, u32[]{:S(2)}, u32[]{:S(2)}) async-start(bf16[128,8,512]{2,1,0:T(8,128)(2,1)} %bitcast.23), calls=%async_computation.3 | async-start | bytes 2097152 | tf_op jit(solution)/shard_map/all_to_all | solution.py:217
  309.1 0.0 all-reduce.3.cloned.1.call-start
  309.1 0.5 all-reduce.3.cloned.1.call-update
  309.6 88.7 %reduce-scatter.2.cloned.1.call-done = bf16[512,512]{1,0:T(8,128)(2,1)} async-done(((bf16[8192,512]{1,0:T(8,128)(2,1)}), bf16[512,512]{1,0:T(8,128)(2,1)}) %reduce-scatter.2.cloned.1.call-update) | async-done | bytes 524304 | tf_op jit(solution)/shard_map/reduce_scatter | solution.py:245
  398.3 2.0 add_convert_fusion.data_ref
  400.3 3.4 pack.7
  403.7 8.5 %all-to-all-start.4 = ((bf16[128,8,512]{2,1,0:T(8,128)(2,1)}), bf16[128,8,512]{2,1,0:T(8,128)(2,1)S(1)}, u32[]{:S(2)}, u32[]{:S(2)}) async-start(bf16[128,8,512]{2,1,0:T(8,128)(2,1)} %bitcast.24), calls=%async_computation.5 | async-start | bytes 2097152 | tf_op jit(solution)/shard_map/all_to_all | solution.py:217
  412.2 0.9 copy.22.flat_ref
  413.0 4.2 unpack.6
  417.2 145.4 %all-reduce.3.cloned.1.call-done = (f32[512,512]{1,0:T(8,128)}, f32[512,512]{1,0:T(8,128)}) async-done(((f32[512,512]{1,0:T(8,128)}, f32[512,512]{1,0:T(8,128)}), (f32[512,512]{1,0:T(8,128)}, f32[512,512]{1,0:T(8,128)})) %all-reduce.3.cloned.1.call-update) | async-done | bytes 2097168 | tf_op jit(solution)/shard_map/psum | solution.py:249
  562.6 3.1 broadcast_multiply_fusion
  565.7 1.0 copy-done.2
  566.7 4.2 unpack.7
  (19 shorter events, 0.0 us)
Async XLA Ops:
  7.2 41.6 %copy-start.9 = (s32[512]{0:T(512)S(1)}, s32[512]{0:T(512)}, u32[]{:S(2)}) copy-start(s32[512]{0:T(512)} %param.12) | copy-start | bytes 6148
  7.2 41.8 %copy-start.5 = (bf16[512,512]{1,0:T(8,128)(2,1)S(1)}, bf16[512,512]{1,0:T(8,128)(2,1)}, u32[]{:S(2)}) copy-start(bf16[512,512]{1,0:T(8,128)(2,1)} %param.17) | copy-start | bytes 1572868
  12.8 30.8 %all-to-all-start = ((bf16[128,8,512]{2,1,0:T(8,128)(2,1)}), bf16[128,8,512]{2,1,0:T(8,128)(2,1)S(1)}, u32[]{:S(2)}, u32[]{:S(2)}) async-start(bf16[128,8,512]{2,1,0:T(8,128)(2,1)} %bitcast.25), calls=%async_computation | async-start | bytes 2097152 | tf_op jit(solution)/shard_map/all_to_all | solution.py:217
  24.3 104.8 %all-gather.3.cloned.1.call-start = ((), (), s32[]{:S(2)}) async-start(), calls=%async_computation.6 | async-start | bytes 8912896 | tf_op jit(solution)/shard_map/all_gather | solution.py:239
  26.8 26.7 %copy-start.7 = (s32[512]{0:T(512)}, s32[512]{0:T(512)S(1)}, u32[]{:S(2)}) copy-start(s32[512]{0:T(512)S(1)} %multiply_add_fusion) | copy-start | bytes 6148
  43.6 1.0 copy-start.3
  44.6 13.5 %copy-start.8 = (s32[1,1,32,8]{2,3,1,0:T(8,128)S(1)}, s32[1,1,32,8]{2,3,1,0:T(8,128)}, u32[]{:S(2)}) copy-start(s32[1,1,32,8]{2,3,1,0:T(8,128)} %param.10) | copy-start | bytes 3076
  53.5 101.7 %all-to-all-start.2 = ((bf16[128,8,640]{2,1,0:T(8,128)(2,1)}), bf16[128,8,640]{2,1,0:T(8,128)(2,1)S(1)}, u32[]{:S(2)}, u32[]{:S(2)}) async-start(bf16[128,8,640]{2,1,0:T(8,128)(2,1)} %bitcast.19), calls=%async_computation.2 | async-start | bytes 2621440 | tf_op jit(solution)/shard_map/all_to_all | solution.py:217
  155.3 1.1 copy-start
  156.4 53.2 %all-to-all-start.1 = ((bf16[8,512,512]{2,1,0:T(8,128)(2,1)}), bf16[8,512,512]{2,1,0:T(8,128)(2,1)}, u32[]{:S(2)}, u32[]{:S(2)}) async-start(bf16[8,512,512]{2,1,0:T(8,128)(2,1)} %bitcast.17), calls=%async_computation.1 | async-start | bytes 8388608 | tf_op jit(solution)/shard_map/all_to_all | solution.py:217
  160.9 107.2 %all-gather.5.cloned.1.call-start = ((), (), s32[]{:S(2)}) async-start(), calls=%async_computation.7 | async-start | bytes 4718592 | tf_op jit(solution)/shard_map/all_gather | solution.py:243
  218.5 179.8 %reduce-scatter.2.cloned.1.call-start = ((), (), s32[]{:S(2)}) async-start(), calls=%async_computation.8 | async-start | bytes 8912896 | tf_op jit(solution)/shard_map/reduce_scatter | solution.py:245
  298.3 100.0 %copy-start.4 = (f32[512,512]{1,0:T(8,128)S(1)}, f32[512,512]{1,0:T(8,128)}, u32[]{:S(2)}) copy-start(f32[512,512]{1,0:T(8,128)} %get-tuple-element.10) | copy-start | bytes 3145732
  301.8 101.9 %all-to-all-start.3 = ((bf16[128,8,512]{2,1,0:T(8,128)(2,1)}), bf16[128,8,512]{2,1,0:T(8,128)(2,1)S(1)}, u32[]{:S(2)}, u32[]{:S(2)}) async-start(bf16[128,8,512]{2,1,0:T(8,128)(2,1)} %bitcast.23), calls=%async_computation.3 | async-start | bytes 2097152 | tf_op jit(solution)/shard_map/all_to_all | solution.py:217
  309.0 103.1 %copy-start.6 = (s32[512]{0:T(512)S(1)}, s32[512]{0:T(512)}, u32[]{:S(2)}) copy-start(s32[512]{0:T(512)} %multiply_add_fusion.1) | copy-start | bytes 6148
  309.1 253.5 %all-reduce.3.cloned.1.call-start = ((), (), s32[]{:S(2)}) async-start(), calls=%async_computation.9 | async-start | bytes 4194304 | tf_op jit(solution)/shard_map/psum | solution.py:249
  403.7 9.3 %copy-start.1 = (bf16[128,8,512]{2,1,0:T(8,128)(2,1)}, bf16[128,8,512]{2,1,0:T(8,128)(2,1)S(1)}, u32[]{:S(2)}) copy-start(bf16[128,8,512]{2,1,0:T(8,128)(2,1)S(1)} %all-to-all-done.3) | copy-start | bytes 3145732
  403.7 162.0 %all-to-all-start.4 = ((bf16[128,8,512]{2,1,0:T(8,128)(2,1)}), bf16[128,8,512]{2,1,0:T(8,128)(2,1)S(1)}, u32[]{:S(2)}, u32[]{:S(2)}) async-start(bf16[128,8,512]{2,1,0:T(8,128)(2,1)} %bitcast.24), calls=%async_computation.5 | async-start | bytes 2097152 | tf_op jit(solution)/shard_map/all_to_all | solution.py:217
  565.7 1.0 copy-start.2
Sparse Core Ops, SparseCore 0:
  48.9 80.2 all-gather.2
  218.6 49.4 all-gather.4
  298.4 99.8 reduce-scatter.1
  403.8 158.7 all-reduce.2

commit v2 on v1

v2 whole, which is shorter than its diff:
```python
import math

import jax
import jax.numpy as jnp
from jax import lax
from jax.experimental import pallas as pl
from jax.experimental.pallas import tpu as pltpu
from jax.sharding import PartitionSpec as P

F32 = jnp.float32
BF16 = jnp.bfloat16
MESH = pl.DeviceIdType.MESH
VMEM_LIMIT = 60 * 1024 * 1024
ROW_T = (((0,), (0,)), ((), ()))
COL_T = (((1,), (1,)), ((), ()))


def rank_within(group_keys, order_keys):
    same_group = group_keys[:, None] == group_keys[None, :]
    earlier = order_keys[None, :] < order_keys[:, None]
    return jnp.sum(same_group & earlier, axis=1)


def params(**kw):
    return pltpu.CompilerParams(vmem_limit_bytes=VMEM_LIMIT, **kw)


def pack_kernel(flat_ref, data_ref, out_ref):
    step = pl.program_id(0)
    size = out_ref.shape[0]
    slot = lax.broadcasted_iota(jnp.int32, (size, flat_ref.shape[1]), 0) + step * size
    pick = jnp.where(slot == flat_ref[...], 1.0, 0.0).astype(BF16)
    out_ref[...] = jnp.dot(pick, data_ref[...], preferred_element_type=F32).astype(BF16)


def pack(flat, data, slots):
    rows, width = data.shape
    parts = 4
    return pl.pallas_call(
        pack_kernel,
        grid=(parts,),
        in_specs=[
            pl.BlockSpec((1, rows), lambda i: (0, 0)),
            pl.BlockSpec((rows, width), lambda i: (0, 0)),
        ],
        out_specs=pl.BlockSpec((slots // parts, width), lambda i: (i, 0)),
        out_shape=jax.ShapeDtypeStruct((slots, width), BF16),
        name="pack",
    )(flat.reshape(1, rows), data)


def unpack_kernel(flat_ref, data_ref, out_ref):
    size = out_ref.shape[0]
    slot = lax.broadcasted_iota(jnp.int32, (size, data_ref.shape[0]), 1)
    pick = jnp.where(slot == flat_ref[...], 1.0, 0.0).astype(BF16)
    out_ref[...] = jnp.dot(pick, data_ref[...], preferred_element_type=F32).astype(BF16)


def unpack(flat, data):
    slots, width = data.shape
    rows = flat.shape[0]
    parts = 4
    return pl.pallas_call(
        unpack_kernel,
        grid=(parts,),
        in_specs=[
            pl.BlockSpec((rows // parts, 1), lambda i: (i, 0)),
            pl.BlockSpec((slots, width), lambda i: (0, 0)),
        ],
        out_specs=pl.BlockSpec((rows // parts, width), lambda i: (i, 0)),
        out_shape=jax.ShapeDtypeStruct((rows, width), BF16),
        name="unpack",
    )(flat.reshape(rows, 1), data)


def unpack_tiles_kernel(flat_ref, data_ref, out_ref):
    size = out_ref.shape[2]
    slot = lax.broadcasted_iota(jnp.int32, (size, data_ref.shape[0]), 1)
    pick = jnp.where(slot == flat_ref[...], 1.0, 0.0).astype(BF16)
    rows = jnp.dot(pick, data_ref[...], preferred_element_type=F32).astype(BF16)
    for c in range(4):
        out_ref[c, 0] = rows[:, c * 128 : (c + 1) * 128]


def unpack_tiles(flat, data):
    slots, width = data.shape
    rows = flat.shape[0]
    return pl.pallas_call(
        unpack_tiles_kernel,
        grid=(4,),
        in_specs=[
            pl.BlockSpec((rows // 4, 1), lambda i: (i, 0)),
            pl.BlockSpec((slots, width), lambda i: (0, 0)),
        ],
        out_specs=pl.BlockSpec((4, 1, 128, 128), lambda i: (0, i, 0, 0)),
        out_shape=jax.ShapeDtypeStruct((4, 4, 128, 128), BF16),
        name="unpack_tiles",
    )(flat.reshape(rows, 1), data)

def place():
    r, c = lax.axis_index("row"), lax.axis_index("col")
    return r // 4, r % 4, c // 8, (c // 2) % 4, c % 2


def at_device(xl, y, xh, z, k):
    return (xl * 4 + y, xh * 8 + z * 2 + k)


def meet(peers):
    barrier = pltpu.get_barrier_semaphore()
    for peer in peers:
        pl.semaphore_signal(barrier, inc=1, device_id=peer, device_id_type=MESH)
    pl.semaphore_wait(barrier, len(peers))


def all_peers():
    xl, y, xh, z, k = place()
    peers = [
        at_device(1 - xl, y, xh, z, k),
        at_device(xl, y, 1 - xh, z, k),
        at_device(xl, y, xh, z, 1 - k),
    ]
    for d in (1, 2, 3):
        peers.append(at_device(xl, (y + d) % 4, xh, z, k))
        peers.append(at_device(xl, y, xh, (z + d) % 4, k))
    return peers


class Copies:
    def __init__(self, send, recv):
        self.send, self.recv, self.used, self.started = send, recv, 0, []

    def remote(self, src, dst, device):
        i, self.used = self.used, self.used + 1
        copy = pltpu.make_async_remote_copy(
            src_ref=src, dst_ref=dst, send_sem=self.send.at[i], recv_sem=self.recv.at[i],
            device_id=device, device_id_type=MESH,
        )
        copy.start()
        self.started.append(copy)
        return copy

    def local(self, src, dst):
        i, self.used = self.used, self.used + 1
        copy = pltpu.make_async_copy(src, dst, self.recv.at[i])
        copy.start()
        return copy

    def finish(self):
        for copy in self.started:
            copy.wait_send()


FAR_FIRST = (2, 1, 3)


def forward_kernel(cols_ref, x_ref, mask_hbm, out_ref, mask, *rest):
    held, part, near, cross, crossed, (send, recv) = (
        rest[0:4], rest[4:8], rest[8:12], rest[12:16], rest[16:20], rest[20:22]
    )
    xl, y, xh, z, k = place()
    copies = Copies(send, recv)
    mask_copy = copies.local(mask_hbm, mask)
    meet(all_peers())
    tiles = lambda slot: pl.ds(slot * 4, 4)
    mine, pair = k * 8 + xh * 4 + z, k * 8 + (1 - xh) * 4 + z
    gathered, over, swap, row_copies, cross_copy = [[] for _ in range(4)], {}, {}, {}, {}

    def own(c):
        gathered[c].append(copies.local(x_ref.at[c], held[c].at[tiles(mine)]))
        over[c] = copies.remote(x_ref.at[c], held[c].at[tiles(mine)], at_device(xl, y, 1 - xh, z, k))
        for d in FAR_FIRST:
            to = at_device(xl, y, xh, (z + d) % 4, k)
            gathered[c].append(copies.remote(x_ref.at[c], held[c].at[tiles(mine)], to))

    def onward(c):
        over[c].wait_recv()
        for d in FAR_FIRST:
            to = at_device(xl, y, xh, (z + d) % 4, k)
            gathered[c].append(copies.remote(held[c].at[tiles(pair)], held[c].at[tiles(pair)], to))

    def swap_cores(c):
        gathered[c][0].wait()
        for copy in gathered[c][1:]:
            copy.wait_recv()
        half = held[c].at[pl.ds(k * 32, 32)]
        swap[c] = copies.remote(half, half, at_device(xl, y, xh, z, 1 - k))

    def product(c):
        swap[c].wait_recv()
        row_copies[c] = []
        for d in FAR_FIRST + (0,):
            to_y = (y + d) % 4

            def one(q, carry):
                t = (q // 4) * 16 + to_y * 4 + q % 4
                left = jnp.concatenate([mask[t * 8 + j] for j in range(8)], axis=1)
                right = jnp.concatenate([held[c][cols_ref[t * 8 + j]] for j in range(8)], axis=0)
                part[c][to_y * 8 + q] = jnp.dot(left, right, preferred_element_type=F32).astype(BF16)
                return carry

            lax.fori_loop(0, 8, one, 0)
            if d:
                i = FAR_FIRST.index(d)
                row_copies[c].append(
                    copies.remote(
                        part[c].at[pl.ds(to_y * 8, 8)], near[c].at[pl.ds(i * 8, 8)], at_device(xl, to_y, xh, z, k)
                    )
                )

    def row_sum(c, side, i):
        total = part[c][y * 8 + side * 4 + i].astype(F32)
        for n in range(3):
            total = total + near[c][n * 8 + side * 4 + i].astype(F32)
        return total

    def sum_rows(c):
        for copy in row_copies[c]:
            copy.wait_recv()

        def one(i, carry):
            cross[c][i] = row_sum(c, 1 - xl, i).astype(BF16)
            return carry

        lax.fori_loop(0, 4, one, 0)
        cross_copy[c] = copies.remote(cross[c], crossed[c], at_device(1 - xl, y, xh, z, k))

    def sum_cross(c):
        cross_copy[c].wait_recv()

        def one(i, carry):
            out_ref[c, i] = row_sum(c, xl, i) + crossed[c][i].astype(F32)
            return carry

        lax.fori_loop(0, 4, one, 0)

    own(0)
    onward(0)
    own(1)
    onward(1)
    swap_cores(0)
    own(2)
    mask_copy.wait()
    product(0)
    onward(2)
    swap_cores(1)
    own(3)
    product(1)
    onward(3)
    swap_cores(2)
    sum_rows(0)
    product(2)
    swap_cores(3)
    sum_rows(1)
    sum_cross(0)
    product(3)
    sum_rows(2)
    sum_cross(1)
    sum_rows(3)
    sum_cross(2)
    sum_cross(3)
    copies.finish()


def remote_params(ident):
    return params(collective_id=ident, has_side_effects=True)


SMEM_SPEC = pl.BlockSpec(memory_space=pltpu.SMEM)
VMEM_SPEC = pl.BlockSpec(memory_space=pltpu.VMEM)
ANY_SPEC = pl.BlockSpec(memory_space=pl.ANY)


def tile_buffer(count):
    return pltpu.VMEM((count, 128, 128), BF16)


def forward_exchange(cols, x, masks):
    return pl.pallas_call(
        forward_kernel,
        in_specs=[SMEM_SPEC, VMEM_SPEC, ANY_SPEC],
        out_specs=VMEM_SPEC,
        out_shape=jax.ShapeDtypeStruct(x.shape, F32),
        scratch_shapes=[tile_buffer(256)]
        + [tile_buffer(64)] * 4
        + [tile_buffer(32)] * 4
        + [tile_buffer(24)] * 4
        + [tile_buffer(4)] * 8
        + [pltpu.SemaphoreType.DMA((64,)), pltpu.SemaphoreType.DMA((64,))],
        compiler_params=remote_params(0),
        name="forward_exchange",
    )(cols, x, masks)


def backward_kernel(pick_ref, from_ref, keep_ref, last_ref, some_ref, s_ref, mask_hbm, out_ref, mask, chain, *rest):
    held, block, traded, paired, near, cross, crossed, (send, recv) = (
        rest[0:4], rest[4:8], rest[8:12], rest[12:16], rest[16:20], rest[20:24], rest[24:28], rest[28:30]
    )
    xl, y, xh, z, k = place()
    copies = Copies(send, recv)
    mask_copy = copies.local(mask_hbm, mask)
    meet(all_peers())
    tiles = lambda slot: pl.ds(slot * 4, 4)
    mine, pair = xl * 4 + y, (1 - xl) * 4 + y
    gathered, over, trade, col_copies, cross_copy = [[] for _ in range(4)], {}, {}, {}, {}

    def own(c):
        gathered[c].append(copies.local(s_ref.at[c], held[c].at[tiles(mine)]))
        over[c] = copies.remote(s_ref.at[c], held[c].at[tiles(mine)], at_device(1 - xl, y, xh, z, k))
        for d in FAR_FIRST:
            to = at_device(xl, (y + d) % 4, xh, z, k)
            gathered[c].append(copies.remote(s_ref.at[c], held[c].at[tiles(mine)], to))

    def onward(c):
        over[c].wait_recv()
        for d in FAR_FIRST:
            to = at_device(xl, (y + d) % 4, xh, z, k)
            gathered[c].append(copies.remote(held[c].at[tiles(pair)], held[c].at[tiles(pair)], to))

    def product(c):
        gathered[c][0].wait()
        for copy in gathered[c][1:]:
            copy.wait_recv()

        def one(g, total):
            for u in range(8):
                e = g * 8 + u
                piece = jnp.dot(held[c][from_ref[e]], mask[pick_ref[e]], preferred_element_type=F32)
                total = total * keep_ref[e] + piece
                chain[e] = total.astype(BF16)
            return total

        lax.fori_loop(0, 32, one, jnp.zeros((128, 128), F32))

        def settle(p, carry):
            block[c][p] = (chain[last_ref[p]].astype(F32) * some_ref[p]).astype(BF16)
            return carry

        lax.fori_loop(0, 64, settle, 0)
        trade[c] = copies.remote(
            block[c].at[pl.ds((1 - k) * 32, 32)], traded[c], at_device(xl, y, xh, z, 1 - k)
        )

    def sum_cores(c):
        trade[c].wait_recv()

        def one(i, carry):
            paired[c][i] = (block[c][k * 32 + i].astype(F32) + traded[c][i].astype(F32)).astype(BF16)
            return carry

        lax.fori_loop(0, 32, one, 0)
        col_copies[c] = []
        for i, d in enumerate(FAR_FIRST):
            to_z = (z + d) % 4
            col_copies[c].append(
                copies.remote(
                    paired[c].at[pl.ds(to_z * 8, 8)], near[c].at[pl.ds(i * 8, 8)], at_device(xl, y, xh, to_z, k)
                )
            )

    def col_sum(c, side, i):
        total = paired[c][z * 8 + side * 4 + i].astype(F32)
        for n in range(3):
            total = total + near[c][n * 8 + side * 4 + i].astype(F32)
        return total

    def sum_cols(c):
        for copy in col_copies[c]:
            copy.wait_recv()

        def one(i, carry):
            cross[c][i] = col_sum(c, 1 - xh, i).astype(BF16)
            return carry

        lax.fori_loop(0, 4, one, 0)
        cross_copy[c] = copies.remote(cross[c], crossed[c], at_device(xl, y, 1 - xh, z, k))

    def sum_cross(c):
        cross_copy[c].wait_recv()

        def one(i, carry):
            out_ref[c, i] = col_sum(c, xh, i) + crossed[c][i].astype(F32)
            return carry

        lax.fori_loop(0, 4, one, 0)

    own(0)
    onward(0)
    own(1)
    onward(1)
    own(2)
    mask_copy.wait()
    product(0)
    onward(2)
    own(3)
    sum_cores(0)
    product(1)
    onward(3)
    sum_cores(1)
    sum_cols(0)
    product(2)
    sum_cores(2)
    sum_cols(1)
    sum_cross(0)
    product(3)
    sum_cores(3)
    sum_cols(2)
    sum_cross(1)
    sum_cols(3)
    sum_cross(2)
    sum_cross(3)
    copies.finish()


def backward_exchange(tables, s, masks):
    return pl.pallas_call(
        backward_kernel,
        in_specs=[SMEM_SPEC] * 5 + [VMEM_SPEC, ANY_SPEC],
        out_specs=VMEM_SPEC,
        out_shape=jax.ShapeDtypeStruct(s.shape, F32),
        scratch_shapes=[tile_buffer(256), tile_buffer(256)]
        + [tile_buffer(32)] * 4
        + [tile_buffer(64)] * 4
        + [tile_buffer(32)] * 8
        + [tile_buffer(24)] * 4
        + [tile_buffer(4)] * 8
        + [pltpu.SemaphoreType.DMA((64,)), pltpu.SemaphoreType.DMA((64,))],
        compiler_params=remote_params(1),
        name="backward_exchange",
    )(*tables, s, masks)


def column_order(columns):
    flat = columns.reshape(-1)
    count = flat.shape[0]
    block = flat // 4
    xh, z, k = block // 8, (block // 2) % 4, block % 2
    held_tile = (k * 8 + xh * 4 + z) * 4 + flat % 4
    back_tile = (k * 8 + z * 2 + xh) * 4 + flat % 4
    entry = jnp.arange(count, dtype=jnp.int32)
    key = back_tile * count + entry
    rank = jnp.sum((key[None, :] < key[:, None]).astype(jnp.int32), axis=1)
    hit = rank[None, :] == entry[:, None]
    pick = jnp.sum(jnp.where(hit, entry[None, :], 0), axis=1)
    sorted_tile = jnp.sum(jnp.where(hit, back_tile[None, :], 0), axis=1)
    before = jnp.concatenate([jnp.full((1,), -1, jnp.int32), sorted_tile[:-1]])
    keep = (sorted_tile == before).astype(F32)
    spot = jnp.arange(64, dtype=jnp.int32)
    upto = jnp.sum((back_tile[None, :] <= spot[:, None]).astype(jnp.int32), axis=1)
    some = jnp.any(back_tile[None, :] == spot[:, None], axis=1).astype(F32)
    last = jnp.maximum(upto - 1, 0)
    return held_tile, (pick, pick // 8, keep, last, some)


def dense_kernel(
    sum_ref, x_ref, extra_ref, ws_ref, wn_ref, hidden_ref, own_ref, spread_ref, gs_ref, gn_ref
):
    step = pl.program_id(0)
    width = hidden_ref.shape[1]
    x = jnp.concatenate([x_ref[c, 0] for c in range(4)], axis=1)
    degrees = extra_ref[:, pl.ds(width, 1)].astype(F32)
    cot = extra_ref[:, pl.ds(0, width)].astype(F32)
    summed = jnp.concatenate([sum_ref[c, 0] for c in range(4)], axis=1)
    aggregate = (summed / degrees).astype(BF16)
    preact = jnp.dot(x, ws_ref[...], preferred_element_type=F32) + jnp.dot(
        aggregate, wn_ref[...], preferred_element_type=F32
    )
    gate = jax.nn.sigmoid(preact)
    hidden_ref[...] = (preact * gate).astype(BF16)
    slopes = (cot * gate * (1.0 + preact * (1.0 - gate))).astype(BF16)
    gs = lax.dot_general(x, slopes, ROW_T, preferred_element_type=F32)
    gn = lax.dot_general(aggregate, slopes, ROW_T, preferred_element_type=F32)

    @pl.when(step == 0)
    def _():
        gs_ref[...] = gs
        gn_ref[...] = gn

    @pl.when(step > 0)
    def _():
        gs_ref[...] += gs
        gn_ref[...] += gn

    own_ref[...] = lax.dot_general(slopes, ws_ref[...], COL_T, preferred_element_type=F32)
    spread = lax.dot_general(slopes, wn_ref[...], COL_T, preferred_element_type=F32) / degrees
    for c in range(4):
        spread_ref[c, 0] = spread[:, c * 128 : (c + 1) * 128].T.astype(BF16)


def dense(summed, x, extra, ws, wn):
    rows, width = extra.shape[0], ws.shape[0]
    step = 128
    whole = lambda i: (0, 0)
    rowwise = lambda i: (i, 0)
    tiled = pl.BlockSpec((4, 1, step, 128), lambda i: (0, i, 0, 0))
    return pl.pallas_call(
        dense_kernel,
        grid=(rows // step,),
        in_specs=[
            tiled,
            tiled,
            pl.BlockSpec((step, extra.shape[1]), rowwise),
            pl.BlockSpec((width, width), whole),
            pl.BlockSpec((width, width), whole),
        ],
        out_specs=[
            pl.BlockSpec((step, width), rowwise),
            pl.BlockSpec((step, width), rowwise),
            tiled,
            pl.BlockSpec((width, width), whole),
            pl.BlockSpec((width, width), whole),
        ],
        out_shape=[
            jax.ShapeDtypeStruct((rows, width), BF16),
            jax.ShapeDtypeStruct((rows, width), F32),
            jax.ShapeDtypeStruct(x.shape, BF16),
            jax.ShapeDtypeStruct((width, width), F32),
            jax.ShapeDtypeStruct((width, width), F32),
        ],
        compiler_params=params(),
        name="dense",
    )(summed, x, extra, ws, wn)


def join_kernel(own_ref, back_ref, out_ref):
    back = jnp.concatenate([back_ref[c, 0].T for c in range(4)], axis=1)
    out_ref[...] = (own_ref[...] + back).astype(BF16)


def join(own_back, back):
    rows, width = own_back.shape
    return pl.pallas_call(
        join_kernel,
        grid=(rows // 128,),
        in_specs=[
            pl.BlockSpec((128, width), lambda i: (i, 0)),
            pl.BlockSpec((4, 1, 128, 128), lambda i: (0, i, 0, 0)),
        ],
        out_specs=pl.BlockSpec((128, width), lambda i: (i, 0)),
        out_shape=jax.ShapeDtypeStruct((rows, width), BF16),
        name="join",
    )(own_back, back)


def swap_all(data, axes):
    return lax.all_to_all(data, axes, split_axis=0, concat_axis=0, tiled=True)


def on_device(
    features, tile_cols, tile_masks, degree, owner_nodes, owner_position, self_weight, neigh_weight, cotangent
):
    rows, width = features.shape
    n_row, n_col = lax.axis_size("row"), lax.axis_size("col")
    devices = n_row * n_col
    slot_count = 2 * rows // devices
    slots = devices * slot_count
    masks = tile_masks.reshape(256, 128, 128)
    own_dest = owner_nodes // rows
    own_flat = own_dest * slot_count + rank_within(own_dest, jnp.arange(rows, dtype=jnp.int32))
    node_source = owner_position // rows
    node_flat = node_source * slot_count + rank_within(node_source, owner_position)
    cols, tables = column_order(tile_cols[0, 0])

    both = ("row", "col")
    degree_cols = jnp.broadcast_to(degree.astype(BF16)[:, None], (rows, 128))
    node_x = unpack_tiles(node_flat, swap_all(pack(own_flat, features, slots), both))
    extra = jnp.concatenate([cotangent, degree_cols], axis=1)
    node_extra = unpack(node_flat, swap_all(pack(own_flat, extra, slots), both))
    summed = forward_exchange(cols, node_x, masks)
    hidden, own_back, spread, grad_self, grad_neigh = dense(summed, node_x, node_extra, self_weight, neigh_weight)
    sums = lax.psum((grad_self, grad_neigh), both)
    back = backward_exchange(tables, spread, masks)
    grad_node = join(own_back, back)
    hidden_out = unpack(own_flat, swap_all(pack(node_flat, hidden, slots), both))
    grad_out = unpack(own_flat, swap_all(pack(node_flat, grad_node, slots), both))
    grad_scale = 1.0 / math.sqrt(rows * devices)
    return hidden_out, grad_out, sums[0] * grad_scale, sums[1] * grad_scale


def solution(mesh):
    both = P(("row", "col"))
    wide = P(("row", "col"), None)
    placed = (
        wide,
        P("row", "col", None, None),
        P("row", "col", None, None, None, None),
        both,
        both,
        both,
        P(),
        P(),
        wide,
    )
    return jax.shard_map(
        on_device, mesh=mesh, in_specs=placed, out_specs=(wide, wide, P(), P()), check_vma=False
    )
```

time: 580 us -> 433 us (0.75)
  waiting for transfers between devices: 415 us -> 163 us
  Pallas kernels: 96 us -> 212 us
  starting transfers between devices: 36.4 us -> 26.4 us
    pallas_call x3 -> x5, Pallas kernels: 65.1 us -> 186 us  [the longest x1 86.9 us: backward_exchange(): pl.pallas_call(backward_kernel, in_specs=[SMEM_SPEC] * 5 + [VMEM_SPEC, AN...]
    all_gather x2 -> x0, waiting for transfers between devices: 120 us -> none  [the longest x1 70.4 us: on_device(): column_x = lax.all_gather(node_x, 'col', axis=0, tiled=True)]
    reduce_scatter x1 -> x0, waiting for transfers between devices: 88.7 us -> none  [on_device(): node_back = lax.psum_scatter(back, 'col', scatter_dimension=0, tiled=True)]
    psum x1, waiting for transfers between devices: 145 us -> 118 us  [on_device(): sums = lax.psum((grad_self, grad_neigh), both)]
    all_to_all x5 -> x4, waiting for transfers between devices: 60.1 us -> 44.3 us  [swap_all(): return lax.all_to_all(data, axes, split_axis=0, concat_axis=0, tiled=True)]
    all_to_all x5 -> x4, starting transfers between devices: 36.3 us -> 26.4 us  [swap_all(): return lax.all_to_all(data, axes, split_axis=0, concat_axis=0, tiled=True)]
    pallas_call x4 -> x3, Pallas kernels: 16.9 us -> 12.7 us  [unpack(): pl.pallas_call(unpack_kernel, grid=(parts,), in_specs=[pl.BlockSpec((rows...]
  transfers between devices with their start and end apart: 9 -> 5, of which waited for: 6 -> 4; matrix products, arithmetic and copies ran while one was open for 2% -> 2% of each run, Pallas kernels for 8% -> 24%
where the time goes in v2:
time: 433 us; the launch traced here: 431 us
  Pallas kernels  212 us (49%)
  waiting for transfers between devices  163 us (38%)
  starting transfers between devices  26.4 us (6%)
  between operations  14.2 us (3%)
  other arithmetic  10.1 us (2%)
  local copies, waits for them, and re-layouts  5.05 us (1%)
    psum x1, waiting for transfers between devices, on_device(): sums = lax.psum((grad_self, grad_neigh), both)  118 us
    pallas_call x1, Pallas kernels, backward_exchange(): pl.pallas_call(backward_kernel, in_specs=[SMEM_SPEC] * 5 + [VMEM_SPEC, AN...  86.9 us
    pallas_call x1, Pallas kernels, forward_exchange(): pl.pallas_call(forward_kernel, in_specs=[SMEM_SPEC, VMEM_SPEC, ANY_SPEC],...  81.9 us
    all_to_all x4, waiting for transfers between devices, swap_all(): return lax.all_to_all(data, axes, split_axis=0, concat_axis=0, tiled=True)  44.3 us
    all_to_all x4, starting transfers between devices, swap_all(): return lax.all_to_all(data, axes, split_axis=0, concat_axis=0, tiled=True)  26.4 us
    pallas_call x4, Pallas kernels, pack(): pl.pallas_call(pack_kernel, grid=(parts,), in_specs=[pl.BlockSpec((1, row...  13.8 us
    pallas_call x3, Pallas kernels, unpack(): pl.pallas_call(unpack_kernel, grid=(parts,), in_specs=[pl.BlockSpec((rows...  12.7 us
    pallas_call x1, Pallas kernels, dense(): pl.pallas_call(dense_kernel, grid=(rows // step,), in_specs=[tiled, tiled...  9.14 us
  transfers between devices with their start and end apart: 5, of which 4 were waited for; matrix products, arithmetic and copies ran while one was open for 2% of the time, Pallas kernels for 24%

profile of v2, /device:TPU:1, one launch (start us, length us, event | category | flops | bytes accessed | tf_op | source)
XLA Modules:
  0.0 431.4 jit_solution(12291073006716407381)
XLA Ops:
  7.2 0.7 add_select_fusion.1
  7.9 0.3 convert_reduce_fusion.1
  8.1 1.3 multiply_add_fusion.1
  9.4 3.4 pack.4
  12.8 11.5 %all-to-all-start = ((bf16[128,8,512]{2,1,0:T(8,128)(2,1)}), bf16[128,8,512]{2,1,0:T(8,128)(2,1)S(1)}, u32[]{:S(2)}, u32[]{:S(2)}) async-start(bf16[128,8,512]{2,1,0:T(8,128)(2,1)} %bitcast.23), calls=%async_computation | async-start | bytes 2097152 | tf_op jit(solution)/shard_map/all_to_all | solution.py:546
  24.3 0.0 copy-done.9
  24.3 0.1 copy.18
  24.4 0.1 reshape_squeeze.3
  24.4 0.0 copy-done.10
  24.5 0.1 broadcast_in_dim.16
  24.6 0.9 pad_maximum_fusion.data_ref
  25.5 3.7 pack.5
  29.2 0.3 convert_reduce_fusion
  29.6 13.9 %all-to-all-done = bf16[128,8,512]{2,1,0:T(8,128)(2,1)S(1)} async-done(((bf16[128,8,512]{2,1,0:T(8,128)(2,1)}), bf16[128,8,512]{2,1,0:T(8,128)(2,1)S(1)}, u32[]{:S(2)}, u32[]{:S(2)}) %all-to-all-start) | async-done | bytes 1048608 | tf_op jit(solution)/shard_map/all_to_all | solution.py:546
  43.5 1.0 copy-done.1
  44.5 4.6 %all-to-all-start.1 = ((bf16[128,8,640]{2,1,0:T(8,128)(2,1)}), bf16[128,8,640]{2,1,0:T(8,128)(2,1)S(1)}, u32[]{:S(2)}, u32[]{:S(2)}) async-start(bf16[128,8,640]{2,1,0:T(8,128)(2,1)} %bitcast.18), calls=%async_computation.1 | async-start | bytes 2621440 | tf_op jit(solution)/shard_map/all_to_all | solution.py:546
  49.1 0.1 fusion.1
  49.2 0.9 copy.19.flat_ref
  50.1 0.6 convert_element_type.27.some_ref
  50.7 0.1 convert_reduce_fusion.3
  50.8 0.2 convert_reduce_fusion.2
  50.9 0.2 select_reduce_fusion
  51.1 0.5 add_maximum_fusion.last_ref
  51.6 0.6 and_select_fusion.from_ref
  52.2 0.7 compare_convert_fusion.keep_ref
  52.9 0.6 multiply_add_fusion.3.cols_ref
  53.5 4.2 unpack_tiles.1.x_ref
  57.7 81.9 %forward_exchange.1.sum_ref = f32[4,4,128,128]{3,2,1,0:T(8,128)} custom-call(s32[256]{0:T(256)} %multiply_add_fusion.3.cols_ref, bf16[4,4,128,128]{3,2,1,0:T(8,128)(2,1)} %unpack_tiles.1.x_ref, bf16[256,128,128]{2,1,0:T(8,128)(2,1)} %bitcast.16), custom_call_target="tpu_custom_call" | custom-call | tf_op jit(solution)/shard_map/forward_exchange/pallas_call | solution.py:279
  139.6 0.0 all-to-all-done.1
  139.6 1.1 copy-done
  140.7 4.4 %unpack.3.extra_ref = bf16[512,640]{1,0:T(8,128)(2,1)} custom-call(s32[512,1]{1,0:T(8,128)} %copy.19.flat_ref, bf16[1024,640]{1,0:T(8,128)(2,1)} %bitcast.19), custom_call_target="tpu_custom_call" | custom-call | tf_op jit(solution)/shard_map/unpack/pallas_call | solution.py:63
  145.1 9.1 %dense.1 = (bf16[512,512]{1,0:T(8,128)(2,1)}, f32[512,512]{1,0:T(8,128)}, bf16[4,4,128,128]{3,2,1,0:T(8,128)(2,1)}, f32[512,512]{1,0:T(8,128)}, f32[512,512]{1,0:T(8,128)}) custom-call(f32[4,4,128,128]{3,2,1,0:T(8,128)} %forward_exchange.1.sum_ref, bf16[4,4,128,128]{3,2,1,0:T(8,128)(2,1)} %unpack_tiles.1.x_ref, bf16[512,640]{1,0:T(8,128)(2,1)} %unpack.3.extra_ref, ...), custom_call_target="tpu_custom_call" | custom-call | tf_op jit(solution)/shard_map/dense/pallas_call | solution.py:496
  154.2 86.9 %backward_exchange.1.back_ref = f32[4,4,128,128]{3,2,1,0:T(8,128)} custom-call(s32[256]{0:T(256)} %copy-done.8, s32[256]{0:T(256)} %and_select_fusion.from_ref, f32[256]{0:T(256)} %compare_convert_fusion.keep_ref, s32[64]{0:T(128)} %add_maximum_fusion.last_ref, f32[64]{0:T(128)} %convert_element_type.27.some_ref, ...), custom_call_target="tpu_custom_call" | custom-call | tf_op jit(solution)/shard_map/backward_exchange/pallas_call | solution.py:416
  241.1 3.7 join.1.data_ref
  244.8 3.4 pack.7
  248.1 5.8 %all-to-all-start.3 = ((bf16[128,8,512]{2,1,0:T(8,128)(2,1)}), bf16[128,8,512]{2,1,0:T(8,128)(2,1)S(1)}, u32[]{:S(2)}, u32[]{:S(2)}) async-start(bf16[128,8,512]{2,1,0:T(8,128)(2,1)} %bitcast.24), calls=%async_computation.3 | async-start | bytes 2097152 | tf_op jit(solution)/shard_map/all_to_all | solution.py:546
  253.9 0.0 all-reduce.3.cloned.1.call-start
  254.0 0.7 all-reduce.3.cloned.1.call-update
  254.7 3.4 pack.6
  258.1 15.1 %all-to-all-done.3 = bf16[128,8,512]{2,1,0:T(8,128)(2,1)S(1)} async-done(((bf16[128,8,512]{2,1,0:T(8,128)(2,1)}), bf16[128,8,512]{2,1,0:T(8,128)(2,1)S(1)}, u32[]{:S(2)}, u32[]{:S(2)}) %all-to-all-start.3) | async-done | bytes 1048608 | tf_op jit(solution)/shard_map/all_to_all | solution.py:546
  273.2 4.6 %all-to-all-start.2 = ((bf16[128,8,512]{2,1,0:T(8,128)(2,1)}), bf16[128,8,512]{2,1,0:T(8,128)(2,1)S(1)}, u32[]{:S(2)}, u32[]{:S(2)}) async-start(bf16[128,8,512]{2,1,0:T(8,128)(2,1)} %bitcast.25), calls=%async_computation.2 | async-start | bytes 2097152 | tf_op jit(solution)/shard_map/all_to_all | solution.py:546
  277.8 0.9 copy.21.flat_ref
  278.7 4.2 unpack.5
  282.8 15.2 %all-to-all-done.2 = bf16[128,8,512]{2,1,0:T(8,128)(2,1)S(1)} async-done(((bf16[128,8,512]{2,1,0:T(8,128)(2,1)}), bf16[128,8,512]{2,1,0:T(8,128)(2,1)S(1)}, u32[]{:S(2)}, u32[]{:S(2)}) %all-to-all-start.2) | async-done | bytes 1048608 | tf_op jit(solution)/shard_map/all_to_all | solution.py:546
  298.1 1.0 copy-done.3
  299.0 4.2 unpack.4
  303.2 118.3 %all-reduce.3.cloned.1.call-done = (f32[512,512]{1,0:T(8,128)}, f32[512,512]{1,0:T(8,128)}) async-done(((f32[512,512]{1,0:T(8,128)}, f32[512,512]{1,0:T(8,128)}), (f32[512,512]{1,0:T(8,128)}, f32[512,512]{1,0:T(8,128)})) %all-reduce.3.cloned.1.call-update) | async-done | bytes 2097168 | tf_op jit(solution)/shard_map/psum | solution.py:571
  421.5 3.1 broadcast_multiply_fusion
  (21 shorter events, 0.1 us)
Async XLA Ops:
  12.8 11.5 %copy-start.9 = (s32[1,1,32,8]{2,3,1,0:T(8,128)S(1)}, s32[1,1,32,8]{2,3,1,0:T(8,128)}, u32[]{:S(2)}) copy-start(s32[1,1,32,8]{2,3,1,0:T(8,128)} %param.10) | copy-start | bytes 3076
  12.8 11.7 %copy-start.10 = (s32[512]{0:T(512)S(1)}, s32[512]{0:T(512)}, u32[]{:S(2)}) copy-start(s32[512]{0:T(512)} %param.12) | copy-start | bytes 6148
  12.8 11.8 %copy-start.4 = (bf16[512,512]{1,0:T(8,128)(2,1)S(1)}, bf16[512,512]{1,0:T(8,128)(2,1)}, u32[]{:S(2)}) copy-start(bf16[512,512]{1,0:T(8,128)(2,1)} %param.17) | copy-start | bytes 1572868
  12.8 30.8 %all-to-all-start = ((bf16[128,8,512]{2,1,0:T(8,128)(2,1)}), bf16[128,8,512]{2,1,0:T(8,128)(2,1)S(1)}, u32[]{:S(2)}, u32[]{:S(2)}) async-start(bf16[128,8,512]{2,1,0:T(8,128)(2,1)} %bitcast.23), calls=%async_computation | async-start | bytes 2097152 | tf_op jit(solution)/shard_map/all_to_all | solution.py:546
  25.5 3.7 copy-start.7
  29.6 19.6 %copy-start.6 = (s32[512]{0:T(512)}, s32[512]{0:T(512)S(1)}, u32[]{:S(2)}) copy-start(s32[512]{0:T(512)S(1)} %multiply_add_fusion) | copy-start | bytes 6148
  43.5 1.0 copy-start.1
  44.5 95.1 %all-to-all-start.1 = ((bf16[128,8,640]{2,1,0:T(8,128)(2,1)}), bf16[128,8,640]{2,1,0:T(8,128)(2,1)S(1)}, u32[]{:S(2)}, u32[]{:S(2)}) async-start(bf16[128,8,640]{2,1,0:T(8,128)(2,1)} %bitcast.18), calls=%async_computation.1 | async-start | bytes 2621440 | tf_op jit(solution)/shard_map/all_to_all | solution.py:546
  51.1 88.5 %copy-start.8 = (s32[256]{0:T(256)}, s32[256]{0:T(256)S(1)}, u32[]{:S(2)}) copy-start(s32[256]{0:T(256)S(1)} %get-tuple-element.15.pick_ref) | copy-start | bytes 3076
  139.6 1.1 copy-start
  248.1 25.1 %all-to-all-start.3 = ((bf16[128,8,512]{2,1,0:T(8,128)(2,1)}), bf16[128,8,512]{2,1,0:T(8,128)(2,1)S(1)}, u32[]{:S(2)}, u32[]{:S(2)}) async-start(bf16[128,8,512]{2,1,0:T(8,128)(2,1)} %bitcast.24), calls=%async_computation.3 | async-start | bytes 2097152 | tf_op jit(solution)/shard_map/all_to_all | solution.py:546
  253.9 167.5 %all-reduce.3.cloned.1.call-start = ((), (), s32[]{:S(2)}) async-start(), calls=%async_computation.4 | async-start | bytes 4194304 | tf_op jit(solution)/shard_map/psum | solution.py:571
  258.1 19.7 %copy-start.5 = (s32[512]{0:T(512)S(1)}, s32[512]{0:T(512)}, u32[]{:S(2)}) copy-start(s32[512]{0:T(512)} %multiply_add_fusion.1) | copy-start | bytes 6148
  273.2 5.4 %copy-start.2 = (bf16[128,8,512]{2,1,0:T(8,128)(2,1)}, bf16[128,8,512]{2,1,0:T(8,128)(2,1)S(1)}, u32[]{:S(2)}) copy-start(bf16[128,8,512]{2,1,0:T(8,128)(2,1)S(1)} %all-to-all-done.3) | copy-start | bytes 3145732
  273.2 24.8 %all-to-all-start.2 = ((bf16[128,8,512]{2,1,0:T(8,128)(2,1)}), bf16[128,8,512]{2,1,0:T(8,128)(2,1)S(1)}, u32[]{:S(2)}, u32[]{:S(2)}) async-start(bf16[128,8,512]{2,1,0:T(8,128)(2,1)} %bitcast.25), calls=%async_computation.2 | async-start | bytes 2097152 | tf_op jit(solution)/shard_map/all_to_all | solution.py:546
  298.0 1.0 copy-start.3
Sparse Core Ops, SparseCore 0:
  260.4 161.0 all-reduce.2

commit v3 on v2

--- a/solution.py
+++ b/solution.py
@@ -1,3 +1,4 @@
+import functools
 import math
 
 import jax
@@ -118,6 +119,7 @@
     peers = [
         at_device(1 - xl, y, xh, z, k),
         at_device(xl, y, 1 - xh, z, k),
+        at_device(1 - xl, y, 1 - xh, z, k),
         at_device(xl, y, xh, z, 1 - k),
     ]
     for d in (1, 2, 3):
@@ -292,10 +294,11 @@
     )(cols, x, masks)
 
 
-def backward_kernel(pick_ref, from_ref, keep_ref, last_ref, some_ref, s_ref, mask_hbm, out_ref, mask, chain, *rest):
+def backward_kernel(scale, pick_ref, from_ref, keep_ref, last_ref, some_ref, s_ref, g_ref, mask_hbm, out_ref, sum_ref, mask, chain, *rest):
     held, block, traded, paired, near, cross, crossed, (send, recv) = (
         rest[0:4], rest[4:8], rest[8:12], rest[12:16], rest[16:20], rest[20:24], rest[24:28], rest[28:30]
     )
+    g_core, g_traded, g_half, g_quarter, g_part, g_eighth, g_piece = rest[30:37]
     xl, y, xh, z, k = place()
     copies = Copies(send, recv)
     mask_copy = copies.local(mask_hbm, mask)
@@ -317,7 +320,7 @@
             to = at_device(xl, (y + d) % 4, xh, z, k)
             gathered[c].append(copies.remote(held[c].at[tiles(pair)], held[c].at[tiles(pair)], to))
 
-    def product(c):
+    def product(c, between):
         gathered[c][0].wait()
         for copy in gathered[c][1:]:
             copy.wait_recv()
@@ -330,7 +333,9 @@
                 chain[e] = total.astype(BF16)
             return total
 
-        lax.fori_loop(0, 32, one, jnp.zeros((128, 128), F32))
+        half = lax.fori_loop(0, 16, one, jnp.zeros((128, 128), F32))
+        between()
+        lax.fori_loop(16, 32, one, half)
 
         def settle(p, carry):
             block[c][p] = (chain[last_ref[p]].astype(F32) * some_ref[p]).astype(BF16)
@@ -384,50 +389,161 @@
 
         lax.fori_loop(0, 4, one, 0)
 
+    width = g_ref.shape[1]
+    quarter_at = k * 512 + z * 128
+    part_at = quarter_at + y * 32
+    x_index = xl * 2 + xh
+    piece_at = part_at + x_index * 8
+    x_others = [((xl + a) % 2, (xh + b) % 2) for a, b in ((1, 1), (0, 1), (1, 0))]
+    level = {}
+
+    def blocks(count, size, body):
+        def one(i, carry):
+            body(pl.ds(pl.multiple_of(i * size, size), size), i * size)
+            return carry
+
+        lax.fori_loop(0, count, one, 0)
+
+    def rows_of(base, offset, size):
+        return pl.ds(pl.multiple_of(base + offset, size), size)
+
+    def grad_core():
+        def body(at, offset):
+            g_core[at] = g_ref[rows_of((1 - k) * 512, offset, 64)].astype(BF16)
+
+        blocks(8, 64, body)
+        level["core"] = copies.remote(g_core, g_traded, at_device(xl, y, xh, z, 1 - k))
+
+    def grad_z():
+        level["core"].wait_recv()
+
+        def body(at, offset):
+            g_half[at] = (g_ref[rows_of(k * 512, offset, 64)] + g_traded[at].astype(F32)).astype(BF16)
+
+        blocks(8, 64, body)
+        level["z"] = []
+        for i, d in enumerate(FAR_FIRST):
+            to_z = (z + d) % 4
+            level["z"].append(
+                copies.remote(g_half.at[rows_of(0, to_z * 128, 128)], g_quarter.at[i], at_device(xl, y, xh, to_z, k))
+            )
+
+    def grad_y():
+        for copy in level["z"]:
+            copy.wait_recv()
+
+        def body(at, offset):
+            total = g_ref[rows_of(quarter_at, offset, 32)] + g_traded[rows_of(z * 128, offset, 32)].astype(F32)
+            for i in range(3):
+                total = total + g_quarter[i, at].astype(F32)
+            g_part[0, at] = total
+
+        blocks(4, 32, body)
+        level["y"] = []
+        for i, d in enumerate(FAR_FIRST):
+            to_y = (y + d) % 4
+            level["y"].append(
+                copies.remote(g_part.at[0, rows_of(0, to_y * 32, 32)], g_eighth.at[i], at_device(xl, to_y, xh, z, k))
+            )
+
+    def grad_x():
+        for copy in level["y"]:
+            copy.wait_recv()
+        total = g_part[0, rows_of(0, y * 32, 32)]
+        for i in range(3):
+            total = total + g_eighth[i]
+        g_eighth_sum = g_piece.at[0]
+        g_eighth_sum[...] = total
+        level["x"] = []
+        for i, (a, b) in enumerate(x_others):
+            at = rows_of(0, (a * 2 + b) * 8, 8)
+            level["x"].append(copies.remote(g_eighth_sum.at[at], g_piece.at[1, pl.ds(i * 8, 8)], at_device(a, y, b, z, k)))
+
+    def grad_total():
+        for copy in level["x"]:
+            copy.wait_recv()
+        total = g_piece[0, rows_of(0, x_index * 8, 8)]
+        for i in range(3):
+            total = total + g_piece[1, pl.ds(i * 8, 8)]
+        at = rows_of(piece_at, 0, 8)
+        sum_ref[at] = total * scale
+        level["to_x"] = [copies.remote(sum_ref.at[at], sum_ref.at[at], at_device(a, y, b, z, k)) for a, b in x_others]
+
+    def grad_to_y():
+        for copy in level["to_x"]:
+            copy.wait_recv()
+        at = rows_of(part_at, 0, 32)
+        level["to_y"] = [
+            copies.remote(sum_ref.at[at], sum_ref.at[at], at_device(xl, (y + d) % 4, xh, z, k)) for d in FAR_FIRST
+        ]
+
+    def grad_to_z():
+        for copy in level["to_y"]:
+            copy.wait_recv()
+        at = rows_of(quarter_at, 0, 128)
+        level["to_z"] = [
+            copies.remote(sum_ref.at[at], sum_ref.at[at], at_device(xl, y, xh, (z + d) % 4, k)) for d in FAR_FIRST
+        ]
+
+    def grad_to_core():
+        for copy in level["to_z"]:
+            copy.wait_recv()
+        at = rows_of(k * 512, 0, 512)
+        level["to_core"] = copies.remote(sum_ref.at[at], sum_ref.at[at], at_device(xl, y, xh, z, 1 - k))
+
     own(0)
+    grad_core()
     onward(0)
     own(1)
     onward(1)
+    grad_z()
     own(2)
     mask_copy.wait()
-    product(0)
+    product(0, grad_y)
     onward(2)
     own(3)
     sum_cores(0)
-    product(1)
+    grad_x()
+    product(1, grad_total)
     onward(3)
     sum_cores(1)
+    grad_to_y()
     sum_cols(0)
-    product(2)
+    product(2, grad_to_z)
     sum_cores(2)
     sum_cols(1)
+    grad_to_core()
     sum_cross(0)
-    product(3)
+    product(3, lambda: None)
     sum_cores(3)
     sum_cols(2)
     sum_cross(1)
     sum_cols(3)
     sum_cross(2)
     sum_cross(3)
+    level["to_core"].wait_recv()
     copies.finish()
 
 
-def backward_exchange(tables, s, masks):
+def backward_exchange(tables, s, grads, masks, scale):
     return pl.pallas_call(
-        backward_kernel,
-        in_specs=[SMEM_SPEC] * 5 + [VMEM_SPEC, ANY_SPEC],
-        out_specs=VMEM_SPEC,
-        out_shape=jax.ShapeDtypeStruct(s.shape, F32),
+        functools.partial(backward_kernel, scale),
+        in_specs=[SMEM_SPEC] * 5 + [VMEM_SPEC, VMEM_SPEC, ANY_SPEC],
+        out_specs=[VMEM_SPEC, VMEM_SPEC],
+        out_shape=[jax.ShapeDtypeStruct(s.shape, F32), jax.ShapeDtypeStruct(grads.shape, F32)],
         scratch_shapes=[tile_buffer(256), tile_buffer(256)]
         + [tile_buffer(32)] * 4
         + [tile_buffer(64)] * 4
         + [tile_buffer(32)] * 8
         + [tile_buffer(24)] * 4
         + [tile_buffer(4)] * 8
-        + [pltpu.SemaphoreType.DMA((64,)), pltpu.SemaphoreType.DMA((64,))],
+        + [pltpu.SemaphoreType.DMA((96,)), pltpu.SemaphoreType.DMA((96,))]
+        + [pltpu.VMEM((512, 512), BF16)] * 3
+        + [pltpu.VMEM((3, 128, 512), BF16), pltpu.VMEM((1, 128, 512), F32)]
+        + [pltpu.VMEM((3, 32, 512), F32), pltpu.VMEM((2, 32, 512), F32)],
         compiler_params=remote_params(1),
         name="backward_exchange",
-    )(*tables, s, masks)
+    )(*tables, s, grads, masks)
 
 
 def column_order(columns):
@@ -453,7 +569,7 @@
 
 
 def dense_kernel(
-    sum_ref, x_ref, extra_ref, ws_ref, wn_ref, hidden_ref, own_ref, spread_ref, gs_ref, gn_ref
+    sum_ref, x_ref, extra_ref, ws_ref, wn_ref, hidden_ref, own_ref, spread_ref, grads_ref
 ):
     step = pl.program_id(0)
     width = hidden_ref.shape[1]
@@ -473,13 +589,13 @@
 
     @pl.when(step == 0)
     def _():
-        gs_ref[...] = gs
-        gn_ref[...] = gn
+        grads_ref[pl.ds(0, width)] = gs
+        grads_ref[pl.ds(width, width)] = gn
 
     @pl.when(step > 0)
     def _():
-        gs_ref[...] += gs
-        gn_ref[...] += gn
+        grads_ref[pl.ds(0, width)] += gs
+        grads_ref[pl.ds(width, width)] += gn
 
     own_ref[...] = lax.dot_general(slopes, ws_ref[...], COL_T, preferred_element_type=F32)
     spread = lax.dot_general(slopes, wn_ref[...], COL_T, preferred_element_type=F32) / degrees
@@ -507,15 +623,13 @@
             pl.BlockSpec((step, width), rowwise),
             pl.BlockSpec((step, width), rowwise),
             tiled,
-            pl.BlockSpec((width, width), whole),
-            pl.BlockSpec((width, width), whole),
+            pl.BlockSpec((2 * width, width), whole),
         ],
         out_shape=[
             jax.ShapeDtypeStruct((rows, width), BF16),
             jax.ShapeDtypeStruct((rows, width), F32),
             jax.ShapeDtypeStruct(x.shape, BF16),
-            jax.ShapeDtypeStruct((width, width), F32),
-            jax.ShapeDtypeStruct((width, width), F32),
+            jax.ShapeDtypeStruct((2 * width, width), F32),
         ],
         compiler_params=params(),
         name="dense",
@@ -567,14 +681,13 @@
     extra = jnp.concatenate([cotangent, degree_cols], axis=1)
     node_extra = unpack(node_flat, swap_all(pack(own_flat, extra, slots), both))
     summed = forward_exchange(cols, node_x, masks)
-    hidden, own_back, spread, grad_self, grad_neigh = dense(summed, node_x, node_extra, self_weight, neigh_weight)
-    sums = lax.psum((grad_self, grad_neigh), both)
-    back = backward_exchange(tables, spread, masks)
+    hidden, own_back, spread, grads = dense(summed, node_x, node_extra, self_weight, neigh_weight)
+    grad_scale = 1.0 / math.sqrt(rows * devices)
+    back, sums = backward_exchange(tables, spread, grads, masks, grad_scale)
     grad_node = join(own_back, back)
     hidden_out = unpack(own_flat, swap_all(pack(node_flat, hidden, slots), both))
     grad_out = unpack(own_flat, swap_all(pack(node_flat, grad_node, slots), both))
-    grad_scale = 1.0 / math.sqrt(rows * devices)
-    return hidden_out, grad_out, sums[0] * grad_scale, sums[1] * grad_scale
+    return hidden_out, grad_out, sums[:width], sums[width:]
 
 
 def solution(mesh):

time: 433 us -> 318 us (0.73)
  waiting for transfers between devices: 163 us -> 41 us
  Pallas kernels: 212 us -> 231 us
  between operations: 14.2 us -> 0.81 us
    psum x1 -> x0, waiting for transfers between devices: 118 us -> none  [on_device(): sums = lax.psum((grad_self, grad_neigh), both)]
    pallas_call x1, Pallas kernels: 86.9 us -> 105 us  [backward_exchange(): pl.pallas_call(functools.partial(backward_kernel, scale), in_specs=[SMEM_...]
  transfers between devices with their start and end apart: 5 -> 4, of which waited for: 4 -> 3; matrix products, arithmetic and copies ran while one was open for 2% -> 3% of each run, Pallas kernels for 24% -> 31%
where the time goes in v3:
time: 318 us; the launch traced here: 317 us
  Pallas kernels  231 us (73%)
  waiting for transfers between devices  41 us (13%)
  starting transfers between devices  29.2 us (9%)
  local copies, waits for them, and re-layouts  8.05 us (3%)
  other arithmetic  6.96 us (2%)
    pallas_call x1, Pallas kernels, backward_exchange(): pl.pallas_call(functools.partial(backward_kernel, scale), in_specs=[SMEM_...  105 us
    pallas_call x1, Pallas kernels, forward_exchange(): pl.pallas_call(forward_kernel, in_specs=[SMEM_SPEC, VMEM_SPEC, ANY_SPEC],...  82 us
    all_to_all x4, waiting for transfers between devices, swap_all(): return lax.all_to_all(data, axes, split_axis=0, concat_axis=0, tiled=True)  41 us
    all_to_all x4, starting transfers between devices, swap_all(): return lax.all_to_all(data, axes, split_axis=0, concat_axis=0, tiled=True)  29.2 us
    pallas_call x4, Pallas kernels, pack(): pl.pallas_call(pack_kernel, grid=(parts,), in_specs=[pl.BlockSpec((1, row...  13.9 us
    pallas_call x3, Pallas kernels, unpack(): pl.pallas_call(unpack_kernel, grid=(parts,), in_specs=[pl.BlockSpec((rows...  12.7 us
    pallas_call x1, Pallas kernels, dense(): pl.pallas_call(dense_kernel, grid=(rows // step,), in_specs=[tiled, tiled...  9.14 us
  transfers between devices with their start and end apart: 4, of which 3 were waited for; matrix products, arithmetic and copies ran while one was open for 3% of the time, Pallas kernels for 31%

profile of v3, /device:TPU:1, one launch (start us, length us, event | category | flops | bytes accessed | tf_op | source)
XLA Modules:
  0.0 316.9 jit_solution(3104271215480586931)
XLA Ops:
  0.6 0.7 add_select_fusion.1
  1.3 0.3 convert_reduce_fusion.1
  1.6 1.3 multiply_add_fusion.1
  2.8 3.4 %pack.4 = bf16[1024,512]{1,0:T(8,128)(2,1)} custom-call(s32[1,512]{1,0:T(1,128)} %bitcast.26, bf16[512,512]{1,0:T(8,128)(2,1)} %data_ref.1), custom_call_target="tpu_custom_call" | custom-call | tf_op jit(solution)/shard_map/pack/pallas_call | solution.py:40
  6.2 11.5 %all-to-all-start = ((bf16[128,8,512]{2,1,0:T(8,128)(2,1)}), bf16[128,8,512]{2,1,0:T(8,128)(2,1)S(1)}, u32[]{:S(2)}, u32[]{:S(2)}) async-start(bf16[128,8,512]{2,1,0:T(8,128)(2,1)} %bitcast.23), calls=%async_computation | async-start | bytes 2097152 | tf_op jit(solution)/shard_map/all_to_all | solution.py:660
  17.7 0.1 copy.18
  17.8 0.1 reshape_squeeze.3
  17.9 0.1 broadcast_in_dim.16
  18.1 0.9 pad_maximum_fusion.data_ref
  19.0 3.7 %pack.5 = bf16[1024,640]{1,0:T(8,128)(2,1)} custom-call(s32[1,512]{1,0:T(1,128)} %bitcast.27, bf16[512,640]{1,0:T(8,128)(2,1)} %pad_maximum_fusion.data_ref), custom_call_target="tpu_custom_call" | custom-call | tf_op jit(solution)/shard_map/pack/pallas_call | solution.py:40
  22.7 0.0 copy-done.7
  22.7 0.3 convert_reduce_fusion
  23.1 0.0 copy-start.6
  23.1 13.9 %all-to-all-done = bf16[128,8,512]{2,1,0:T(8,128)(2,1)S(1)} async-done(((bf16[128,8,512]{2,1,0:T(8,128)(2,1)}), bf16[128,8,512]{2,1,0:T(8,128)(2,1)S(1)}, u32[]{:S(2)}, u32[]{:S(2)}) %all-to-all-start) | async-done | bytes 1048608 | tf_op jit(solution)/shard_map/all_to_all | solution.py:660
  37.0 1.0 copy-done.1
  38.0 4.6 %all-to-all-start.1 = ((bf16[128,8,640]{2,1,0:T(8,128)(2,1)}), bf16[128,8,640]{2,1,0:T(8,128)(2,1)S(1)}, u32[]{:S(2)}, u32[]{:S(2)}) async-start(bf16[128,8,640]{2,1,0:T(8,128)(2,1)} %bitcast.18), calls=%async_computation.1 | async-start | bytes 2621440 | tf_op jit(solution)/shard_map/all_to_all | solution.py:660
  42.5 0.1 fusion.1
  42.6 0.0 copy-done.6
  42.6 0.9 copy.19.flat_ref
  43.5 0.5 convert_element_type.27.some_ref
  44.0 0.1 convert_reduce_fusion.3
  44.1 0.2 convert_reduce_fusion.2
  44.3 0.2 select_reduce_fusion
  44.5 0.0 copy-start.8
  44.5 0.5 add_maximum_fusion.last_ref
  45.0 0.6 and_select_fusion.from_ref
  45.6 0.7 compare_convert_fusion.keep_ref
  46.3 0.6 multiply_add_fusion.3.cols_ref
  46.9 4.2 %unpack_tiles.1.x_ref = bf16[4,4,128,128]{3,2,1,0:T(8,128)(2,1)} custom-call(s32[512,1]{1,0:T(8,128)} %copy.19.flat_ref, bf16[1024,512]{1,0:T(8,128)(2,1)} %bitcast.20), custom_call_target="tpu_custom_call" | custom-call | tf_op jit(solution)/shard_map/unpack_tiles/pallas_call | solution.py:89
  51.0 82.0 %forward_exchange.1.sum_ref = f32[4,4,128,128]{3,2,1,0:T(8,128)} custom-call(s32[256]{0:T(256)} %multiply_add_fusion.3.cols_ref, bf16[4,4,128,128]{3,2,1,0:T(8,128)(2,1)} %unpack_tiles.1.x_ref, bf16[256,128,128]{2,1,0:T(8,128)(2,1)} %bitcast.16), custom_call_target="tpu_custom_call" | custom-call | tf_op jit(solution)/shard_map/forward_exchange/pallas_call | solution.py:281
  133.0 0.0 all-to-all-done.1
  133.1 0.0 copy-start
  133.1 1.0 copy-done
  134.1 4.4 %unpack.3.extra_ref = bf16[512,640]{1,0:T(8,128)(2,1)} custom-call(s32[512,1]{1,0:T(8,128)} %copy.19.flat_ref, bf16[1024,640]{1,0:T(8,128)(2,1)} %bitcast.19), custom_call_target="tpu_custom_call" | custom-call | tf_op jit(solution)/shard_map/unpack/pallas_call | solution.py:64
  138.5 9.1 %dense.1 = (bf16[512,512]{1,0:T(8,128)(2,1)}, f32[512,512]{1,0:T(8,128)}, bf16[4,4,128,128]{3,2,1,0:T(8,128)(2,1)}, f32[1024,512]{1,0:T(8,128)}) custom-call(f32[4,4,128,128]{3,2,1,0:T(8,128)} %forward_exchange.1.sum_ref, bf16[4,4,128,128]{3,2,1,0:T(8,128)(2,1)} %unpack_tiles.1.x_ref, bf16[512,640]{1,0:T(8,128)(2,1)} %unpack.3.extra_ref, ...), custom_call_target="tpu_custom_call" | custom-call | tf_op jit(solution)/shard_map/dense/pallas_call | solution.py:612
  147.6 105.3 %backward_exchange.1 = (f32[4,4,128,128]{3,2,1,0:T(8,128)}, f32[1024,512]{1,0:T(8,128)}) custom-call(s32[256]{0:T(256)} %copy-done.8, s32[256]{0:T(256)} %and_select_fusion.from_ref, f32[256]{0:T(256)} %compare_convert_fusion.keep_ref, s32[64]{0:T(128)} %add_maximum_fusion.last_ref, f32[64]{0:T(128)} %convert_element_type.27.some_ref, ...), custom_call_target="tpu_custom_call" | custom-call | tf_op jit(solution)/shard_map/backward_exchange/pallas_call | solution.py:529
  253.0 3.7 %join.1.data_ref = bf16[512,512]{1,0:T(8,128)(2,1)} custom-call(f32[512,512]{1,0:T(8,128)} %get-tuple-element.11.own_ref, f32[4,4,128,128]{3,2,1,0:T(8,128)} %get-tuple-element.14.back_ref), custom_call_target="tpu_custom_call" | custom-call | tf_op jit(solution)/shard_map/join/pallas_call | solution.py:646
  256.7 3.4 %pack.7 = bf16[1024,512]{1,0:T(8,128)(2,1)} custom-call(s32[1,512]{1,0:T(1,128)} %bitcast.30, bf16[512,512]{1,0:T(8,128)(2,1)} %join.1.data_ref), custom_call_target="tpu_custom_call" | custom-call | tf_op jit(solution)/shard_map/pack/pallas_call | solution.py:40
  260.0 8.6 %all-to-all-start.3 = ((bf16[128,8,512]{2,1,0:T(8,128)(2,1)}), bf16[128,8,512]{2,1,0:T(8,128)(2,1)S(1)}, u32[]{:S(2)}, u32[]{:S(2)}) async-start(bf16[128,8,512]{2,1,0:T(8,128)(2,1)} %bitcast.25), calls=%async_computation.3 | async-start | bytes 2097152 | tf_op jit(solution)/shard_map/all_to_all | solution.py:660
  268.6 3.4 %pack.6 = bf16[1024,512]{1,0:T(8,128)(2,1)} custom-call(s32[1,512]{1,0:T(1,128)} %bitcast.31, bf16[512,512]{1,0:T(8,128)(2,1)} %get-tuple-element.10.data_ref), custom_call_target="tpu_custom_call" | custom-call | tf_op jit(solution)/shard_map/pack/pallas_call | solution.py:40
  272.0 15.8 %all-to-all-done.3 = bf16[128,8,512]{2,1,0:T(8,128)(2,1)S(1)} async-done(((bf16[128,8,512]{2,1,0:T(8,128)(2,1)}), bf16[128,8,512]{2,1,0:T(8,128)(2,1)S(1)}, u32[]{:S(2)}, u32[]{:S(2)}) %all-to-all-start.3) | async-done | bytes 1048608 | tf_op jit(solution)/shard_map/all_to_all | solution.py:660
  287.9 4.6 %all-to-all-start.2 = ((bf16[128,8,512]{2,1,0:T(8,128)(2,1)}), bf16[128,8,512]{2,1,0:T(8,128)(2,1)S(1)}, u32[]{:S(2)}, u32[]{:S(2)}) async-start(bf16[128,8,512]{2,1,0:T(8,128)(2,1)} %bitcast.24), calls=%async_computation.2 | async-start | bytes 2097152 | tf_op jit(solution)/shard_map/all_to_all | solution.py:660
  292.5 0.9 copy.21.flat_ref
  293.3 3.0 fusion.8
  296.3 4.2 %unpack.5 = bf16[512,512]{1,0:T(8,128)(2,1)} custom-call(s32[512,1]{1,0:T(8,128)} %copy.21.flat_ref, bf16[1024,512]{1,0:T(8,128)(2,1)} %bitcast.21), custom_call_target="tpu_custom_call" | custom-call | tf_op jit(solution)/shard_map/unpack/pallas_call | solution.py:64
  300.5 11.2 %all-to-all-done.2 = bf16[128,8,512]{2,1,0:T(8,128)(2,1)S(1)} async-done(((bf16[128,8,512]{2,1,0:T(8,128)(2,1)}), bf16[128,8,512]{2,1,0:T(8,128)(2,1)S(1)}, u32[]{:S(2)}, u32[]{:S(2)}) %all-to-all-start.2) | async-done | bytes 1048608 | tf_op jit(solution)/shard_map/all_to_all | solution.py:660
  311.7 1.0 copy-done.3
  312.7 4.2 %unpack.4 = bf16[512,512]{1,0:T(8,128)(2,1)} custom-call(s32[512,1]{1,0:T(8,128)} %copy.21.flat_ref, bf16[1024,512]{1,0:T(8,128)(2,1)} %bitcast.22), custom_call_target="tpu_custom_call" | custom-call | tf_op jit(solution)/shard_map/unpack/pallas_call | solution.py:64
  (18 shorter events, 0.1 us)
Async XLA Ops:
  6.2 11.5 %copy-start.9 = (s32[1,1,32,8]{2,3,1,0:T(8,128)S(1)}, s32[1,1,32,8]{2,3,1,0:T(8,128)}, u32[]{:S(2)}) copy-start(s32[1,1,32,8]{2,3,1,0:T(8,128)} %param.10) | copy-start | bytes 3076
  6.2 11.7 %copy-start.10 = (s32[512]{0:T(512)S(1)}, s32[512]{0:T(512)}, u32[]{:S(2)}) copy-start(s32[512]{0:T(512)} %param.12) | copy-start | bytes 6148
  6.2 11.8 %copy-start.4 = (bf16[512,512]{1,0:T(8,128)(2,1)S(1)}, bf16[512,512]{1,0:T(8,128)(2,1)}, u32[]{:S(2)}) copy-start(bf16[512,512]{1,0:T(8,128)(2,1)} %param.17) | copy-start | bytes 1572868
  6.2 30.8 %all-to-all-start = ((bf16[128,8,512]{2,1,0:T(8,128)(2,1)}), bf16[128,8,512]{2,1,0:T(8,128)(2,1)S(1)}, u32[]{:S(2)}, u32[]{:S(2)}) async-start(bf16[128,8,512]{2,1,0:T(8,128)(2,1)} %bitcast.23), calls=%async_computation | async-start | bytes 2097152 | tf_op jit(solution)/shard_map/all_to_all | solution.py:660
  19.0 3.7 %copy-start.7 = (s32[512]{0:T(512)S(1)}, s32[512]{0:T(512)}, u32[]{:S(2)}) copy-start(s32[512]{0:T(512)} %param.14) | copy-start | bytes 6148
  23.1 19.6 %copy-start.6 = (s32[512]{0:T(512)}, s32[512]{0:T(512)S(1)}, u32[]{:S(2)}) copy-start(s32[512]{0:T(512)S(1)} %multiply_add_fusion) | copy-start | bytes 6148
  37.0 1.0 copy-start.1
  38.0 95.1 %all-to-all-start.1 = ((bf16[128,8,640]{2,1,0:T(8,128)(2,1)}), bf16[128,8,640]{2,1,0:T(8,128)(2,1)S(1)}, u32[]{:S(2)}, u32[]{:S(2)}) async-start(bf16[128,8,640]{2,1,0:T(8,128)(2,1)} %bitcast.18), calls=%async_computation.1 | async-start | bytes 2621440 | tf_op jit(solution)/shard_map/all_to_all | solution.py:660
  44.5 88.5 %copy-start.8 = (s32[256]{0:T(256)}, s32[256]{0:T(256)S(1)}, u32[]{:S(2)}) copy-start(s32[256]{0:T(256)S(1)} %get-tuple-element.17.pick_ref) | copy-start | bytes 3076
  133.1 1.1 copy-start
  260.0 27.9 %all-to-all-start.3 = ((bf16[128,8,512]{2,1,0:T(8,128)(2,1)}), bf16[128,8,512]{2,1,0:T(8,128)(2,1)S(1)}, u32[]{:S(2)}, u32[]{:S(2)}) async-start(bf16[128,8,512]{2,1,0:T(8,128)(2,1)} %bitcast.25), calls=%async_computation.3 | async-start | bytes 2097152 | tf_op jit(solution)/shard_map/all_to_all | solution.py:660
  272.0 20.4 %copy-start.5 = (s32[512]{0:T(512)S(1)}, s32[512]{0:T(512)}, u32[]{:S(2)}) copy-start(s32[512]{0:T(512)} %multiply_add_fusion.1) | copy-start | bytes 6148
  287.9 8.5 %copy-start.2 = (bf16[128,8,512]{2,1,0:T(8,128)(2,1)}, bf16[128,8,512]{2,1,0:T(8,128)(2,1)S(1)}, u32[]{:S(2)}) copy-start(bf16[128,8,512]{2,1,0:T(8,128)(2,1)S(1)} %all-to-all-done.3) | copy-start | bytes 3145732
  287.9 23.8 %all-to-all-start.2 = ((bf16[128,8,512]{2,1,0:T(8,128)(2,1)}), bf16[128,8,512]{2,1,0:T(8,128)(2,1)S(1)}, u32[]{:S(2)}, u32[]{:S(2)}) async-start(bf16[128,8,512]{2,1,0:T(8,128)(2,1)} %bitcast.24), calls=%async_computation.2 | async-start | bytes 2097152 | tf_op jit(solution)/shard_map/all_to_all | solution.py:660
  311.7 1.0 copy-start.3

commit v4 on v3

--- a/solution.py
+++ b/solution.py
@@ -9,6 +9,7 @@
 from jax.sharding import PartitionSpec as P
 
 F32 = jnp.float32
+DEVICES = 128
 BF16 = jnp.bfloat16
 MESH = pl.DeviceIdType.MESH
 VMEM_LIMIT = 60 * 1024 * 1024
@@ -26,78 +27,6 @@
     return pltpu.CompilerParams(vmem_limit_bytes=VMEM_LIMIT, **kw)
 
 
-def pack_kernel(flat_ref, data_ref, out_ref):
-    step = pl.program_id(0)
-    size = out_ref.shape[0]
-    slot = lax.broadcasted_iota(jnp.int32, (size, flat_ref.shape[1]), 0) + step * size
-    pick = jnp.where(slot == flat_ref[...], 1.0, 0.0).astype(BF16)
-    out_ref[...] = jnp.dot(pick, data_ref[...], preferred_element_type=F32).astype(BF16)
-
-
-def pack(flat, data, slots):
-    rows, width = data.shape
-    parts = 4
-    return pl.pallas_call(
-        pack_kernel,
-        grid=(parts,),
-        in_specs=[
-            pl.BlockSpec((1, rows), lambda i: (0, 0)),
-            pl.BlockSpec((rows, width), lambda i: (0, 0)),
-        ],
-        out_specs=pl.BlockSpec((slots // parts, width), lambda i: (i, 0)),
-        out_shape=jax.ShapeDtypeStruct((slots, width), BF16),
-        name="pack",
-    )(flat.reshape(1, rows), data)
-
-
-def unpack_kernel(flat_ref, data_ref, out_ref):
-    size = out_ref.shape[0]
-    slot = lax.broadcasted_iota(jnp.int32, (size, data_ref.shape[0]), 1)
-    pick = jnp.where(slot == flat_ref[...], 1.0, 0.0).astype(BF16)
-    out_ref[...] = jnp.dot(pick, data_ref[...], preferred_element_type=F32).astype(BF16)
-
-
-def unpack(flat, data):
-    slots, width = data.shape
-    rows = flat.shape[0]
-    parts = 4
-    return pl.pallas_call(
-        unpack_kernel,
-        grid=(parts,),
-        in_specs=[
-            pl.BlockSpec((rows // parts, 1), lambda i: (i, 0)),
-            pl.BlockSpec((slots, width), lambda i: (0, 0)),
-        ],
-        out_specs=pl.BlockSpec((rows // parts, width), lambda i: (i, 0)),
-        out_shape=jax.ShapeDtypeStruct((rows, width), BF16),
-        name="unpack",
-    )(flat.reshape(rows, 1), data)
-
-
-def unpack_tiles_kernel(flat_ref, data_ref, out_ref):
-    size = out_ref.shape[2]
-    slot = lax.broadcasted_iota(jnp.int32, (size, data_ref.shape[0]), 1)
-    pick = jnp.where(slot == flat_ref[...], 1.0, 0.0).astype(BF16)
-    rows = jnp.dot(pick, data_ref[...], preferred_element_type=F32).astype(BF16)
-    for c in range(4):
-        out_ref[c, 0] = rows[:, c * 128 : (c + 1) * 128]
-
-
-def unpack_tiles(flat, data):
-    slots, width = data.shape
-    rows = flat.shape[0]
-    return pl.pallas_call(
-        unpack_tiles_kernel,
-        grid=(4,),
-        in_specs=[
-            pl.BlockSpec((rows // 4, 1), lambda i: (i, 0)),
-            pl.BlockSpec((slots, width), lambda i: (0, 0)),
-        ],
-        out_specs=pl.BlockSpec((4, 1, 128, 128), lambda i: (0, i, 0, 0)),
-        out_shape=jax.ShapeDtypeStruct((4, 4, 128, 128), BF16),
-        name="unpack_tiles",
-    )(flat.reshape(rows, 1), data)
-
 def place():
     r, c = lax.axis_index("row"), lax.axis_index("col")
     return r // 4, r % 4, c // 8, (c // 2) % 4, c % 2
@@ -107,25 +36,108 @@
     return (xl * 4 + y, xh * 8 + z * 2 + k)
 
 
-def meet(peers):
-    barrier = pltpu.get_barrier_semaphore()
-    for peer in peers:
-        pl.semaphore_signal(barrier, inc=1, device_id=peer, device_id_type=MESH)
-    pl.semaphore_wait(barrier, len(peers))
-
-
-def all_peers():
-    xl, y, xh, z, k = place()
-    peers = [
-        at_device(1 - xl, y, xh, z, k),
-        at_device(xl, y, 1 - xh, z, k),
-        at_device(1 - xl, y, 1 - xh, z, k),
-        at_device(xl, y, xh, z, 1 - k),
-    ]
-    for d in (1, 2, 3):
-        peers.append(at_device(xl, (y + d) % 4, xh, z, k))
-        peers.append(at_device(xl, y, xh, (z + d) % 4, k))
-    return peers
+def device_number():
+    return lax.axis_index("row") * 16 + lax.axis_index("col")
+
+
+def greet():
+    barrier, me = pltpu.get_barrier_semaphore(), device_number()
+
+    def one(step, carry):
+        peer = (me + step) % DEVICES
+        pl.semaphore_signal(barrier, inc=1, device_id=(peer // 16, peer % 16), device_id_type=MESH)
+        return carry
+
+    lax.fori_loop(1, DEVICES, one, 0)
+
+
+def meet():
+    pl.semaphore_wait(pltpu.get_barrier_semaphore(), DEVICES - 1)
+
+
+class Relay:
+    def __init__(self, outbox, inbox, sems):
+        self.outbox, self.inbox, self.sems = outbox, inbox, sems
+        self.width = outbox.shape[2]
+
+    def pack(self, spread_out, data, first):
+        def one(i, carry):
+            rows = jnp.dot(
+                spread_out[pl.ds(pl.multiple_of(i * 128, 128), 128)],
+                data[:, pl.ds(first, self.width)],
+                preferred_element_type=F32,
+            )
+            self.outbox[pl.ds(i * 16, 16)] = rows.reshape(16, 8, self.width).astype(BF16)
+            return carry
+
+        lax.fori_loop(0, 8, one, 0)
+
+    def whole(self):
+        slots = pl.ds(0, DEVICES - 1)
+        peer = (device_number() + 1) % DEVICES
+        return pltpu.make_async_remote_copy(
+            src_ref=self.outbox.at[slots], dst_ref=self.inbox.at[slots], send_sem=self.sems.at[0],
+            recv_sem=self.sems.at[1], device_id=(peer // 16, peer % 16), device_id_type=MESH,
+        )
+
+    def kept(self):
+        me = device_number()
+        return pltpu.make_async_copy(self.outbox.at[me], self.inbox.at[me], self.sems.at[2])
+
+    def start(self):
+        me = device_number()
+        self.kept().start()
+
+        def one(step, carry):
+            peer = (me + step) % DEVICES
+            pltpu.make_async_remote_copy(
+                src_ref=self.outbox.at[peer], dst_ref=self.inbox.at[me], send_sem=self.sems.at[0],
+                recv_sem=self.sems.at[1], device_id=(peer // 16, peer % 16), device_id_type=MESH,
+            ).start()
+            return carry
+
+        lax.fori_loop(1, DEVICES, one, 0)
+
+    def collect(self, flat):
+        self.kept().wait()
+        self.whole().wait_recv()
+
+        def one(i, carry):
+            rows = self.inbox[pl.ds(i * 16, 16)].astype(F32).reshape(128, self.width)
+            flat[pl.ds(pl.multiple_of(i * 128, 128), 128), pl.ds(0, self.width)] = rows.astype(BF16)
+            return carry
+
+        lax.fori_loop(0, 8, one, 0)
+
+    def finish(self):
+        self.whole().wait_send()
+
+
+def pick_rows(table, flat_row):
+    def one(i, carry):
+        slot = lax.broadcasted_iota(jnp.int32, (128, table.shape[1]), 0) + i * 128
+        table[pl.ds(pl.multiple_of(i * 128, 128), 128)] = jnp.where(slot == flat_row[...], 1.0, 0.0).astype(BF16)
+        return carry
+
+    lax.fori_loop(0, table.shape[0] // 128, one, 0)
+
+
+def pick_slots(table, flat_col):
+    def one(i, carry):
+        at = pl.ds(pl.multiple_of(i * 128, 128), 128)
+        slot = lax.broadcasted_iota(jnp.int32, (128, table.shape[1]), 1)
+        table[at] = jnp.where(slot == flat_col[at], 1.0, 0.0).astype(BF16)
+        return carry
+
+    lax.fori_loop(0, table.shape[0] // 128, one, 0)
+
+
+def each_block(count, body):
+    def one(i, carry):
+        body(i, pl.ds(pl.multiple_of(i * 128, 128), 128))
+        return carry
+
+    lax.fori_loop(0, count, one, 0)
 
 
 class Copies:
@@ -156,14 +168,46 @@
 FAR_FIRST = (2, 1, 3)
 
 
-def forward_kernel(cols_ref, x_ref, mask_hbm, out_ref, mask, *rest):
+def forward_kernel(
+    cols_ref, own_row, node_col, features, extra, mask_hbm, out_ref, x_ref, node_extra, mask, *rest
+):
     held, part, near, cross, crossed, (send, recv) = (
         rest[0:4], rest[4:8], rest[8:12], rest[12:16], rest[16:20], rest[20:22]
     )
     xl, y, xh, z, k = place()
     copies = Copies(send, recv)
     mask_copy = copies.local(mask_hbm, mask)
-    meet(all_peers())
+    packing, unpacking, flat, flat_extra = rest[22:26]
+    relays = [Relay(rest[26], rest[27], rest[28]), Relay(rest[29], rest[30], rest[31])]
+    extra_relay = Relay(rest[32], rest[33], rest[34])
+    greet()
+    pick_rows(packing, own_row)
+    relays[0].pack(packing, features, 0)
+    meet()
+    relays[0].start()
+    relays[1].pack(packing, features, 256)
+    relays[1].start()
+    pick_slots(unpacking, node_col)
+    extra_relay.pack(packing, extra, 0)
+
+    def unpack(c):
+        if c % 2 == 0:
+            relays[c // 2].collect(flat)
+
+        def one(i, at):
+            rows = jnp.dot(unpacking[at], flat[:, pl.ds(c % 2 * 128, 128)], preferred_element_type=F32)
+            x_ref[c, i] = rows.astype(BF16)
+
+        each_block(4, one)
+
+    def unpack_extra():
+        extra_relay.collect(flat_extra)
+
+        def one(i, at):
+            node_extra[at] = jnp.dot(unpacking[at], flat_extra[...], preferred_element_type=F32).astype(BF16)
+
+        each_block(4, one)
+
     tiles = lambda slot: pl.ds(slot * 4, 4)
     mine, pair = k * 8 + xh * 4 + z, k * 8 + (1 - xh) * 4 + z
     gathered, over, swap, row_copies, cross_copy = [[] for _ in range(4)], {}, {}, {}, {}
@@ -236,12 +280,16 @@
 
         lax.fori_loop(0, 4, one, 0)
 
+    unpack(0)
     own(0)
+    unpack(1)
     onward(0)
     own(1)
+    unpack(2)
     onward(1)
     swap_cores(0)
     own(2)
+    unpack(3)
     mask_copy.wait()
     product(0)
     onward(2)
@@ -250,6 +298,7 @@
     product(1)
     onward(3)
     swap_cores(2)
+    extra_relay.start()
     sum_rows(0)
     product(2)
     swap_cores(3)
@@ -258,10 +307,13 @@
     product(3)
     sum_rows(2)
     sum_cross(1)
+    unpack_extra()
     sum_rows(3)
     sum_cross(2)
     sum_cross(3)
     copies.finish()
+    for relay in relays + [extra_relay]:
+        relay.finish()
 
 
 def remote_params(ident):
@@ -277,32 +329,61 @@
     return pltpu.VMEM((count, 128, 128), BF16)
 
 
-def forward_exchange(cols, x, masks):
+def boxes(width):
+    return [
+        pltpu.VMEM((DEVICES, 8, width), BF16),
+        pltpu.VMEM((DEVICES, 8, width), BF16),
+        pltpu.SemaphoreType.DMA((3,)),
+    ]
+
+
+def forward_exchange(cols, own_row, node_col, features, extra, masks):
+    rows, width = features.shape
+    slots, wide = DEVICES * 8, extra.shape[1]
+    tiled = (4, 4, 128, 128)
     return pl.pallas_call(
         forward_kernel,
-        in_specs=[SMEM_SPEC, VMEM_SPEC, ANY_SPEC],
-        out_specs=VMEM_SPEC,
-        out_shape=jax.ShapeDtypeStruct(x.shape, F32),
+        in_specs=[SMEM_SPEC] + [VMEM_SPEC] * 4 + [ANY_SPEC],
+        out_specs=[VMEM_SPEC] * 3,
+        out_shape=[
+            jax.ShapeDtypeStruct(tiled, F32),
+            jax.ShapeDtypeStruct(tiled, BF16),
+            jax.ShapeDtypeStruct((rows, wide), BF16),
+        ],
         scratch_shapes=[tile_buffer(256)]
         + [tile_buffer(64)] * 4
         + [tile_buffer(32)] * 4
         + [tile_buffer(24)] * 4
         + [tile_buffer(4)] * 8
-        + [pltpu.SemaphoreType.DMA((64,)), pltpu.SemaphoreType.DMA((64,))],
+        + [pltpu.SemaphoreType.DMA((64,)), pltpu.SemaphoreType.DMA((64,))]
+        + [pltpu.VMEM((slots, rows), BF16), pltpu.VMEM((rows, slots), BF16)]
+        + [pltpu.VMEM((slots, width // 2), BF16), pltpu.VMEM((slots, wide), BF16)]
+        + boxes(width // 2) * 2
+        + boxes(wide),
         compiler_params=remote_params(0),
         name="forward_exchange",
-    )(cols, x, masks)
-
-
-def backward_kernel(scale, pick_ref, from_ref, keep_ref, last_ref, some_ref, s_ref, g_ref, mask_hbm, out_ref, sum_ref, mask, chain, *rest):
-    held, block, traded, paired, near, cross, crossed, (send, recv) = (
-        rest[0:4], rest[4:8], rest[8:12], rest[12:16], rest[16:20], rest[20:24], rest[24:28], rest[28:30]
+    )(cols, own_row, node_col, features, extra, masks)
+
+
+def backward_kernel(
+    scale, pick_ref, from_ref, keep_ref, last_ref, some_ref, node_row, own_col, hidden, own_back, s_ref, g_ref, mask_hbm,
+    hidden_out, grad_out, sum_ref, mask, chain, *rest
+):
+    held, block, traded, near, cross, crossed, (send, recv) = (
+        rest[0:4], rest[4:8], rest[8:12], rest[12:16], rest[16:20], rest[20:24], rest[24:26]
     )
-    g_core, g_traded, g_half, g_quarter, g_part, g_eighth, g_piece = rest[30:37]
+    g_core, g_traded, g_half, g_quarter, g_part, g_eighth, g_piece = rest[26:33]
     xl, y, xh, z, k = place()
     copies = Copies(send, recv)
     mask_copy = copies.local(mask_hbm, mask)
-    meet(all_peers())
+    packing, unpacking, flat, joined = rest[33:37]
+    hidden_relay = Relay(rest[37], rest[38], rest[39])
+    relays = [Relay(rest[i], rest[i + 1], rest[i + 2]) for i in (40, 43, 46)]
+    greet()
+    pick_rows(packing, node_row)
+    pick_slots(unpacking, own_col)
+    hidden_relay.pack(packing, hidden, 0)
+    meet()
     tiles = lambda slot: pl.ds(slot * 4, 4)
     mine, pair = xl * 4 + y, (1 - xl) * 4 + y
     gathered, over, trade, col_copies, cross_copy = [[] for _ in range(4)], {}, {}, {}, {}
@@ -350,7 +431,7 @@
         trade[c].wait_recv()
 
         def one(i, carry):
-            paired[c][i] = (block[c][k * 32 + i].astype(F32) + traded[c][i].astype(F32)).astype(BF16)
+            block[c][k * 32 + i] = (block[c][k * 32 + i].astype(F32) + traded[c][i].astype(F32)).astype(BF16)
             return carry
 
         lax.fori_loop(0, 32, one, 0)
@@ -359,12 +440,12 @@
             to_z = (z + d) % 4
             col_copies[c].append(
                 copies.remote(
-                    paired[c].at[pl.ds(to_z * 8, 8)], near[c].at[pl.ds(i * 8, 8)], at_device(xl, y, xh, to_z, k)
+                    block[c].at[pl.ds(k * 32 + to_z * 8, 8)], near[c].at[pl.ds(i * 8, 8)], at_device(xl, y, xh, to_z, k)
                 )
             )
 
     def col_sum(c, side, i):
-        total = paired[c][z * 8 + side * 4 + i].astype(F32)
+        total = block[c][k * 32 + z * 8 + side * 4 + i].astype(F32)
         for n in range(3):
             total = total + near[c][n * 8 + side * 4 + i].astype(F32)
         return total
@@ -384,7 +465,9 @@
         cross_copy[c].wait_recv()
 
         def one(i, carry):
-            out_ref[c, i] = col_sum(c, xh, i) + crossed[c][i].astype(F32)
+            back = col_sum(c, xh, i) + crossed[c][i].astype(F32)
+            at = (pl.ds(pl.multiple_of(i * 128, 128), 128), pl.ds(c * 128, 128))
+            joined[at] = (own_back[at] + back.T).astype(BF16)
             return carry
 
         lax.fori_loop(0, 4, one, 0)
@@ -490,6 +573,20 @@
             copy.wait_recv()
         at = rows_of(k * 512, 0, 512)
         level["to_core"] = copies.remote(sum_ref.at[at], sum_ref.at[at], at_device(xl, y, xh, z, 1 - k))
+
+    def take(relay, out, first):
+        relay.collect(flat)
+
+        def one(i, at):
+            rows = jnp.dot(unpacking[at], flat[:, pl.ds(0, relay.width)], preferred_element_type=F32)
+            out[at, pl.ds(first, relay.width)] = rows.astype(BF16)
+
+        each_block(4, one)
+
+    def send_first():
+        sum_cross(1)
+        relays[0].pack(packing, joined, 0)
+        relays[0].start()
 
     own(0)
     grad_core()
@@ -506,6 +603,7 @@
     grad_x()
     product(1, grad_total)
     onward(3)
+    hidden_relay.start()
     sum_cores(1)
     grad_to_y()
     sum_cols(0)
@@ -514,36 +612,56 @@
     sum_cols(1)
     grad_to_core()
     sum_cross(0)
-    product(3, lambda: None)
+    product(3, send_first)
     sum_cores(3)
     sum_cols(2)
-    sum_cross(1)
+    take(hidden_relay, hidden_out, 0)
+    sum_cross(2)
+    relays[1].pack(packing, joined, 256)
+    relays[1].start()
     sum_cols(3)
-    sum_cross(2)
     sum_cross(3)
+    relays[2].pack(packing, joined, 384)
+    relays[2].start()
+    take(relays[0], grad_out, 0)
+    take(relays[1], grad_out, 256)
+    take(relays[2], grad_out, 384)
     level["to_core"].wait_recv()
     copies.finish()
-
-
-def backward_exchange(tables, s, grads, masks, scale):
+    for relay in relays + [hidden_relay]:
+        relay.finish()
+
+
+def backward_exchange(tables, node_row, own_col, hidden, own_back, s, grads, masks, scale):
+    rows, width = hidden.shape
+    slots = DEVICES * 8
     return pl.pallas_call(
         functools.partial(backward_kernel, scale),
-        in_specs=[SMEM_SPEC] * 5 + [VMEM_SPEC, VMEM_SPEC, ANY_SPEC],
-        out_specs=[VMEM_SPEC, VMEM_SPEC],
-        out_shape=[jax.ShapeDtypeStruct(s.shape, F32), jax.ShapeDtypeStruct(grads.shape, F32)],
+        in_specs=[SMEM_SPEC] * 5 + [VMEM_SPEC] * 6 + [ANY_SPEC],
+        out_specs=[VMEM_SPEC] * 3,
+        out_shape=[
+            jax.ShapeDtypeStruct((rows, width), BF16),
+            jax.ShapeDtypeStruct((rows, width), BF16),
+            jax.ShapeDtypeStruct(grads.shape, F32),
+        ],
         scratch_shapes=[tile_buffer(256), tile_buffer(256)]
         + [tile_buffer(32)] * 4
         + [tile_buffer(64)] * 4
-        + [tile_buffer(32)] * 8
+        + [tile_buffer(32)] * 4
         + [tile_buffer(24)] * 4
         + [tile_buffer(4)] * 8
         + [pltpu.SemaphoreType.DMA((96,)), pltpu.SemaphoreType.DMA((96,))]
         + [pltpu.VMEM((512, 512), BF16)] * 3
         + [pltpu.VMEM((3, 128, 512), BF16), pltpu.VMEM((1, 128, 512), F32)]
-        + [pltpu.VMEM((3, 32, 512), F32), pltpu.VMEM((2, 32, 512), F32)],
+        + [pltpu.VMEM((3, 32, 512), F32), pltpu.VMEM((2, 32, 512), F32)]
+        + [pltpu.VMEM((slots, rows), BF16), pltpu.VMEM((rows, slots), BF16)]
+        + [pltpu.VMEM((slots, width), BF16), pltpu.VMEM((rows, width), BF16)]
+        + boxes(width)
+        + boxes(width // 2)
+        + boxes(width // 4) * 2,
         compiler_params=remote_params(1),
         name="backward_exchange",
-    )(*tables, s, grads, masks)
+    )(*tables, node_row, own_col, hidden, own_back, s, grads, masks)
 
 
 def column_order(columns):
@@ -636,30 +754,6 @@
     )(summed, x, extra, ws, wn)
 
 
-def join_kernel(own_ref, back_ref, out_ref):
-    back = jnp.concatenate([back_ref[c, 0].T for c in range(4)], axis=1)
-    out_ref[...] = (own_ref[...] + back).astype(BF16)
-
-
-def join(own_back, back):
-    rows, width = own_back.shape
-    return pl.pallas_call(
-        join_kernel,
-        grid=(rows // 128,),
-        in_specs=[
-            pl.BlockSpec((128, width), lambda i: (i, 0)),
-            pl.BlockSpec((4, 1, 128, 128), lambda i: (0, i, 0, 0)),
-        ],
-        out_specs=pl.BlockSpec((128, width), lambda i: (i, 0)),
-        out_shape=jax.ShapeDtypeStruct((rows, width), BF16),
-        name="join",
-    )(own_back, back)
-
-
-def swap_all(data, axes):
-    return lax.all_to_all(data, axes, split_axis=0, concat_axis=0, tiled=True)
-
-
 def on_device(
     features, tile_cols, tile_masks, degree, owner_nodes, owner_position, self_weight, neigh_weight, cotangent
 ):
@@ -667,7 +761,6 @@
     n_row, n_col = lax.axis_size("row"), lax.axis_size("col")
     devices = n_row * n_col
     slot_count = 2 * rows // devices
-    slots = devices * slot_count
     masks = tile_masks.reshape(256, 128, 128)
     own_dest = owner_nodes // rows
     own_flat = own_dest * slot_count + rank_within(own_dest, jnp.arange(rows, dtype=jnp.int32))
@@ -675,18 +768,16 @@
     node_flat = node_source * slot_count + rank_within(node_source, owner_position)
     cols, tables = column_order(tile_cols[0, 0])
 
-    both = ("row", "col")
     degree_cols = jnp.broadcast_to(degree.astype(BF16)[:, None], (rows, 128))
-    node_x = unpack_tiles(node_flat, swap_all(pack(own_flat, features, slots), both))
     extra = jnp.concatenate([cotangent, degree_cols], axis=1)
-    node_extra = unpack(node_flat, swap_all(pack(own_flat, extra, slots), both))
-    summed = forward_exchange(cols, node_x, masks)
+    own_row, own_col = own_flat.reshape(1, rows), own_flat.reshape(rows, 1)
+    node_row, node_col = node_flat.reshape(1, rows), node_flat.reshape(rows, 1)
+    summed, node_x, node_extra = forward_exchange(cols, own_row, node_col, features, extra, masks)
     hidden, own_back, spread, grads = dense(summed, node_x, node_extra, self_weight, neigh_weight)
     grad_scale = 1.0 / math.sqrt(rows * devices)
-    back, sums = backward_exchange(tables, spread, grads, masks, grad_scale)
-    grad_node = join(own_back, back)
-    hidden_out = unpack(own_flat, swap_all(pack(node_flat, hidden, slots), both))
-    grad_out = unpack(own_flat, swap_all(pack(node_flat, grad_node, slots), both))
+    hidden_out, grad_out, sums = backward_exchange(
+        tables, node_row, own_col, hidden, own_back, spread, grads, masks, grad_scale
+    )
     return hidden_out, grad_out, sums[:width], sums[width:]
 
 

time: 318 us -> 285 us (0.90)
  waiting for transfers between devices: 41 us -> 0 us
  Pallas kernels: 231 us -> 266 us
  starting transfers between devices: 29.2 us -> 0 us
  other arithmetic: 6.96 us -> 10.2 us
    all_to_all x4 -> x0, waiting for transfers between devices: 41 us -> none  [swap_all(): return lax.all_to_all(data, axes, split_axis=0, concat_axis=0, tiled=True)]
    pallas_call x1, Pallas kernels: 105 us -> 143 us  [backward_exchange(): pl.pallas_call(functools.partial(backward_kernel, scale), in_specs=[SMEM_...]
    all_to_all x4 -> x0, starting transfers between devices: 29.2 us -> none  [swap_all(): return lax.all_to_all(data, axes, split_axis=0, concat_axis=0, tiled=True)]
    pallas_call x10 -> x1, Pallas kernels: 116 us -> 113 us  [forward_exchange(): pl.pallas_call(forward_kernel, in_specs=[SMEM_SPEC] + [VMEM_SPEC] * 4 + [...]
  transfers between devices with their start and end apart: 4 -> 0, of which waited for: 3 -> 0; matrix products, arithmetic and copies ran while one was open for 3% -> 0% of each run, Pallas kernels for 31% -> 0%
where the time goes in v4:
time: 285 us; the launch traced here: 284 us
  Pallas kernels  266 us (93%)
  other arithmetic  10.2 us (4%)
  local copies, waits for them, and re-layouts  7.42 us (3%)
    pallas_call x1, Pallas kernels, backward_exchange(): pl.pallas_call(functools.partial(backward_kernel, scale), in_specs=[SMEM_...  143 us
    pallas_call x1, Pallas kernels, forward_exchange(): pl.pallas_call(forward_kernel, in_specs=[SMEM_SPEC] + [VMEM_SPEC] * 4 + [...  113 us
    pallas_call x1, Pallas kernels, dense(): pl.pallas_call(dense_kernel, grid=(rows // step,), in_specs=[tiled, tiled...  9.19 us

profile of v4, /device:TPU:1, one launch (start us, length us, event | category | flops | bytes accessed | tf_op | source)
XLA Modules:
  0.0 284.4 jit_solution(16843840461239398790)
XLA Ops:
  0.6 0.7 convert_element_type.27
  1.3 0.7 add_select_fusion
  2.0 0.3 convert_reduce_fusion
  2.3 0.7 multiply_add_fusion
  3.0 0.0 copy-start.3
  3.0 0.7 add_select_fusion.1
  3.6 1.1 convert_reduce_fusion.1
  4.7 0.7 multiply_add_fusion.1
  5.4 0.0 copy-start.2
  5.4 0.8 copy.16
  6.2 0.1 reshape_squeeze.3
  6.3 0.6 multiply_add_fusion.2
  6.9 0.2 convert_reduce_fusion.2
  7.1 0.1 convert_reduce_fusion.3
  7.2 0.6 add_maximum_fusion.last_ref
  7.7 0.1 fusion.1
  7.8 0.5 convert_element_type.24.some_ref
  8.4 0.2 select_reduce_fusion
  8.5 0.0 copy-start.4
  8.5 0.7 compare_convert_fusion.keep_ref
  9.2 0.6 and_select_fusion.from_ref
  9.8 0.1 broadcast_in_dim.23
  9.9 0.9 copy.17.node_col
  10.8 0.9 copy.18.own_col
  11.7 1.9 pad_maximum_fusion.extra
  13.6 0.0 copy-done.3
  13.6 113.3 %forward_exchange.1 = (f32[4,4,128,128]{3,2,1,0:T(8,128)}, bf16[4,4,128,128]{3,2,1,0:T(8,128)(2,1)}, bf16[512,640]{1,0:T(8,128)(2,1)}) custom-call(s32[256]{0:T(256)} %get-tuple-element.26.cols_ref, s32[1,512]{1,0:T(1,128)} %bitcast.13, s32[512,1]{1,0:T(8,128)} %copy.17.node_col, bf16[512,512]{1,0:T(8,128)(2,1)} %features.1, ...), custom_call_target="tpu_custom_call" | custom-call | tf_op jit(solution)/shard_map/forward_exchange/pallas_call | solution.py:344
  127.0 0.0 copy-done.2
  127.0 0.0 copy-done.4
  127.0 9.2 %dense.1 = (bf16[512,512]{1,0:T(8,128)(2,1)}, f32[512,512]{1,0:T(8,128)}, bf16[4,4,128,128]{3,2,1,0:T(8,128)(2,1)}, f32[1024,512]{1,0:T(8,128)}) custom-call(f32[4,4,128,128]{3,2,1,0:T(8,128)} %get-tuple-element.14.sum_ref, bf16[4,4,128,128]{3,2,1,0:T(8,128)(2,1)} %get-tuple-element.15.x_ref, bf16[512,640]{1,0:T(8,128)(2,1)} %get-tuple-element.16.extra_ref, ...), custom_call_target="tpu_custom_call" | custom-call | tf_op jit(solution)/shard_map/dense/pallas_call | solution.py:730
  136.2 143.5 %backward_exchange.1 = (bf16[512,512]{1,0:T(8,128)(2,1)}, bf16[512,512]{1,0:T(8,128)(2,1)}, f32[1024,512]{1,0:T(8,128)}) custom-call(s32[256]{0:T(256)} %copy-done.4, s32[256]{0:T(256)} %and_select_fusion.from_ref, f32[256]{0:T(256)} %compare_convert_fusion.keep_ref, s32[64]{0:T(128)} %add_maximum_fusion.last_ref, f32[64]{0:T(128)} %convert_element_type.24.some_ref, ...), custom_call_target="tpu_custom_call" | custom-call | tf_op jit(solution)/shard_map/backward_exchange/pallas_call | solution.py:638
  279.7 0.0 copy-start.1
  279.7 0.0 copy-start
  279.7 3.1 %fusion.8 = (f32[512,512]{1,0:T(8,128)}, f32[512,512]{1,0:T(8,128)}) fusion(f32[1024,512]{1,0:T(8,128)} %get-tuple-element.23), kind=kLoop, calls=%fused_computation.61 | loop fusion | bytes 4194304 | tf_op jit(solution)/shard_map/slice | solution.py:781
  282.8 0.0 copy-done.1
  282.8 0.8 copy.21
  283.6 0.0 copy-done
  283.6 0.8 copy.22
  (1 shorter events, 0.0 us)
Async XLA Ops:
  3.0 10.6 %copy-start.3 = (s32[512]{0:T(512)}, s32[512]{0:T(512)S(1)}, u32[]{:S(2)}) copy-start(s32[512]{0:T(512)S(1)} %multiply_add_fusion) | copy-start | bytes 6148
  5.4 121.5 %copy-start.2 = (s32[512]{0:T(512)}, s32[512]{0:T(512)S(1)}, u32[]{:S(2)}) copy-start(s32[512]{0:T(512)S(1)} %multiply_add_fusion.1) | copy-start | bytes 6148
  8.5 118.4 %copy-start.4 = (s32[256]{0:T(256)}, s32[256]{0:T(256)S(1)}, u32[]{:S(2)}) copy-start(s32[256]{0:T(256)S(1)} %get-tuple-element.25.pick_ref) | copy-start | bytes 3076
  279.7 3.1 %copy-start.1 = (bf16[512,512]{1,0:T(8,128)(2,1)S(1)}, bf16[512,512]{1,0:T(8,128)(2,1)}, u32[]{:S(2)}) copy-start(bf16[512,512]{1,0:T(8,128)(2,1)} %get-tuple-element.37) | copy-start | bytes 1572868
  279.7 3.9 %copy-start = (bf16[512,512]{1,0:T(8,128)(2,1)S(1)}, bf16[512,512]{1,0:T(8,128)(2,1)}, u32[]{:S(2)}) copy-start(bf16[512,512]{1,0:T(8,128)(2,1)} %get-tuple-element.38) | copy-start | bytes 1572868

commit v5 on v4

--- a/solution.py
+++ b/solution.py
@@ -15,12 +15,6 @@
 VMEM_LIMIT = 60 * 1024 * 1024
 ROW_T = (((0,), (0,)), ((), ()))
 COL_T = (((1,), (1,)), ((), ()))
-
-
-def rank_within(group_keys, order_keys):
-    same_group = group_keys[:, None] == group_keys[None, :]
-    earlier = order_keys[None, :] < order_keys[:, None]
-    return jnp.sum(same_group & earlier, axis=1)
 
 
 def params(**kw):
@@ -116,7 +110,7 @@
 def pick_rows(table, flat_row):
     def one(i, carry):
         slot = lax.broadcasted_iota(jnp.int32, (128, table.shape[1]), 0) + i * 128
-        table[pl.ds(pl.multiple_of(i * 128, 128), 128)] = jnp.where(slot == flat_row[...], 1.0, 0.0).astype(BF16)
+        table[pl.ds(pl.multiple_of(i * 128, 128), 128)] = jnp.where(slot == flat_row, 1.0, 0.0).astype(BF16)
         return carry
 
     lax.fori_loop(0, table.shape[0] // 128, one, 0)
@@ -130,6 +124,45 @@
         return carry
 
     lax.fori_loop(0, table.shape[0] // 128, one, 0)
+
+
+def upright(row):
+    return jnp.broadcast_to(row, (128, row.shape[1])).T
+
+
+def rank_row(group, order, side):
+    count = group.shape[1]
+    side[0, pl.ds(0, count)] = upright(group)
+    side[1, pl.ds(0, count)] = upright(order)
+
+    def one(i, total):
+        at = pl.ds(pl.multiple_of(i * 128, 128), 128)
+        before = (side[0, at, pl.ds(0, 1)] == group) & (side[1, at, pl.ds(0, 1)] < order)
+        return total + jnp.sum(jnp.where(before, 1, 0), axis=0, keepdims=True)
+
+    return lax.fori_loop(0, count // 128, one, jnp.zeros((1, count), jnp.int32))
+
+
+def column_tables(cols, tables):
+    count = cols.shape[1]
+    block = cols // 4
+    tile = ((block % 2) * 8 + ((block // 2) % 4) * 2 + block // 8) * 4 + cols % 4
+    entry = lax.broadcasted_iota(jnp.int32, (1, count), 1)
+    key = tile * count + entry
+    rank = jnp.sum(jnp.where(upright(key)[:, :1] < key, 1, 0), axis=0, keepdims=True)
+    place_of, tile_of = upright(rank)[:, :1], upright(tile)[:, :1]
+    source = lax.broadcasted_iota(jnp.int32, (count, count), 0)
+    spot = lax.broadcasted_iota(jnp.int32, (count, count), 1)
+    add = lambda values: jnp.sum(values, axis=0, keepdims=True)
+    pick = add(jnp.where(place_of == spot, source, 0))
+    here = add(jnp.where(place_of == spot, tile_of, 0))
+    before = add(jnp.where(place_of == spot - 1, tile_of + 1, 0)) - 1
+    tables[0:1] = pick
+    tables[1:2] = pick // 8
+    tables[2:3] = jnp.where(here == before, 1, 0)
+    tables[3:4] = jnp.maximum(add(jnp.where(tile_of <= spot, 1, 0)) - 1, 0)
+    tables[4:5] = jnp.minimum(add(jnp.where(tile_of == spot, 1, 0)), 1)
+    tables[5:8] = jnp.zeros((3, count), jnp.int32)
 
 
 def each_block(count, body):
@@ -168,8 +201,15 @@
 FAR_FIRST = (2, 1, 3)
 
 
+def held_tile(col):
+    block = lax.shift_right_logical(col, 2)
+    half = (block & 1) * 8 + lax.shift_right_logical(block, 3) * 4 + (lax.shift_right_logical(block, 1) & 3)
+    return half * 4 + (col & 3)
+
+
 def forward_kernel(
-    cols_ref, own_row, node_col, features, extra, mask_hbm, out_ref, x_ref, node_extra, mask, *rest
+    cols_ref, cols_row, nodes, position, degree, features, cotangent, mask_hbm,
+    out_ref, x_ref, node_extra, own_col, node_row, tables, mask, *rest
 ):
     held, part, near, cross, crossed, (send, recv) = (
         rest[0:4], rest[4:8], rest[8:12], rest[12:16], rest[16:20], rest[20:22]
@@ -180,14 +220,27 @@
     packing, unpacking, flat, flat_extra = rest[22:26]
     relays = [Relay(rest[26], rest[27], rest[28]), Relay(rest[29], rest[30], rest[31])]
     extra_relay = Relay(rest[32], rest[33], rest[34])
+    extra, side, node_col = rest[35:38]
+    width = features.shape[1]
     greet()
+    lane = lax.broadcasted_iota(jnp.int32, nodes.shape, 1)
+    dest = nodes[...] // width
+    own_row = dest * 8 + rank_row(dest, lane, side)
     pick_rows(packing, own_row)
     relays[0].pack(packing, features, 0)
     meet()
     relays[0].start()
     relays[1].pack(packing, features, 256)
     relays[1].start()
+    source = position[...] // width
+    node_slot = source * 8 + rank_row(source, position[...], side)
+    node_row[...] = node_slot
+    node_col[...] = upright(node_slot)[:, :1]
     pick_slots(unpacking, node_col)
+    own_col[...] = upright(own_row)[:, :1]
+    column_tables(cols_row[...], tables)
+    extra[:, pl.ds(0, width)] = cotangent[...]
+    extra[:, pl.ds(width, 128)] = upright(degree[...]).astype(F32).astype(BF16)
     extra_relay.pack(packing, extra, 0)
 
     def unpack(c):
@@ -241,7 +294,7 @@
             def one(q, carry):
                 t = (q // 4) * 16 + to_y * 4 + q % 4
                 left = jnp.concatenate([mask[t * 8 + j] for j in range(8)], axis=1)
-                right = jnp.concatenate([held[c][cols_ref[t * 8 + j]] for j in range(8)], axis=0)
+                right = jnp.concatenate([held[c][held_tile(cols_ref[t * 8 + j])] for j in range(8)], axis=0)
                 part[c][to_y * 8 + q] = jnp.dot(left, right, preferred_element_type=F32).astype(BF16)
                 return carry
 
@@ -337,18 +390,23 @@
     ]
 
 
-def forward_exchange(cols, own_row, node_col, features, extra, masks):
+def forward_exchange(cols, nodes, position, degree, features, cotangent, masks):
     rows, width = features.shape
-    slots, wide = DEVICES * 8, extra.shape[1]
+    slots, wide = DEVICES * 8, width + 128
     tiled = (4, 4, 128, 128)
+    count = cols.shape[0]
+    as_row = lambda values: values.reshape(1, -1)
     return pl.pallas_call(
         forward_kernel,
-        in_specs=[SMEM_SPEC] + [VMEM_SPEC] * 4 + [ANY_SPEC],
-        out_specs=[VMEM_SPEC] * 3,
+        in_specs=[SMEM_SPEC] + [VMEM_SPEC] * 6 + [ANY_SPEC],
+        out_specs=[VMEM_SPEC] * 6,
         out_shape=[
             jax.ShapeDtypeStruct(tiled, F32),
             jax.ShapeDtypeStruct(tiled, BF16),
             jax.ShapeDtypeStruct((rows, wide), BF16),
+            jax.ShapeDtypeStruct((rows, 1), jnp.int32),
+            jax.ShapeDtypeStruct((1, rows), jnp.int32),
+            jax.ShapeDtypeStruct((8, count), jnp.int32),
         ],
         scratch_shapes=[tile_buffer(256)]
         + [tile_buffer(64)] * 4
@@ -359,14 +417,15 @@
         + [pltpu.VMEM((slots, rows), BF16), pltpu.VMEM((rows, slots), BF16)]
         + [pltpu.VMEM((slots, width // 2), BF16), pltpu.VMEM((slots, wide), BF16)]
         + boxes(width // 2) * 2
-        + boxes(wide),
+        + boxes(wide)
+        + [pltpu.VMEM((rows, wide), BF16), pltpu.VMEM((2, rows, 128), jnp.int32), pltpu.VMEM((rows, 1), jnp.int32)],
         compiler_params=remote_params(0),
         name="forward_exchange",
-    )(cols, own_row, node_col, features, extra, masks)
+    )(cols, as_row(cols), as_row(nodes), as_row(position), as_row(degree), features, cotangent, masks)
 
 
 def backward_kernel(
-    scale, pick_ref, from_ref, keep_ref, last_ref, some_ref, node_row, own_col, hidden, own_back, s_ref, g_ref, mask_hbm,
+    scale, tables, node_row, own_col, hidden, own_back, s_ref, g_ref, mask_hbm,
     hidden_out, grad_out, sum_ref, mask, chain, *rest
 ):
     held, block, traded, near, cross, crossed, (send, recv) = (
@@ -380,7 +439,7 @@
     hidden_relay = Relay(rest[37], rest[38], rest[39])
     relays = [Relay(rest[i], rest[i + 1], rest[i + 2]) for i in (40, 43, 46)]
     greet()
-    pick_rows(packing, node_row)
+    pick_rows(packing, node_row[...])
     pick_slots(unpacking, own_col)
     hidden_relay.pack(packing, hidden, 0)
     meet()
@@ -409,8 +468,8 @@
         def one(g, total):
             for u in range(8):
                 e = g * 8 + u
-                piece = jnp.dot(held[c][from_ref[e]], mask[pick_ref[e]], preferred_element_type=F32)
-                total = total * keep_ref[e] + piece
+                piece = jnp.dot(held[c][tables[1, e]], mask[tables[0, e]], preferred_element_type=F32)
+                total = total * tables[2, e].astype(F32) + piece
                 chain[e] = total.astype(BF16)
             return total
 
@@ -419,7 +478,7 @@
         lax.fori_loop(16, 32, one, half)
 
         def settle(p, carry):
-            block[c][p] = (chain[last_ref[p]].astype(F32) * some_ref[p]).astype(BF16)
+            block[c][p] = (chain[tables[3, p]].astype(F32) * tables[4, p].astype(F32)).astype(BF16)
             return carry
 
         lax.fori_loop(0, 64, settle, 0)
@@ -474,9 +533,7 @@
 
     width = g_ref.shape[1]
     quarter_at = k * 512 + z * 128
-    part_at = quarter_at + y * 32
     x_index = xl * 2 + xh
-    piece_at = part_at + x_index * 8
     x_others = [((xl + a) % 2, (xh + b) % 2) for a, b in ((1, 1), (0, 1), (1, 0))]
     level = {}
 
@@ -548,31 +605,26 @@
         total = g_piece[0, rows_of(0, x_index * 8, 8)]
         for i in range(3):
             total = total + g_piece[1, pl.ds(i * 8, 8)]
-        at = rows_of(piece_at, 0, 8)
+        at = (k, z, y, rows_of(0, x_index * 8, 8))
         sum_ref[at] = total * scale
         level["to_x"] = [copies.remote(sum_ref.at[at], sum_ref.at[at], at_device(a, y, b, z, k)) for a, b in x_others]
 
+    def grad_to_z():
+        for copy in level["to_x"]:
+            copy.wait_recv()
+        at = sum_ref.at[k, z, y]
+        level["to_z"] = [copies.remote(at, at, at_device(xl, y, xh, (z + d) % 4, k)) for d in FAR_FIRST]
+
     def grad_to_y():
-        for copy in level["to_x"]:
-            copy.wait_recv()
-        at = rows_of(part_at, 0, 32)
-        level["to_y"] = [
-            copies.remote(sum_ref.at[at], sum_ref.at[at], at_device(xl, (y + d) % 4, xh, z, k)) for d in FAR_FIRST
-        ]
-
-    def grad_to_z():
+        for copy in level["to_z"]:
+            copy.wait_recv()
+        at = sum_ref.at[k, :, y]
+        level["to_y"] = [copies.remote(at, at, at_device(xl, (y + d) % 4, xh, z, k)) for d in FAR_FIRST]
+
+    def grad_to_core():
         for copy in level["to_y"]:
             copy.wait_recv()
-        at = rows_of(quarter_at, 0, 128)
-        level["to_z"] = [
-            copies.remote(sum_ref.at[at], sum_ref.at[at], at_device(xl, y, xh, (z + d) % 4, k)) for d in FAR_FIRST
-        ]
-
-    def grad_to_core():
-        for copy in level["to_z"]:
-            copy.wait_recv()
-        at = rows_of(k * 512, 0, 512)
-        level["to_core"] = copies.remote(sum_ref.at[at], sum_ref.at[at], at_device(xl, y, xh, z, 1 - k))
+        level["to_core"] = copies.remote(sum_ref.at[k], sum_ref.at[k], at_device(xl, y, xh, z, 1 - k))
 
     def take(relay, out, first):
         relay.collect(flat)
@@ -605,9 +657,9 @@
     onward(3)
     hidden_relay.start()
     sum_cores(1)
-    grad_to_y()
+    grad_to_z()
     sum_cols(0)
-    product(2, grad_to_z)
+    product(2, grad_to_y)
     sum_cores(2)
     sum_cols(1)
     grad_to_core()
@@ -637,12 +689,12 @@
     slots = DEVICES * 8
     return pl.pallas_call(
         functools.partial(backward_kernel, scale),
-        in_specs=[SMEM_SPEC] * 5 + [VMEM_SPEC] * 6 + [ANY_SPEC],
+        in_specs=[SMEM_SPEC] + [VMEM_SPEC] * 6 + [ANY_SPEC],
         out_specs=[VMEM_SPEC] * 3,
         out_shape=[
             jax.ShapeDtypeStruct((rows, width), BF16),
             jax.ShapeDtypeStruct((rows, width), BF16),
-            jax.ShapeDtypeStruct(grads.shape, F32),
+            jax.ShapeDtypeStruct((2, 4, 4, 32, width), F32),
         ],
         scratch_shapes=[tile_buffer(256), tile_buffer(256)]
         + [tile_buffer(32)] * 4
@@ -661,29 +713,7 @@
         + boxes(width // 4) * 2,
         compiler_params=remote_params(1),
         name="backward_exchange",
-    )(*tables, node_row, own_col, hidden, own_back, s, grads, masks)
-
-
-def column_order(columns):
-    flat = columns.reshape(-1)
-    count = flat.shape[0]
-    block = flat // 4
-    xh, z, k = block // 8, (block // 2) % 4, block % 2
-    held_tile = (k * 8 + xh * 4 + z) * 4 + flat % 4
-    back_tile = (k * 8 + z * 2 + xh) * 4 + flat % 4
-    entry = jnp.arange(count, dtype=jnp.int32)
-    key = back_tile * count + entry
-    rank = jnp.sum((key[None, :] < key[:, None]).astype(jnp.int32), axis=1)
-    hit = rank[None, :] == entry[:, None]
-    pick = jnp.sum(jnp.where(hit, entry[None, :], 0), axis=1)
-    sorted_tile = jnp.sum(jnp.where(hit, back_tile[None, :], 0), axis=1)
-    before = jnp.concatenate([jnp.full((1,), -1, jnp.int32), sorted_tile[:-1]])
-    keep = (sorted_tile == before).astype(F32)
-    spot = jnp.arange(64, dtype=jnp.int32)
-    upto = jnp.sum((back_tile[None, :] <= spot[:, None]).astype(jnp.int32), axis=1)
-    some = jnp.any(back_tile[None, :] == spot[:, None], axis=1).astype(F32)
-    last = jnp.maximum(upto - 1, 0)
-    return held_tile, (pick, pick // 8, keep, last, some)
+    )(tables, node_row, own_col, hidden, own_back, s, grads, masks)
 
 
 def dense_kernel(
@@ -758,27 +788,17 @@
     features, tile_cols, tile_masks, degree, owner_nodes, owner_position, self_weight, neigh_weight, cotangent
 ):
     rows, width = features.shape
-    n_row, n_col = lax.axis_size("row"), lax.axis_size("col")
-    devices = n_row * n_col
-    slot_count = 2 * rows // devices
-    masks = tile_masks.reshape(256, 128, 128)
-    own_dest = owner_nodes // rows
-    own_flat = own_dest * slot_count + rank_within(own_dest, jnp.arange(rows, dtype=jnp.int32))
-    node_source = owner_position // rows
-    node_flat = node_source * slot_count + rank_within(node_source, owner_position)
-    cols, tables = column_order(tile_cols[0, 0])
-
-    degree_cols = jnp.broadcast_to(degree.astype(BF16)[:, None], (rows, 128))
-    extra = jnp.concatenate([cotangent, degree_cols], axis=1)
-    own_row, own_col = own_flat.reshape(1, rows), own_flat.reshape(rows, 1)
-    node_row, node_col = node_flat.reshape(1, rows), node_flat.reshape(rows, 1)
-    summed, node_x, node_extra = forward_exchange(cols, own_row, node_col, features, extra, masks)
+    masks = tile_masks.reshape(-1, *tile_masks.shape[-2:])
+    summed, node_x, node_extra, own_col, node_row, tables = forward_exchange(
+        tile_cols.reshape(-1), owner_nodes, owner_position, degree, features, cotangent, masks
+    )
     hidden, own_back, spread, grads = dense(summed, node_x, node_extra, self_weight, neigh_weight)
-    grad_scale = 1.0 / math.sqrt(rows * devices)
+    grad_scale = 1.0 / math.sqrt(rows * DEVICES)
     hidden_out, grad_out, sums = backward_exchange(
         tables, node_row, own_col, hidden, own_back, spread, grads, masks, grad_scale
     )
-    return hidden_out, grad_out, sums[:width], sums[width:]
+    sums = sums.reshape(2, width, width)
+    return hidden_out, grad_out, sums[0], sums[1]
 
 
 def solution(mesh):

time: 285 us -> 279 us (0.979)
  other arithmetic: 10.2 us -> 0 us
  Pallas kernels: 266 us -> 272 us
    pallas_call x1, Pallas kernels: 143 us -> 149 us  [backward_exchange(): pl.pallas_call(functools.partial(backward_kernel, scale), in_specs=[SMEM_...]
where the time goes in v5:
time: 279 us
  Pallas kernels  272 us (97%)
  local copies, waits for them, and re-layouts  6.88 us (2%)
    pallas_call x1, Pallas kernels, backward_exchange(): pl.pallas_call(functools.partial(backward_kernel, scale), in_specs=[SMEM_...  149 us
    pallas_call x1, Pallas kernels, forward_exchange(): pl.pallas_call(forward_kernel, in_specs=[SMEM_SPEC] + [VMEM_SPEC] * 6 + [...  114 us
    pallas_call x1, Pallas kernels, dense(): pl.pallas_call(dense_kernel, grid=(rows // step,), in_specs=[tiled, tiled...  9.18 us

profile of v5, /device:TPU:1, one launch (start us, length us, event | category | flops | bytes accessed | tf_op | source)
XLA Modules:
  0.0 279.2 jit_solution(10582236424651394952)
XLA Ops:
  0.6 0.8 copy.14
  1.4 0.7 reshape_reshape.3.cols_row
  2.0 0.7 reshape.28.cols_ref
  2.7 113.7 %forward_exchange.1 = (f32[4,4,128,128]{3,2,1,0:T(8,128)}, bf16[4,4,128,128]{3,2,1,0:T(8,128)(2,1)}, bf16[512,640]{1,0:T(8,128)(2,1)}, s32[512,1]{1,0:T(8,128)}, s32[1,512]{1,0:T(1,128)}, /*index=5*/s32[8,256]{1,0:T(8,128)}) custom-call(s32[256]{0:T(256)} %reshape.28.cols_ref, s32[1,256]{1,0:T(1,128)} %reshape_reshape.3.cols_row, s32[1,512]{1,0:T(1,128)} %bitcast.14, ...), custom_call_target="tpu_custom_call" | custom-call | tf_op jit(solution)/shard_map/forward_exchange/pallas_call | solution.py:399
  116.4 9.2 %dense.1 = (bf16[512,512]{1,0:T(8,128)(2,1)}, f32[512,512]{1,0:T(8,128)}, bf16[4,4,128,128]{3,2,1,0:T(8,128)(2,1)}, f32[1024,512]{1,0:T(8,128)}) custom-call(f32[4,4,128,128]{3,2,1,0:T(8,128)} %get-tuple-element.20.sum_ref, bf16[4,4,128,128]{3,2,1,0:T(8,128)(2,1)} %get-tuple-element.21.x_ref, bf16[512,640]{1,0:T(8,128)(2,1)} %get-tuple-element.22.extra_ref, ...), custom_call_target="tpu_custom_call" | custom-call | tf_op jit(solution)/shard_map/dense/pallas_call | solution.py:760
  125.6 148.7 %backward_exchange.1 = (bf16[512,512]{1,0:T(8,128)(2,1)}, bf16[512,512]{1,0:T(8,128)(2,1)}, f32[2,4,4,32,512]{4,3,2,1,0:T(8,128)}) custom-call(s32[8,256]{1,0:T(8,128)} %get-tuple-element.17.tables, s32[1,512]{1,0:T(1,128)} %get-tuple-element.18.node_row, s32[512,1]{1,0:T(8,128)} %get-tuple-element.19.own_col, bf16[512,512]{1,0:T(8,128)(2,1)} %get-tuple-element.23.hidden, ...), custom_call_target="tpu_custom_call" | custom-call | tf_op jit(solution)/shard_map/backward_exchange/pallas_call | solution.py:690
  274.4 0.0 copy-start.1
  274.4 0.0 copy-start
  274.4 3.2 %fusion = (f32[1,4,4,32,512]{4,3,2,1,0:T(8,128)}, f32[1,4,4,32,512]{4,3,2,1,0:T(8,128)}) fusion(f32[2,4,4,32,512]{4,3,2,1,0:T(8,128)} %get-tuple-element.29), kind=kLoop, calls=%fused_computation | loop fusion | bytes 4194304 | tf_op jit(solution)/shard_map/slice | solution.py:801
  277.6 0.0 copy-done.1
  277.6 0.8 copy.18
  278.4 0.0 copy-done
  278.4 0.8 copy.19
Async XLA Ops:
  274.4 3.2 %copy-start.1 = (bf16[512,512]{1,0:T(8,128)(2,1)S(1)}, bf16[512,512]{1,0:T(8,128)(2,1)}, u32[]{:S(2)}) copy-start(bf16[512,512]{1,0:T(8,128)(2,1)} %get-tuple-element.36) | copy-start | bytes 1572868
  274.4 4.0 %copy-start = (bf16[512,512]{1,0:T(8,128)(2,1)S(1)}, bf16[512,512]{1,0:T(8,128)(2,1)}, u32[]{:S(2)}) copy-start(bf16[512,512]{1,0:T(8,128)(2,1)} %get-tuple-element.37) | copy-start | bytes 1572868

commit v6 on v5

--- a/solution.py
+++ b/solution.py
@@ -199,6 +199,103 @@
 
 
 FAR_FIRST = (2, 1, 3)
+NEXT = (1, 3)
+
+
+class Gather:
+    def __init__(self, copies, source, held, slot, ring, place_in_ring, across):
+        self.copies, self.source, self.held, self.slot = copies, source, held, slot
+        self.ring, self.place, self.across = ring, place_in_ring, across
+        self.first, self.last = {}, []
+
+    def tiles(self, side, step, first=0, count=4):
+        return self.held.at[pl.ds(self.slot(side, (self.place + step) % 4) * 4 + first, count)]
+
+    def over(self):
+        mine = self.tiles(0, 0)
+        self.kept = self.copies.local(self.source, mine)
+        self.crossing = self.copies.remote(self.source, mine, self.across)
+
+    def own(self):
+        self.first[0] = [self.copies.remote(self.source, self.tiles(0, 0), self.ring(d)) for d in NEXT]
+
+    def onward(self):
+        self.crossing.wait_recv()
+        block = self.tiles(1, 0)
+        self.first[1] = [self.copies.remote(block, block, self.ring(d)) for d in NEXT]
+
+    def pass_on(self, side):
+        for copy, d in zip(self.first[side], NEXT):
+            copy.wait_recv()
+            half = self.tiles(side, -d, 0 if d == 1 else 2, 2)
+            self.last.append(self.copies.remote(half, half, self.ring(d)))
+
+    def wait(self):
+        self.kept.wait()
+        for copy in self.last:
+            copy.wait_recv()
+
+
+class Sum:
+    def __init__(self, copies, part, base, via, near, cross, crossed, ring, place_in_ring, side, across):
+        self.copies, self.part, self.base, self.via, self.near = copies, part, base, via, near
+        self.cross, self.crossed, self.ring, self.place = cross, crossed, ring, place_in_ring
+        self.side, self.across = side, across
+
+    def at(self, step, first=0):
+        return self.base + (self.place + step) % 4 * 8 + first
+
+    def far(self):
+        self.vias = []
+        for d, first in zip(NEXT, (0, 4)):
+            self.vias.append(
+                self.copies.remote(
+                    self.part.at[pl.ds(self.at(2, first), 4)], self.via.at[pl.ds(first, 4)], self.ring(d)
+                )
+            )
+
+    def hop(self):
+        self.nears = []
+        for n, (d, first) in enumerate(zip(NEXT, (0, 4))):
+            start = self.at(d, first)
+
+            def one(i, carry):
+                self.part[start + i] = (self.part[start + i].astype(F32) + self.via[first + i].astype(F32)).astype(BF16)
+                return carry
+
+            self.vias[n].wait_recv()
+            lax.fori_loop(0, 4, one, 0)
+            self.nears.append(
+                self.copies.remote(self.part.at[pl.ds(self.at(d), 8)], self.near.at[pl.ds(n * 8, 8)], self.ring(d))
+            )
+
+    def total(self, side, i):
+        total = (
+            self.part[self.at(0, side * 4 + i)].astype(F32)
+            + self.near[side * 4 + i].astype(F32)
+            + self.near[8 + side * 4 + i].astype(F32)
+        )
+        return total
+
+    def over(self):
+        for copy in self.nears:
+            copy.wait_recv()
+
+        def one(i, carry):
+            self.cross[i] = self.total(1 - self.side, i).astype(BF16)
+            return carry
+
+        lax.fori_loop(0, 4, one, 0)
+        self.crossing = self.copies.remote(self.cross, self.crossed, self.across)
+
+    def finish(self, body):
+        self.crossing.wait_recv()
+
+        def one(i, carry):
+            body(i, self.total(self.side, i) + self.crossed[i].astype(F32))
+            return carry
+
+        lax.fori_loop(0, 4, one, 0)
 
 
 def held_tile(col):
@@ -428,9 +525,9 @@
     scale, tables, node_row, own_col, hidden, own_back, s_ref, g_ref, mask_hbm,
     hidden_out, grad_out, sum_ref, mask, chain, *rest
 ):
-    held, block, traded, near, cross, crossed, (send, recv) = (
-        rest[0:4], rest[4:8], rest[8:12], rest[12:16], rest[16:20], rest[20:24], rest[24:26]
-    )
+    held, block, traded, via, near, cross, crossed = [rest[i : i + 4] for i in range(0, 28, 4)]
+    send, recv = rest[28:30]
+    rest = rest[4:]
     g_core, g_traded, g_half, g_quarter, g_part, g_eighth, g_piece = rest[26:33]
     xl, y, xh, z, k = place()
     copies = Copies(send, recv)
@@ -443,27 +540,23 @@
     pick_slots(unpacking, own_col)
     hidden_relay.pack(packing, hidden, 0)
     meet()
-    tiles = lambda slot: pl.ds(slot * 4, 4)
-    mine, pair = xl * 4 + y, (1 - xl) * 4 + y
-    gathered, over, trade, col_copies, cross_copy = [[] for _ in range(4)], {}, {}, {}, {}
-
-    def own(c):
-        gathered[c].append(copies.local(s_ref.at[c], held[c].at[tiles(mine)]))
-        over[c] = copies.remote(s_ref.at[c], held[c].at[tiles(mine)], at_device(1 - xl, y, xh, z, k))
-        for d in FAR_FIRST:
-            to = at_device(xl, (y + d) % 4, xh, z, k)
-            gathered[c].append(copies.remote(s_ref.at[c], held[c].at[tiles(mine)], to))
-
-    def onward(c):
-        over[c].wait_recv()
-        for d in FAR_FIRST:
-            to = at_device(xl, (y + d) % 4, xh, z, k)
-            gathered[c].append(copies.remote(held[c].at[tiles(pair)], held[c].at[tiles(pair)], to))
-
-    def product(c, between):
-        gathered[c][0].wait()
-        for copy in gathered[c][1:]:
-            copy.wait_recv()
+    ring_z = lambda d: at_device(xl, y, xh, (z + d) % 4, k)
+    ring_y = lambda d: at_device(xl, (y + d) % 4, xh, z, k)
+    slot = lambda side, at: (xl + side) % 2 * 4 + at
+    gather = [
+        Gather(copies, s_ref.at[c], held[c], slot, ring_y, y, at_device(1 - xl, y, xh, z, k)) for c in range(4)
+    ]
+    cols = [
+        Sum(
+            copies, block[c], k * 32, via[c], near[c], cross[c], crossed[c], ring_z, z, xh,
+            at_device(xl, y, 1 - xh, z, k),
+        )
+        for c in range(4)
+    ]
+    trade = {}
+
+    def product(c, *between):
+        gather[c].wait()
 
         def one(g, total):
             for u in range(8):
@@ -473,9 +566,11 @@
                 chain[e] = total.astype(BF16)
             return total
 
-        half = lax.fori_loop(0, 16, one, jnp.zeros((128, 128), F32))
-        between()
-        lax.fori_loop(16, 32, one, half)
+        total = jnp.zeros((128, 128), F32)
+        for n in range(4):
+            total = lax.fori_loop(n * 8, n * 8 + 8, one, total)
+            for action in between[n : n + 1]:
+                action()
 
         def settle(p, carry):
             block[c][p] = (chain[tables[3, p]].astype(F32) * tables[4, p].astype(F32)).astype(BF16)
@@ -494,42 +589,14 @@
             return carry
 
         lax.fori_loop(0, 32, one, 0)
-        col_copies[c] = []
-        for i, d in enumerate(FAR_FIRST):
-            to_z = (z + d) % 4
-            col_copies[c].append(
-                copies.remote(
-                    block[c].at[pl.ds(k * 32 + to_z * 8, 8)], near[c].at[pl.ds(i * 8, 8)], at_device(xl, y, xh, to_z, k)
-                )
-            )
-
-    def col_sum(c, side, i):
-        total = block[c][k * 32 + z * 8 + side * 4 + i].astype(F32)
-        for n in range(3):
-            total = total + near[c][n * 8 + side * 4 + i].astype(F32)
-        return total
-
-    def sum_cols(c):
-        for copy in col_copies[c]:
-            copy.wait_recv()
-
-        def one(i, carry):
-            cross[c][i] = col_sum(c, 1 - xh, i).astype(BF16)
-            return carry
-
-        lax.fori_loop(0, 4, one, 0)
-        cross_copy[c] = copies.remote(cross[c], crossed[c], at_device(xl, y, 1 - xh, z, k))
-
-    def sum_cross(c):
-        cross_copy[c].wait_recv()
-
-        def one(i, carry):
-            back = col_sum(c, xh, i) + crossed[c][i].astype(F32)
+        cols[c].far()
+
+    def finish(c):
+        def body(i, total):
             at = (pl.ds(pl.multiple_of(i * 128, 128), 128), pl.ds(c * 128, 128))
-            joined[at] = (own_back[at] + back.T).astype(BF16)
-            return carry
-
-        lax.fori_loop(0, 4, one, 0)
+            joined[at] = (own_back[at] + total.T).astype(BF16)
+
+        cols[c].finish(body)
 
     width = g_ref.shape[1]
     quarter_at = k * 512 + z * 128
@@ -635,46 +702,69 @@
 
         each_block(4, one)
 
-    def send_first():
-        sum_cross(1)
-        relays[0].pack(packing, joined, 0)
-        relays[0].start()
-
-    own(0)
+    def send(relay, first):
+        relay.pack(packing, joined, first)
+        relay.start()
+
+    def steps(*actions):
+        def run():
+            for action in actions:
+                action()
+
+        return run
+
+    def passing(c, side):
+        return lambda: gather[c].pass_on(side)
+
+    def paired(c):
+        return lambda: sum_cores(c)
+
+    for c in range(4):
+        gather[c].over()
+    gather[0].own()
     grad_core()
-    onward(0)
-    own(1)
-    onward(1)
+    gather[0].onward()
+    gather[0].pass_on(0)
+    gather[0].pass_on(1)
+    gather[1].own()
+    gather[1].onward()
     grad_z()
-    own(2)
     mask_copy.wait()
-    product(0, grad_y)
-    onward(2)
-    own(3)
-    sum_cores(0)
-    grad_x()
-    product(1, grad_total)
-    onward(3)
-    hidden_relay.start()
-    sum_cores(1)
-    grad_to_z()
-    sum_cols(0)
-    product(2, grad_to_y)
-    sum_cores(2)
-    sum_cols(1)
+    product(
+        0,
+        passing(1, 0),
+        steps(passing(1, 1), gather[2].own),
+        steps(gather[2].onward, grad_y),
+    )
+    product(
+        1,
+        steps(paired(0), passing(2, 0)),
+        steps(passing(2, 1), gather[3].own, gather[3].onward),
+        steps(cols[0].hop, grad_x),
+    )
+    product(
+        2,
+        steps(paired(1), passing(3, 0)),
+        steps(passing(3, 1), cols[0].over, hidden_relay.start),
+        steps(cols[1].hop, grad_total),
+    )
+    product(
+        3,
+        steps(paired(2), lambda: finish(0)),
+        steps(cols[1].over, grad_to_z),
+        steps(cols[2].hop, lambda: finish(1), lambda: send(relays[0], 0)),
+    )
+    sum_cores(3)
+    grad_to_y()
+    cols[2].over()
+    cols[3].hop()
+    take(hidden_relay, hidden_out, 0)
+    finish(2)
+    send(relays[1], 256)
+    cols[3].over()
     grad_to_core()
-    sum_cross(0)
-    product(3, send_first)
-    sum_cores(3)
-    sum_cols(2)
-    take(hidden_relay, hidden_out, 0)
-    sum_cross(2)
-    relays[1].pack(packing, joined, 256)
-    relays[1].start()
-    sum_cols(3)
-    sum_cross(3)
-    relays[2].pack(packing, joined, 384)
-    relays[2].start()
+    finish(3)
+    send(relays[2], 384)
     take(relays[0], grad_out, 0)
     take(relays[1], grad_out, 256)
     take(relays[2], grad_out, 384)
@@ -700,9 +790,10 @@
         + [tile_buffer(32)] * 4
         + [tile_buffer(64)] * 4
         + [tile_buffer(32)] * 4
-        + [tile_buffer(24)] * 4
+        + [tile_buffer(8)] * 4
+        + [tile_buffer(16)] * 4
         + [tile_buffer(4)] * 8
-        + [pltpu.SemaphoreType.DMA((96,)), pltpu.SemaphoreType.DMA((96,))]
+        + [pltpu.SemaphoreType.DMA((128,)), pltpu.SemaphoreType.DMA((128,))]
         + [pltpu.VMEM((512, 512), BF16)] * 3
         + [pltpu.VMEM((3, 128, 512), BF16), pltpu.VMEM((1, 128, 512), F32)]
         + [pltpu.VMEM((3, 32, 512), F32), pltpu.VMEM((2, 32, 512), F32)]
@@ -721,10 +812,12 @@
 ):
     step = pl.program_id(0)
     width = hidden_ref.shape[1]
-    x = jnp.concatenate([x_ref[c, 0] for c in range(4)], axis=1)
+    parts = x_ref.shape[1]
+    whole = lambda ref: jnp.concatenate([ref[c].reshape(parts * 128, 128) for c in range(4)], axis=1)
+    x = whole(x_ref)
     degrees = extra_ref[:, pl.ds(width, 1)].astype(F32)
     cot = extra_ref[:, pl.ds(0, width)].astype(F32)
-    summed = jnp.concatenate([sum_ref[c, 0] for c in range(4)], axis=1)
+    summed = whole(sum_ref)
     aggregate = (summed / degrees).astype(BF16)
     preact = jnp.dot(x, ws_ref[...], preferred_element_type=F32) + jnp.dot(
         aggregate, wn_ref[...], preferred_element_type=F32
@@ -748,15 +841,16 @@
     own_ref[...] = lax.dot_general(slopes, ws_ref[...], COL_T, preferred_element_type=F32)
     spread = lax.dot_general(slopes, wn_ref[...], COL_T, preferred_element_type=F32) / degrees
     for c in range(4):
-        spread_ref[c, 0] = spread[:, c * 128 : (c + 1) * 128].T.astype(BF16)
+        for i in range(parts):
+            spread_ref[c, i] = spread[i * 128 : (i + 1) * 128, c * 128 : (c + 1) * 128].T.astype(BF16)
 
 
 def dense(summed, x, extra, ws, wn):
     rows, width = extra.shape[0], ws.shape[0]
-    step = 128
+    step = 256
     whole = lambda i: (0, 0)
     rowwise = lambda i: (i, 0)
-    tiled = pl.BlockSpec((4, 1, step, 128), lambda i: (0, i, 0, 0))
+    tiled = pl.BlockSpec((4, step // 128, 128, 128), lambda i: (0, i, 0, 0))
     return pl.pallas_call(
         dense_kernel,
         grid=(rows // step,),

time: 279 us -> 254 us (0.910)
  Pallas kernels: 272 us -> 246 us
    pallas_call x1, Pallas kernels: 149 us -> 126 us  [backward_exchange(): pl.pallas_call(functools.partial(backward_kernel, scale), in_specs=[SMEM_...]
where the time goes in v6:
time: 254 us; the launch traced here: 253 us
  Pallas kernels  246 us (97%)
  local copies, waits for them, and re-layouts  6.88 us (3%)
    pallas_call x1, Pallas kernels, backward_exchange(): pl.pallas_call(functools.partial(backward_kernel, scale), in_specs=[SMEM_...  126 us
    pallas_call x1, Pallas kernels, forward_exchange(): pl.pallas_call(forward_kernel, in_specs=[SMEM_SPEC] + [VMEM_SPEC] * 6 + [...  114 us
    pallas_call x1, Pallas kernels, dense(): pl.pallas_call(dense_kernel, grid=(rows // step,), in_specs=[tiled, tiled...  6.57 us

profile of v6, /device:TPU:1, one launch (start us, length us, event | category | flops | bytes accessed | tf_op | source)
XLA Modules:
  0.0 253.5 jit_solution(15029788077579001596)
XLA Ops:
  0.6 0.8 copy.14
  1.4 0.7 reshape_reshape.3.cols_row
  2.0 0.7 reshape.28.cols_ref
  2.7 113.7 %forward_exchange.1 = (f32[4,4,128,128]{3,2,1,0:T(8,128)}, bf16[4,4,128,128]{3,2,1,0:T(8,128)(2,1)}, bf16[512,640]{1,0:T(8,128)(2,1)}, s32[512,1]{1,0:T(8,128)}, s32[1,512]{1,0:T(1,128)}, /*index=5*/s32[8,256]{1,0:T(8,128)}) custom-call(s32[256]{0:T(256)} %reshape.28.cols_ref, s32[1,256]{1,0:T(1,128)} %reshape_reshape.3.cols_row, s32[1,512]{1,0:T(1,128)} %bitcast.14, ...), custom_call_target="tpu_custom_call" | custom-call | tf_op jit(solution)/shard_map/forward_exchange/pallas_call | solution.py:496
  116.4 6.6 %dense.1 = (bf16[512,512]{1,0:T(8,128)(2,1)}, f32[512,512]{1,0:T(8,128)}, bf16[4,4,128,128]{3,2,1,0:T(8,128)(2,1)}, f32[1024,512]{1,0:T(8,128)}) custom-call(f32[4,4,128,128]{3,2,1,0:T(8,128)} %get-tuple-element.20.sum_ref, bf16[4,4,128,128]{3,2,1,0:T(8,128)(2,1)} %get-tuple-element.21.x_ref, bf16[512,640]{1,0:T(8,128)(2,1)} %get-tuple-element.22.extra_ref, ...), custom_call_target="tpu_custom_call" | custom-call | tf_op jit(solution)/shard_map/dense/pallas_call | solution.py:854
  123.0 125.7 %backward_exchange.1 = (bf16[512,512]{1,0:T(8,128)(2,1)}, bf16[512,512]{1,0:T(8,128)(2,1)}, f32[2,4,4,32,512]{4,3,2,1,0:T(8,128)}) custom-call(s32[8,256]{1,0:T(8,128)} %get-tuple-element.17.tables, s32[1,512]{1,0:T(1,128)} %get-tuple-element.18.node_row, s32[512,1]{1,0:T(8,128)} %get-tuple-element.19.own_col, bf16[512,512]{1,0:T(8,128)(2,1)} %get-tuple-element.23.hidden, ...), custom_call_target="tpu_custom_call" | custom-call | tf_op jit(solution)/shard_map/backward_exchange/pallas_call | solution.py:780
  248.7 0.0 copy-start.1
  248.7 0.0 copy-start
  248.7 3.2 %fusion = (f32[1,4,4,32,512]{4,3,2,1,0:T(8,128)}, f32[1,4,4,32,512]{4,3,2,1,0:T(8,128)}) fusion(f32[2,4,4,32,512]{4,3,2,1,0:T(8,128)} %get-tuple-element.29), kind=kLoop, calls=%fused_computation | loop fusion | bytes 4194304 | tf_op jit(solution)/shard_map/slice | solution.py:895
  251.9 0.0 copy-done.1
  251.9 0.8 copy.18
  252.7 0.0 copy-done
  252.7 0.8 copy.19
Async XLA Ops:
  248.7 3.2 %copy-start.1 = (bf16[512,512]{1,0:T(8,128)(2,1)S(1)}, bf16[512,512]{1,0:T(8,128)(2,1)}, u32[]{:S(2)}) copy-start(bf16[512,512]{1,0:T(8,128)(2,1)} %get-tuple-element.36) | copy-start | bytes 1572868
  248.7 4.0 %copy-start = (bf16[512,512]{1,0:T(8,128)(2,1)S(1)}, bf16[512,512]{1,0:T(8,128)(2,1)}, u32[]{:S(2)}) copy-start(bf16[512,512]{1,0:T(8,128)(2,1)} %get-tuple-element.37) | copy-start | bytes 1572868

commit v7 on v6

--- a/solution.py
+++ b/solution.py
@@ -522,8 +522,8 @@
 
 
 def backward_kernel(
-    scale, tables, node_row, own_col, hidden, own_back, s_ref, g_ref, mask_hbm,
-    hidden_out, grad_out, sum_ref, mask, chain, *rest
+    scale, tables, node_row, own_col, summed, x_ref, extra, self_weight, neigh_weight, mask_hbm,
+    hidden_out, grad_out, sum_ref, mask, chain, hidden, own_back, s_ref, g_ref, slopes, aggregate, *rest
 ):
     held, block, traded, via, near, cross, crossed = [rest[i : i + 4] for i in range(0, 28, 4)]
     send, recv = rest[28:30]
@@ -536,9 +536,38 @@
     hidden_relay = Relay(rest[37], rest[38], rest[39])
     relays = [Relay(rest[i], rest[i + 1], rest[i + 2]) for i in (40, 43, 46)]
     greet()
-    pick_rows(packing, node_row[...])
-    pick_slots(unpacking, own_col)
-    hidden_relay.pack(packing, hidden, 0)
+    each_big = lambda body: lax.fori_loop(0, 2, lambda i, carry: body(i, pl.ds(pl.multiple_of(i * 256, 256), 256)), 0)
+
+    def dense_front(i, at):
+        whole = lambda ref: jnp.concatenate([ref[c, pl.ds(i * 2, 2)].reshape(256, 128) for c in range(4)], axis=1)
+        degrees = extra[at, pl.ds(512, 1)].astype(F32)
+        mean = (whole(summed) / degrees).astype(BF16)
+        aggregate[at] = mean
+        preact = jnp.dot(whole(x_ref), self_weight[...], preferred_element_type=F32) + jnp.dot(
+            mean, neigh_weight[...], preferred_element_type=F32
+        )
+        gate = jax.nn.sigmoid(preact)
+        hidden[at] = (preact * gate).astype(BF16)
+        slope = (extra[at, pl.ds(0, 512)].astype(F32) * gate * (1.0 + preact * (1.0 - gate))).astype(BF16)
+        slopes[at] = slope
+        spread = lax.dot_general(slope, neigh_weight[...], COL_T, preferred_element_type=F32) / degrees
+        for c in range(4):
+            for n in range(2):
+                s_ref[c, i * 2 + n] = spread[n * 128 : (n + 1) * 128, c * 128 : (c + 1) * 128].T.astype(BF16)
+        return 0
+
+    def dense_own(i, at):
+        own_back[at] = lax.dot_general(slopes[at], self_weight[...], COL_T, preferred_element_type=F32)
+        return 0
+
+    def dense_grads(c, at):
+        columns = x_ref[c].reshape(512, 128)
+        g_ref[at] = lax.dot_general(columns, slopes[...], ROW_T, preferred_element_type=F32)
+        means = aggregate[:, pl.ds(pl.multiple_of(c * 128, 128), 128)]
+        below = pl.ds(pl.multiple_of(512 + c * 128, 128), 128)
+        g_ref[below] = lax.dot_general(means, slopes[...], ROW_T, preferred_element_type=F32)
+
+    each_big(dense_front)
     meet()
     ring_z = lambda d: at_device(xl, y, xh, (z + d) % 4, k)
     ring_y = lambda d: at_device(xl, (y + d) % 4, xh, z, k)
@@ -722,23 +751,27 @@
     for c in range(4):
         gather[c].over()
     gather[0].own()
-    grad_core()
+    pick_rows(packing, node_row[...])
     gather[0].onward()
+    hidden_relay.pack(packing, hidden, 0)
     gather[0].pass_on(0)
     gather[0].pass_on(1)
     gather[1].own()
     gather[1].onward()
-    grad_z()
+    each_block(4, dense_grads)
+    grad_core()
+    each_big(dense_own)
+    pick_slots(unpacking, own_col)
     mask_copy.wait()
     product(
         0,
-        passing(1, 0),
+        steps(passing(1, 0), grad_z),
         steps(passing(1, 1), gather[2].own),
-        steps(gather[2].onward, grad_y),
+        gather[2].onward,
     )
     product(
         1,
-        steps(paired(0), passing(2, 0)),
+        steps(paired(0), passing(2, 0), grad_y),
         steps(passing(2, 1), gather[3].own, gather[3].onward),
         steps(cols[0].hop, grad_x),
     )
@@ -774,12 +807,12 @@
         relay.finish()
 
 
-def backward_exchange(tables, node_row, own_col, hidden, own_back, s, grads, masks, scale):
-    rows, width = hidden.shape
+def backward_exchange(tables, node_row, own_col, summed, x, extra, self_weight, neigh_weight, masks, scale):
+    rows, width = extra.shape[0], self_weight.shape[0]
     slots = DEVICES * 8
     return pl.pallas_call(
         functools.partial(backward_kernel, scale),
-        in_specs=[SMEM_SPEC] + [VMEM_SPEC] * 6 + [ANY_SPEC],
+        in_specs=[SMEM_SPEC] + [VMEM_SPEC] * 7 + [ANY_SPEC],
         out_specs=[VMEM_SPEC] * 3,
         out_shape=[
             jax.ShapeDtypeStruct((rows, width), BF16),
@@ -787,6 +820,8 @@
             jax.ShapeDtypeStruct((2, 4, 4, 32, width), F32),
         ],
         scratch_shapes=[tile_buffer(256), tile_buffer(256)]
+        + [pltpu.VMEM((rows, width), BF16), pltpu.VMEM((rows, width), F32), pltpu.VMEM(x.shape, BF16)]
+        + [pltpu.VMEM((2 * rows, width), F32), pltpu.VMEM((rows, width), BF16), pltpu.VMEM((rows, width), BF16)]
         + [tile_buffer(32)] * 4
         + [tile_buffer(64)] * 4
         + [tile_buffer(32)] * 4
@@ -804,78 +839,7 @@
         + boxes(width // 4) * 2,
         compiler_params=remote_params(1),
         name="backward_exchange",
-    )(tables, node_row, own_col, hidden, own_back, s, grads, masks)
-
-
-def dense_kernel(
-    sum_ref, x_ref, extra_ref, ws_ref, wn_ref, hidden_ref, own_ref, spread_ref, grads_ref
-):
-    step = pl.program_id(0)
-    width = hidden_ref.shape[1]
-    parts = x_ref.shape[1]
-    whole = lambda ref: jnp.concatenate([ref[c].reshape(parts * 128, 128) for c in range(4)], axis=1)
-    x = whole(x_ref)
-    degrees = extra_ref[:, pl.ds(width, 1)].astype(F32)
-    cot = extra_ref[:, pl.ds(0, width)].astype(F32)
-    summed = whole(sum_ref)
-    aggregate = (summed / degrees).astype(BF16)
-    preact = jnp.dot(x, ws_ref[...], preferred_element_type=F32) + jnp.dot(
-        aggregate, wn_ref[...], preferred_element_type=F32
-    )
-    gate = jax.nn.sigmoid(preact)
-    hidden_ref[...] = (preact * gate).astype(BF16)
-    slopes = (cot * gate * (1.0 + preact * (1.0 - gate))).astype(BF16)
-    gs = lax.dot_general(x, slopes, ROW_T, preferred_element_type=F32)
-    gn = lax.dot_general(aggregate, slopes, ROW_T, preferred_element_type=F32)
-
-    @pl.when(step == 0)
-    def _():
-        grads_ref[pl.ds(0, width)] = gs
-        grads_ref[pl.ds(width, width)] = gn
-
-    @pl.when(step > 0)
-    def _():
-        grads_ref[pl.ds(0, width)] += gs
-        grads_ref[pl.ds(width, width)] += gn
-
-    own_ref[...] = lax.dot_general(slopes, ws_ref[...], COL_T, preferred_element_type=F32)
-    spread = lax.dot_general(slopes, wn_ref[...], COL_T, preferred_element_type=F32) / degrees
-    for c in range(4):
-        for i in range(parts):
-            spread_ref[c, i] = spread[i * 128 : (i + 1) * 128, c * 128 : (c + 1) * 128].T.astype(BF16)
-
-
-def dense(summed, x, extra, ws, wn):
-    rows, width = extra.shape[0], ws.shape[0]
-    step = 256
-    whole = lambda i: (0, 0)
-    rowwise = lambda i: (i, 0)
-    tiled = pl.BlockSpec((4, step // 128, 128, 128), lambda i: (0, i, 0, 0))
-    return pl.pallas_call(
-        dense_kernel,
-        grid=(rows // step,),
-        in_specs=[
-            tiled,
-            tiled,
-            pl.BlockSpec((step, extra.shape[1]), rowwise),
-            pl.BlockSpec((width, width), whole),
-            pl.BlockSpec((width, width), whole),
-        ],
-        out_specs=[
-            pl.BlockSpec((step, width), rowwise),
-            pl.BlockSpec((step, width), rowwise),
-            tiled,
-            pl.BlockSpec((2 * width, width), whole),
-        ],
-        out_shape=[
-            jax.ShapeDtypeStruct((rows, width), BF16),
-            jax.ShapeDtypeStruct((rows, width), F32),
-            jax.ShapeDtypeStruct(x.shape, BF16),
-            jax.ShapeDtypeStruct((2 * width, width), F32),
-        ],
-        compiler_params=params(),
-        name="dense",
-    )(summed, x, extra, ws, wn)
+    )(tables, node_row, own_col, summed, x, extra, self_weight, neigh_weight, masks)
 
 
 def on_device(
@@ -886,10 +850,9 @@
     summed, node_x, node_extra, own_col, node_row, tables = forward_exchange(
         tile_cols.reshape(-1), owner_nodes, owner_position, degree, features, cotangent, masks
     )
-    hidden, own_back, spread, grads = dense(summed, node_x, node_extra, self_weight, neigh_weight)
     grad_scale = 1.0 / math.sqrt(rows * DEVICES)
     hidden_out, grad_out, sums = backward_exchange(
-        tables, node_row, own_col, hidden, own_back, spread, grads, masks, grad_scale
+        tables, node_row, own_col, summed, node_x, node_extra, self_weight, neigh_weight, masks, grad_scale
     )
     sums = sums.reshape(2, width, width)
     return hidden_out, grad_out, sums[0], sums[1]

time: 254 us -> 247 us (0.972)
  Pallas kernels: 246 us -> 240 us
    pallas_call x1 -> x0, Pallas kernels: 6.57 us -> none  [dense(): pl.pallas_call(dense_kernel, grid=(rows // step,), in_specs=[tiled, tiled...]
where the time goes in v7:
time: 247 us
  Pallas kernels  240 us (97%)
  local copies, waits for them, and re-layouts  6.88 us (3%)
    pallas_call x1, Pallas kernels, backward_exchange(): pl.pallas_call(functools.partial(backward_kernel, scale), in_specs=[SMEM_...  126 us
    pallas_call x1, Pallas kernels, forward_exchange(): pl.pallas_call(forward_kernel, in_specs=[SMEM_SPEC] + [VMEM_SPEC] * 6 + [...  114 us

profile of v7, /device:TPU:1, one launch (start us, length us, event | category | flops | bytes accessed | tf_op | source)
XLA Modules:
  0.0 247.2 jit_solution(8821578389030285153)
XLA Ops:
  0.6 0.8 copy.14
  1.4 0.7 reshape_reshape.3.cols_row
  2.0 0.7 reshape.28.cols_ref
  2.7 113.7 %forward_exchange.1 = (f32[4,4,128,128]{3,2,1,0:T(8,128)}, bf16[4,4,128,128]{3,2,1,0:T(8,128)(2,1)}, bf16[512,640]{1,0:T(8,128)(2,1)}, s32[512,1]{1,0:T(8,128)}, s32[1,512]{1,0:T(1,128)}, /*index=5*/s32[8,256]{1,0:T(8,128)}) custom-call(s32[256]{0:T(256)} %reshape.28.cols_ref, s32[1,256]{1,0:T(1,128)} %reshape_reshape.3.cols_row, s32[1,512]{1,0:T(1,128)} %bitcast.14, ...), custom_call_target="tpu_custom_call" | custom-call | tf_op jit(solution)/shard_map/forward_exchange/pallas_call | solution.py:496
  116.4 125.9 %backward_exchange.1 = (bf16[512,512]{1,0:T(8,128)(2,1)}, bf16[512,512]{1,0:T(8,128)(2,1)}, f32[2,4,4,32,512]{4,3,2,1,0:T(8,128)}) custom-call(s32[8,256]{1,0:T(8,128)} %get-tuple-element.13.tables, s32[1,512]{1,0:T(1,128)} %get-tuple-element.14.node_row, s32[512,1]{1,0:T(8,128)} %get-tuple-element.15.own_col, f32[4,4,128,128]{3,2,1,0:T(8,128)} %get-tuple-element.16.summed, ...), custom_call_target="tpu_custom_call" | custom-call | tf_op jit(solution)/shard_map/backward_exchange/pallas_call | solution.py:813
  242.3 0.0 copy-start.1
  242.3 0.0 copy-start
  242.4 3.2 %fusion = (f32[1,4,4,32,512]{4,3,2,1,0:T(8,128)}, f32[1,4,4,32,512]{4,3,2,1,0:T(8,128)}) fusion(f32[2,4,4,32,512]{4,3,2,1,0:T(8,128)} %get-tuple-element.21), kind=kLoop, calls=%fused_computation | loop fusion | bytes 4194304 | tf_op jit(solution)/shard_map/slice | solution.py:858
  245.6 0.0 copy-done.1
  245.6 0.8 copy.18
  246.4 0.0 copy-done
  246.4 0.8 copy.19
Async XLA Ops:
  242.3 3.2 %copy-start.1 = (bf16[512,512]{1,0:T(8,128)(2,1)S(1)}, bf16[512,512]{1,0:T(8,128)(2,1)}, u32[]{:S(2)}) copy-start(bf16[512,512]{1,0:T(8,128)(2,1)} %get-tuple-element.28) | copy-start | bytes 1572868
  242.3 4.0 %copy-start = (bf16[512,512]{1,0:T(8,128)(2,1)S(1)}, bf16[512,512]{1,0:T(8,128)(2,1)}, u32[]{:S(2)}) copy-start(bf16[512,512]{1,0:T(8,128)(2,1)} %get-tuple-element.29) | copy-start | bytes 1572868

commit v8 on v7

--- a/solution.py
+++ b/solution.py
@@ -10,6 +10,7 @@
 
 F32 = jnp.float32
 DEVICES = 128
+UNROLL = 8
 BF16 = jnp.bfloat16
 MESH = pl.DeviceIdType.MESH
 VMEM_LIMIT = 60 * 1024 * 1024
@@ -34,15 +35,27 @@
     return lax.axis_index("row") * 16 + lax.axis_index("col")
 
 
+def each_peer(me, body):
+    def some(first, count):
+        for step in range(count):
+            peer = lax.rem(me + first + step, DEVICES)
+            body(peer, lax.div(peer, 16), lax.rem(peer, 16))
+
+    def one(i, carry):
+        some(i * UNROLL, UNROLL)
+        return carry
+
+    some(1, UNROLL - 1)
+    lax.fori_loop(1, DEVICES // UNROLL, one, 0)
+
+
 def greet():
     barrier, me = pltpu.get_barrier_semaphore(), device_number()
 
-    def one(step, carry):
-        peer = (me + step) % DEVICES
-        pl.semaphore_signal(barrier, inc=1, device_id=(peer // 16, peer % 16), device_id_type=MESH)
-        return carry
-
-    lax.fori_loop(1, DEVICES, one, 0)
+    def one(peer, row, col):
+        pl.semaphore_signal(barrier, inc=1, device_id=(row, col), device_id_type=MESH)
+
+    each_peer(me, one)
 
 
 def meet():
@@ -82,15 +95,13 @@
         me = device_number()
         self.kept().start()
 
-        def one(step, carry):
-            peer = (me + step) % DEVICES
+        def one(peer, row, col):
             pltpu.make_async_remote_copy(
                 src_ref=self.outbox.at[peer], dst_ref=self.inbox.at[me], send_sem=self.sems.at[0],
-                recv_sem=self.sems.at[1], device_id=(peer // 16, peer % 16), device_id_type=MESH,
+                recv_sem=self.sems.at[1], device_id=(row, col), device_id_type=MESH,
             ).start()
-            return carry
-
-        lax.fori_loop(1, DEVICES, one, 0)
+
+        each_peer(me, one)
 
     def collect(self, flat):
         self.kept().wait()

time: 247 us -> 242 us (0.980)
  Pallas kernels: 240 us -> 234 us
    pallas_call x1, Pallas kernels: 126 us -> 122 us  [backward_exchange(): pl.pallas_call(functools.partial(backward_kernel, scale), in_specs=[SMEM_...]
where the time goes in v8:
time: 242 us
  Pallas kernels  234 us (97%)
  local copies, waits for them, and re-layouts  6.88 us (3%)
    pallas_call x1, Pallas kernels, backward_exchange(): pl.pallas_call(functools.partial(backward_kernel, scale), in_specs=[SMEM_...  122 us
    pallas_call x1, Pallas kernels, forward_exchange(): pl.pallas_call(forward_kernel, in_specs=[SMEM_SPEC] + [VMEM_SPEC] * 6 + [...  113 us

profile of v8, /device:TPU:1, one launch (start us, length us, event | category | flops | bytes accessed | tf_op | source)
XLA Modules:
  0.0 242.0 jit_solution(12472447905318969209)
XLA Ops:
  0.6 0.8 copy.14
  1.4 0.7 reshape_reshape.3.cols_row
  2.0 0.7 reshape.28.cols_ref
  2.7 112.9 %forward_exchange.1 = (f32[4,4,128,128]{3,2,1,0:T(8,128)}, bf16[4,4,128,128]{3,2,1,0:T(8,128)(2,1)}, bf16[512,640]{1,0:T(8,128)(2,1)}, s32[512,1]{1,0:T(8,128)}, s32[1,512]{1,0:T(1,128)}, /*index=5*/s32[8,256]{1,0:T(8,128)}) custom-call(s32[256]{0:T(256)} %reshape.28.cols_ref, s32[1,256]{1,0:T(1,128)} %reshape_reshape.3.cols_row, s32[1,512]{1,0:T(1,128)} %bitcast.14, ...), custom_call_target="tpu_custom_call" | custom-call | tf_op jit(solution)/shard_map/forward_exchange/pallas_call | solution.py:507
  115.6 121.6 %backward_exchange.1 = (bf16[512,512]{1,0:T(8,128)(2,1)}, bf16[512,512]{1,0:T(8,128)(2,1)}, f32[2,4,4,32,512]{4,3,2,1,0:T(8,128)}) custom-call(s32[8,256]{1,0:T(8,128)} %get-tuple-element.13.tables, s32[1,512]{1,0:T(1,128)} %get-tuple-element.14.node_row, s32[512,1]{1,0:T(8,128)} %get-tuple-element.15.own_col, f32[4,4,128,128]{3,2,1,0:T(8,128)} %get-tuple-element.16.summed, ...), custom_call_target="tpu_custom_call" | custom-call | tf_op jit(solution)/shard_map/backward_exchange/pallas_call | solution.py:824
  237.2 0.0 copy-start.1
  237.2 0.0 copy-start
  237.2 3.2 %fusion = (f32[1,4,4,32,512]{4,3,2,1,0:T(8,128)}, f32[1,4,4,32,512]{4,3,2,1,0:T(8,128)}) fusion(f32[2,4,4,32,512]{4,3,2,1,0:T(8,128)} %get-tuple-element.21), kind=kLoop, calls=%fused_computation | loop fusion | bytes 4194304 | tf_op jit(solution)/shard_map/slice | solution.py:869
  240.4 0.0 copy-done.1
  240.4 0.8 copy.18
  241.2 0.0 copy-done
  241.2 0.8 copy.19
Async XLA Ops:
  237.2 3.2 %copy-start.1 = (bf16[512,512]{1,0:T(8,128)(2,1)S(1)}, bf16[512,512]{1,0:T(8,128)(2,1)}, u32[]{:S(2)}) copy-start(bf16[512,512]{1,0:T(8,128)(2,1)} %get-tuple-element.28) | copy-start | bytes 1572868
  237.2 4.0 %copy-start = (bf16[512,512]{1,0:T(8,128)(2,1)S(1)}, bf16[512,512]{1,0:T(8,128)(2,1)}, u32[]{:S(2)}) copy-start(bf16[512,512]{1,0:T(8,128)(2,1)} %get-tuple-element.29) | copy-start | bytes 1572868

commit v9 on v8

--- a/solution.py
+++ b/solution.py
@@ -11,6 +11,7 @@
 F32 = jnp.float32
 DEVICES = 128
 UNROLL = 8
+STRIDE = 53
 BF16 = jnp.bfloat16
 MESH = pl.DeviceIdType.MESH
 VMEM_LIMIT = 60 * 1024 * 1024
@@ -38,7 +39,7 @@
 def each_peer(me, body):
     def some(first, count):
         for step in range(count):
-            peer = lax.rem(me + first + step, DEVICES)
+            peer = lax.rem(me + (first + step) * STRIDE, DEVICES)
             body(peer, lax.div(peer, 16), lax.rem(peer, 16))
 
     def one(i, carry):
@@ -545,7 +546,7 @@
     mask_copy = copies.local(mask_hbm, mask)
     packing, unpacking, flat, joined = rest[33:37]
     hidden_relay = Relay(rest[37], rest[38], rest[39])
-    relays = [Relay(rest[i], rest[i + 1], rest[i + 2]) for i in (40, 43, 46)]
+    relays = [Relay(rest[i], rest[i + 1], rest[i + 2]) for i in (40, 43)]
     greet()
     each_big = lambda body: lax.fori_loop(0, 2, lambda i, carry: body(i, pl.ds(pl.multiple_of(i * 256, 256), 256)), 0)
 
@@ -804,14 +805,12 @@
     cols[3].hop()
     take(hidden_relay, hidden_out, 0)
     finish(2)
-    send(relays[1], 256)
     cols[3].over()
     grad_to_core()
     finish(3)
-    send(relays[2], 384)
+    send(relays[1], 256)
     take(relays[0], grad_out, 0)
     take(relays[1], grad_out, 256)
-    take(relays[2], grad_out, 384)
     level["to_core"].wait_recv()
     copies.finish()
     for relay in relays + [hidden_relay]:
@@ -846,8 +845,7 @@
         + [pltpu.VMEM((slots, rows), BF16), pltpu.VMEM((rows, slots), BF16)]
         + [pltpu.VMEM((slots, width), BF16), pltpu.VMEM((rows, width), BF16)]
         + boxes(width)
-        + boxes(width // 2)
-        + boxes(width // 4) * 2,
+        + boxes(width // 2) * 2,
         compiler_params=remote_params(1),
         name="backward_exchange",
     )(tables, node_row, own_col, summed, x, extra, self_weight, neigh_weight, masks)

time: 242 us -> 240 us (level)
  Pallas kernels: 234 us -> 231 us
where the time goes in v9:
time: 240 us; the launch traced here: 239 us
  Pallas kernels  231 us (96%)
  local copies, waits for them, and re-layouts  6.88 us (3%)
    pallas_call x1, Pallas kernels, backward_exchange(): pl.pallas_call(functools.partial(backward_kernel, scale), in_specs=[SMEM_...  120 us
    pallas_call x1, Pallas kernels, forward_exchange(): pl.pallas_call(forward_kernel, in_specs=[SMEM_SPEC] + [VMEM_SPEC] * 6 + [...  111 us

profile of v9, /device:TPU:1, one launch (start us, length us, event | category | flops | bytes accessed | tf_op | source)
XLA Modules:
  0.0 239.0 jit_solution(2654185244558749386)
XLA Ops:
  0.6 0.8 copy.14
  1.4 0.7 reshape_reshape.3.cols_row
  2.0 0.7 reshape.28.cols_ref
  2.7 111.1 %forward_exchange.1 = (f32[4,4,128,128]{3,2,1,0:T(8,128)}, bf16[4,4,128,128]{3,2,1,0:T(8,128)(2,1)}, bf16[512,640]{1,0:T(8,128)(2,1)}, s32[512,1]{1,0:T(8,128)}, s32[1,512]{1,0:T(1,128)}, /*index=5*/s32[8,256]{1,0:T(8,128)}) custom-call(s32[256]{0:T(256)} %reshape.28.cols_ref, s32[1,256]{1,0:T(1,128)} %reshape_reshape.3.cols_row, s32[1,512]{1,0:T(1,128)} %bitcast.14, ...), custom_call_target="tpu_custom_call" | custom-call | tf_op jit(solution)/shard_map/forward_exchange/pallas_call | solution.py:508
  113.8 120.3 %backward_exchange.1 = (bf16[512,512]{1,0:T(8,128)(2,1)}, bf16[512,512]{1,0:T(8,128)(2,1)}, f32[2,4,4,32,512]{4,3,2,1,0:T(8,128)}) custom-call(s32[8,256]{1,0:T(8,128)} %get-tuple-element.13.tables, s32[1,512]{1,0:T(1,128)} %get-tuple-element.14.node_row, s32[512,1]{1,0:T(8,128)} %get-tuple-element.15.own_col, f32[4,4,128,128]{3,2,1,0:T(8,128)} %get-tuple-element.16.summed, ...), custom_call_target="tpu_custom_call" | custom-call | tf_op jit(solution)/shard_map/backward_exchange/pallas_call | solution.py:823
  234.1 0.0 copy-start.1
  234.1 0.0 copy-start
  234.2 3.2 %fusion = (f32[1,4,4,32,512]{4,3,2,1,0:T(8,128)}, f32[1,4,4,32,512]{4,3,2,1,0:T(8,128)}) fusion(f32[2,4,4,32,512]{4,3,2,1,0:T(8,128)} %get-tuple-element.21), kind=kLoop, calls=%fused_computation | loop fusion | bytes 4194304 | tf_op jit(solution)/shard_map/slice | solution.py:867
  237.4 0.0 copy-done.1
  237.4 0.8 copy.18
  238.2 0.0 copy-done
  238.2 0.8 copy.19
Async XLA Ops:
  234.1 3.2 %copy-start.1 = (bf16[512,512]{1,0:T(8,128)(2,1)S(1)}, bf16[512,512]{1,0:T(8,128)(2,1)}, u32[]{:S(2)}) copy-start(bf16[512,512]{1,0:T(8,128)(2,1)} %get-tuple-element.28) | copy-start | bytes 1572868
  234.1 4.0 %copy-start = (bf16[512,512]{1,0:T(8,128)(2,1)S(1)}, bf16[512,512]{1,0:T(8,128)(2,1)}, u32[]{:S(2)}) copy-start(bf16[512,512]{1,0:T(8,128)(2,1)} %get-tuple-element.29) | copy-start | bytes 1572868
